TPU v7x, 512 devices: a whole 4x4x16 slice. The times are simulated.
512 devices in a mesh: gx: 16 (over z), gy: 32 (over x, y, core).
Axes of the slice: x: 4, y: 4, z: 16, core: 2. Of those that a mesh axis runs over, the one named last changes fastest.
Arguments:
- a_tiles: float32 [4096, 4, 128, 128], P(('gx', 'gy')), may hold values from -6 to 6
- a_cols: int32 [4096, 4], P(('gx', 'gy')), may hold values from 0 to 4095, as said below
- new_row: int32 [4096], P(('gx', 'gy')), may hold values from 0 to 4095, as said below
- p_tiles: float32 [4096, 2, 128, 128], P(('gx', 'gy')), may hold values from -0.5 to 0.5
- p_cols: int32 [4096, 2], P(('gx', 'gy')), may hold values from 0 to 1023, as said below
Outputs:
- coarse: float32 [1024, 10, 128, 128], P(('gx', 'gy'))
Inputs may be any that keep to these rules, and one draw needn't show every extreme that they name: A permutation; the new owner new_row // 8 of a block row has the same gy index as its old owner and a gx index 0 to 5 above the old owner's, modulo the number of gx indices; at most 2 block rows of one device go to one new owner. `a_cols`: the first column block of old block row o is new_row[o]; the others are distinct block rows of the devices with the same gx index as new_row[o]'s owner and gy index one below, equal or one above. `p_cols`: for block row g owned by device d (gy index y), the first coarse block is one of d's 2 coarse blocks, the second one of device d + 1's, or of d's where y is the last gy index.
All inputs are finite; a program needn't handle non-finite values.
Results may differ from a plain program's by a relative error of at most 0.0003.
Values sent between devices are 32-bit elements; how exact they have to be, the bound alone decides.
No kernel may reach another device: no remote copies, remote signals or barrier semaphores. Data moves between devices by JAX's collectives and lax.ppermute only.
A program may use at most 128 MiB of HBM per device.

v0:
```python
import jax
import jax.numpy as jnp
from jax import lax
from jax.sharding import PartitionSpec as P

A_TILES = 4
P_TILES = 2
CAP = 2


def with_halo(shard, sides, width):
    for axis, dim in sides:
        size, length = (lax.axis_size(axis), shard.shape[dim])
        up = [(i, (i + 1) % size) for i in range(size - 1)]
        down = [(j, i) for i, j in up]
        last = lax.slice_in_dim(shard, length - width, length, axis=dim)
        leading = lax.slice_in_dim(shard, 0, width, axis=dim)
        before = lax.ppermute(last, axis, up)
        after = lax.ppermute(leading, axis, down)
        shard = jnp.concatenate([before, shard, after], axis=dim)
    return shard


def from_behind(block, axis, distance):
    devices = range(lax.axis_size(axis))
    route = [((i - distance) % len(devices), i) for i in devices]
    return lax.ppermute(block, axis, route)


def shifted(value, axis, steps):
    count = lax.axis_size(axis)
    leading, last = (max(0, -steps), min(count, count - steps))
    return lax.ppermute(value, axis, [(source, source + steps) for source in range(leading, last)])


def fetch_neighbours(p_tiles, p_cols, row_count):
    return (
        with_halo(p_tiles, (("gy", 0),), row_count),
        with_halo(p_cols.astype(jnp.float32), (("gy", 0),), row_count),
    )


def shards(a_tiles, a_cols, new_row, p_tiles, p_cols):
    row_count = a_tiles.shape[0]
    tile_size = a_tiles.shape[2]
    gx_count = lax.axis_size("gx")
    gy_count = lax.axis_size("gy")
    coarse_count = row_count // 4
    my_x = lax.axis_index("gx")
    device_id = my_x * gy_count + lax.axis_index("gy")
    target_x = new_row // row_count // gy_count
    new_local = new_row % row_count
    row_order = jnp.arange(row_count)
    earlier = (target_x[:, None] == target_x[None, :]) & (row_order[None, :] < row_order[:, None])
    rank_in_peer = jnp.sum(earlier.astype(jnp.int32), axis=1)
    span_count = min(6, gx_count)
    distance = (target_x - my_x) % gx_count
    bucket = distance * CAP + rank_in_peer
    send_tiles = (
        jnp.zeros((span_count * CAP,) + a_tiles.shape[1:], jnp.float32).at[bucket].set(a_tiles)
    )
    send_cols = (
        jnp.zeros((span_count * CAP, A_TILES), jnp.float32)
        .at[bucket]
        .set(a_cols.astype(jnp.float32))
    )
    send_dest = (
        jnp.full((span_count * CAP,), float(row_count), jnp.float32)
        .at[bucket]
        .set(new_local.astype(jnp.float32))
    )
    tile_parts = [send_tiles[:CAP]]
    col_parts = [send_cols[:CAP]]
    dest_parts = [send_dest[:CAP]]
    for step_by in range(1, span_count):
        lower = step_by * CAP
        came_tiles, came_cols, came_dest = from_behind(
            (
                send_tiles[lower : lower + CAP],
                send_cols[lower : lower + CAP],
                send_dest[lower : lower + CAP],
            ),
            "gx",
            step_by,
        )
        tile_parts.append(came_tiles)
        col_parts.append(came_cols)
        dest_parts.append(came_dest)
    got_tiles = jnp.concatenate(tile_parts, axis=0)
    got_cols = jnp.concatenate(col_parts, axis=0)
    got_dest = jnp.concatenate(dest_parts, axis=0)
    dest_slot = got_dest.astype(jnp.int32)
    moved = jnp.zeros_like(a_tiles).at[dest_slot].set(got_tiles, mode="drop")
    moved_cols = (
        jnp.zeros((row_count, A_TILES), jnp.int32)
        .at[dest_slot]
        .set(got_cols.astype(jnp.int32), mode="drop")
    )
    local_index = moved_cols - (device_id - 1) * row_count
    ext_tiles, ext_cols = fetch_neighbours(p_tiles, p_cols, row_count)
    fetched = ext_tiles[local_index]
    products = jnp.einsum("rkab,rkqbc->rkqac", moved, fetched, precision=lax.Precision.HIGHEST)
    targets = ext_cols.astype(jnp.int32)[local_index]
    wide_slot = targets - (device_id - 1) * coarse_count
    select = (wide_slot[:, None, :, :] == jnp.arange(4 * coarse_count)[None, :, None, None]).astype(
        jnp.float32
    )
    select = select.reshape(row_count, 4 * coarse_count, A_TILES * P_TILES)
    flat_products = products.reshape(row_count, A_TILES * P_TILES, tile_size, tile_size)
    summed = jnp.einsum("rsm,rmac->rsac", select, flat_products, precision=lax.Precision.HIGHEST)
    lifted = jnp.einsum("rpba,rsbc->rpsac", p_tiles, summed, precision=lax.Precision.HIGHEST)
    owner_slot = p_cols - device_id * coarse_count
    owner_pick = (owner_slot[None, :, :] == jnp.arange(2 * coarse_count)[:, None, None]).astype(
        jnp.float32
    )
    partial_value = jnp.einsum(
        "trp,rpsac->tsac", owner_pick, lifted, precision=lax.Precision.HIGHEST
    )
    zero_band = jnp.zeros((coarse_count, coarse_count, tile_size, tile_size), jnp.float32)
    own_rows = jnp.concatenate([zero_band, partial_value[:coarse_count]], axis=1)
    next_rows = jnp.concatenate([partial_value[coarse_count:], zero_band], axis=1)
    arrived = shifted(next_rows, "gy", 1)
    return own_rows + arrived


def solution(mesh):
    in_specs = (
        P(("gx", "gy"), None, None, None),
        P(("gx", "gy"), None),
        P(("gx", "gy")),
        P(("gx", "gy"), None, None, None),
        P(("gx", "gy"), None),
    )
    out_specs = P(("gx", "gy"), None, None, None)
    return jax.shard_map(shards, mesh=mesh, in_specs=in_specs, out_specs=out_specs, check_vma=False)
```

profile of v0, /device:TPU:38, one launch (start us, length us, event | category | flops | bytes accessed | tf_op | source)
XLA Modules:
  0.0 340.8 jit_solution(10567180512278071702)
XLA Ops:
  0.0 0.8 broadcast_subtract_fusion.1
  0.8 4.6 %collective-permute-start.1 = (f32[8,2]{0,1:T(2,128)S(1)}, f32[8,2]{0,1:T(2,128)S(1)}, u32[]{:S(2)}, u32[]{:S(2)}) collective-permute-start(f32[8,2]{0,1:T(2,128)S(1)} %get-tuple-element.20), channel_id=1, source_target_pairs={{1,0},{2,1},{3,2},{4,3},{5,4},{6,5},{7,6},{8,7},{9,8},{10,9},{11,1... | collective-permute-start | bytes 200 | tf_op jit(solution)/shard_map/ppermute | solution.py:19
  5.4 1.9 collective-permute-start
  7.3 0.7 fusion.21
  8.9 10.4 %collective-permute-start.6 = (f32[2]{0:T(128)S(1)}, f32[2]{0:T(128)S(1)}, u32[]{:S(2)}, u32[]{:S(2)}) collective-permute-start(f32[2]{0:T(128)S(1)} %get-tuple-element.21), channel_id=1, source_target_pairs={{352,0},{384,32},{416,64},{448,96},{480,128},{0,160},{32,192},{64,... | collective-permute-start | bytes 32 | tf_op jit(solution)/shard_map/ppermute | solution.py:27
  19.3 7.3 %collective-permute-start.5 = (f32[2]{0:T(128)S(1)}, f32[2]{0:T(128)S(1)}, u32[]{:S(2)}, u32[]{:S(2)}) collective-permute-start(f32[2]{0:T(128)S(1)} %get-tuple-element.22), channel_id=1, source_target_pairs={{384,0},{416,32},{448,64},{480,96},{0,128},{32,160},{64,192},{96,2... | collective-permute-start | bytes 32 | tf_op jit(solution)/shard_map/ppermute | solution.py:27
  26.6 3.8 %collective-permute-start.4 = (f32[2]{0:T(128)S(1)}, f32[2]{0:T(128)S(1)}, u32[]{:S(2)}, u32[]{:S(2)}) collective-permute-start(f32[2]{0:T(128)S(1)} %get-tuple-element.23), channel_id=1, source_target_pairs={{416,0},{448,32},{480,64},{0,96},{32,128},{64,160},{96,192},{128,2... | collective-permute-start | bytes 32 | tf_op jit(solution)/shard_map/ppermute | solution.py:27
  30.5 0.7 convert_element_type.35
  32.3 2.5 scatter_fusion
  34.8 1.7 fusion.26
  36.5 3.4 collective-permute-start.3
  39.9 1.9 collective-permute-start.2
  41.9 4.2 %collective-permute-start.11 = (f32[2,4]{1,0:T(2,128)S(1)}, f32[2,4]{1,0:T(2,128)S(1)}, u32[]{:S(2)}, u32[]{:S(2)}) collective-permute-start(f32[2,4]{1,0:T(2,128)S(1)} %get-tuple-element.13), channel_id=1, source_target_pairs={{352,0},{384,32},{416,64},{448,96},{480,128},{0,160},{32,192},{64,... | collective-permute-start | bytes 104 | tf_op jit(solution)/shard_map/ppermute | solution.py:27
  46.1 5.2 %collective-permute-start.15 = (f32[2,4,128,128]{3,2,1,0:T(8,128)}, f32[2,4,128,128]{3,2,1,0:T(8,128)S(1)}, u32[]{:S(2)}, u32[]{:S(2)}) collective-permute-start(f32[2,4,128,128]{3,2,1,0:T(8,128)} %get-tuple-element.8), channel_id=1, source_target_pairs={{448,0},{480,32},{0,64},{32,96},{64,128},{96,160},{128,192},{160,2... | collective-permute-start | bytes 1572872 | tf_op jit(solution)/shard_map/ppermute | solution.py:27
  51.3 5.0 %collective-permute-start.14 = (f32[2,4,128,128]{3,2,1,0:T(8,128)}, f32[2,4,128,128]{3,2,1,0:T(8,128)S(1)}, u32[]{:S(2)}, u32[]{:S(2)}) collective-permute-start(f32[2,4,128,128]{3,2,1,0:T(8,128)} %get-tuple-element.9), channel_id=1, source_target_pairs={{480,0},{0,32},{32,64},{64,96},{96,128},{128,160},{160,192},{192,2... | collective-permute-start | bytes 1572872 | tf_op jit(solution)/shard_map/ppermute | solution.py:27
  56.4 4.3 %collective-permute-start.10 = (f32[2,4]{1,0:T(2,128)S(1)}, f32[2,4]{1,0:T(2,128)S(1)}, u32[]{:S(2)}, u32[]{:S(2)}) collective-permute-start(f32[2,4]{1,0:T(2,128)S(1)} %get-tuple-element.14), channel_id=1, source_target_pairs={{384,0},{416,32},{448,64},{480,96},{0,128},{32,160},{64,192},{96,2... | collective-permute-start | bytes 104 | tf_op jit(solution)/shard_map/ppermute | solution.py:27
  60.8 23.5 %collective-permute-done.10 = f32[2,4]{1,0:T(2,128)S(1)} collective-permute-done((f32[2,4]{1,0:T(2,128)S(1)}, f32[2,4]{1,0:T(2,128)S(1)}, u32[]{:S(2)}, u32[]{:S(2)}) %collective-permute-start.10) | collective-permute-done | bytes 64 | tf_op jit(solution)/shard_map/ppermute | solution.py:27
  84.3 5.3 %collective-permute-start.9 = (f32[2,4]{1,0:T(2,128)S(1)}, f32[2,4]{1,0:T(2,128)S(1)}, u32[]{:S(2)}, u32[]{:S(2)}) collective-permute-start(f32[2,4]{1,0:T(2,128)S(1)} %get-tuple-element.15), channel_id=1, source_target_pairs={{416,0},{448,32},{480,64},{0,96},{32,128},{64,160},{96,192},{128,2... | collective-permute-start | bytes 104 | tf_op jit(solution)/shard_map/ppermute | solution.py:27
  89.8 3.0 collective-permute-done.9
  92.8 3.6 %collective-permute-start.8 = (f32[2,4]{1,0:T(2,128)S(1)}, f32[2,4]{1,0:T(2,128)S(1)}, u32[]{:S(2)}, u32[]{:S(2)}) collective-permute-start(f32[2,4]{1,0:T(2,128)S(1)} %get-tuple-element.16), channel_id=1, source_target_pairs={{448,0},{480,32},{0,64},{32,96},{64,128},{96,160},{128,192},{160,2... | collective-permute-start | bytes 104 | tf_op jit(solution)/shard_map/ppermute | solution.py:27
  96.5 3.9 %collective-permute-done.8 = f32[2,4]{1,0:T(2,128)S(1)} collective-permute-done((f32[2,4]{1,0:T(2,128)S(1)}, f32[2,4]{1,0:T(2,128)S(1)}, u32[]{:S(2)}, u32[]{:S(2)}) %collective-permute-start.8) | collective-permute-done | bytes 64 | tf_op jit(solution)/shard_map/ppermute | solution.py:27
  100.4 1.9 collective-permute-start.7
  102.4 3.4 %collective-permute-done.7 = f32[2,4]{1,0:T(2,128)S(1)} collective-permute-done((f32[2,4]{1,0:T(2,128)S(1)}, f32[2,4]{1,0:T(2,128)S(1)}, u32[]{:S(2)}, u32[]{:S(2)}) %collective-permute-start.7) | collective-permute-done | bytes 64 | tf_op jit(solution)/shard_map/ppermute | solution.py:27
  105.8 2.3 collective-permute-start.13
  109.1 2.0 collective-permute-start.12
  111.2 6.8 %collective-permute-start.16 = (f32[2,4,128,128]{3,2,1,0:T(8,128)}, f32[2,4,128,128]{3,2,1,0:T(8,128)S(1)}, u32[]{:S(2)}, u32[]{:S(2)}) collective-permute-start(f32[2,4,128,128]{3,2,1,0:T(8,128)} %get-tuple-element.7), channel_id=1, source_target_pairs={{416,0},{448,32},{480,64},{0,96},{32,128},{64,160},{96,192},{128,2... | collective-permute-start | bytes 1572872 | tf_op jit(solution)/shard_map/ppermute | solution.py:27
  118.8 6.3 %collective-permute-start.18 = (f32[2,4,128,128]{3,2,1,0:T(8,128)}, f32[2,4,128,128]{3,2,1,0:T(8,128)S(1)}, u32[]{:S(2)}, u32[]{:S(2)}) collective-permute-start(f32[2,4,128,128]{3,2,1,0:T(8,128)} %get-tuple-element.5), channel_id=1, source_target_pairs={{352,0},{384,32},{416,64},{448,96},{480,128},{0,160},{32,192},{64,... | collective-permute-start | bytes 1572872 | tf_op jit(solution)/shard_map/ppermute | solution.py:27
  125.1 4.5 %collective-permute-start.17 = (f32[2,4,128,128]{3,2,1,0:T(8,128)}, f32[2,4,128,128]{3,2,1,0:T(8,128)S(1)}, u32[]{:S(2)}, u32[]{:S(2)}) collective-permute-start(f32[2,4,128,128]{3,2,1,0:T(8,128)} %get-tuple-element.6), channel_id=1, source_target_pairs={{384,0},{416,32},{448,64},{480,96},{0,128},{32,160},{64,192},{96,2... | collective-permute-start | bytes 1572872 | tf_op jit(solution)/shard_map/ppermute | solution.py:27
  129.7 0.8 constant_dynamic-update-slice_fusion.4
  130.5 0.9 constant_dynamic-update-slice_fusion.3
  131.4 21.1 %collective-permute-done.16 = f32[2,4,128,128]{3,2,1,0:T(8,128)S(1)} collective-permute-done((f32[2,4,128,128]{3,2,1,0:T(8,128)}, f32[2,4,128,128]{3,2,1,0:T(8,128)S(1)}, u32[]{:S(2)}, u32[]{:S(2)}) %collective-permute-start.16) | collective-permute-done | bytes 524320 | tf_op jit(solution)/shard_map/ppermute | solution.py:27
  152.5 0.8 constant_dynamic-update-slice_fusion.2
  153.3 103.6 %collective-permute-done.17 = f32[2,4,128,128]{3,2,1,0:T(8,128)S(1)} collective-permute-done((f32[2,4,128,128]{3,2,1,0:T(8,128)}, f32[2,4,128,128]{3,2,1,0:T(8,128)S(1)}, u32[]{:S(2)}, u32[]{:S(2)}) %collective-permute-start.17) | collective-permute-done | bytes 524320 | tf_op jit(solution)/shard_map/ppermute | solution.py:27
  256.9 0.8 constant_dynamic-update-slice_fusion.1
  257.7 0.8 constant_dynamic-update-slice_fusion
  258.8 4.0 %scatter_fusion.1 = f32[8,4,128,128]{3,2,1,0:T(8,128)S(1)} fusion(f32[8,4,128,128]{3,2,1,0:T(8,128)S(1)} %broadcast_in_dim.13, s32[12]{0:T(128)S(1)} %fusion.23, f32[12,4,128,128]{3,2,1,0:T(8,128)} %constant_dynamic-update-slice_fusion), kind=kCustom, calls=%fused_computation.6 | custom fusion | bytes 9437232 | tf_op jit(solution)/shard_map/scatter | solution.py:93
  262.8 3.5 %pad_maximum_fusion = f32[24,2,128,128]{3,2,1,0:T(8,128)} fusion(f32[8,2,128,128]{3,2,1,0:T(8,128)} %collective-permute-done.13, f32[8,2,128,128]{3,2,1,0:T(8,128)S(1)} %copy-done, f32[8,2,128,128]{3,2,1,0:T(8,128)} %collective-permute-done.12), kind=kLoop, calls=%fused_computation.10 | loop fusion | flops 1572864 | bytes 6291456 | tf_op jit(solution)/shard_map/concatenate | solution.py:20
  266.3 4.6 %gather_fusion.1 = f32[32,2,128,128]{3,2,1,0:T(8,128)} fusion(f32[24,2,128,128]{3,2,1,0:T(8,128)} %pad_maximum_fusion, s32[1024]{0:T(1024)S(1)} %pad_clamp_fusion), kind=kCustom, calls=%fused_computation.1 | custom fusion | bytes 8388736 | tf_op jit(solution)/shard_map/gather | solution.py:101
  271.0 10.5 %fusion.5 = f32[8,4,2,128,128]{4,3,2,1,0:T(8,128)} fusion(f32[8,4,2,128,128]{4,3,2,1,0:T(8,128)} %bitcast.49, f32[8,4,128,128]{3,2,1,0:T(8,128)S(1)} %scatter_fusion.1), kind=kOutput, calls=%fused_computation.12 | convolution fusion | flops 1610612736 | bytes 10485760 | tf_op jit(solution)/shard_map/rkab,rkqbc->rkqac/dot_general | solution.py:102
  281.4 5.4 %copy.64 = f32[8,8,128,128]{3,1,2,0:T(8,128)} copy(f32[8,8,128,128]{2,3,1,0:T(8,128)} %bitcast.48) | data formatting | bytes 8388608 | tf_op jit(solution)/shard_map/reshape | solution.py:109
  286.8 4.3 %convolution_bitcast_fusion = f32[8,8,128,128,1]{3,1,2,0,4:T(8,128)S(1)} fusion(f32[8,8,128,128]{3,1,2,0:T(8,128)} %copy.64, s32[8,8]{1,0:T(8,128)S(1)} %sub.53), kind=kOutput, calls=%fused_computation.11 | convolution fusion | flops 100663808 | bytes 8388864 | tf_op jit(solution)/shard_map/rsm,rmac->rsac/dot_general | solution.py:110
  291.1 9.0 %fusion.2 = f32[8,2,8,128,128]{3,4,1,2,0:T(8,128)} fusion(f32[8,8,128,128,1]{3,1,2,0,4:T(8,128)S(1)} %convolution_bitcast_fusion, f32[8,2,128,128]{3,2,1,0:T(8,128)S(1)} %copy-done), kind=kOutput, calls=%fused_computation.9 | convolution fusion | flops 3221225472 | bytes 13631488 | tf_op jit(solution)/shard_map/rpba,rsbc->rpsac/dot_general | solution.py:111
  300.1 9.2 %copy.66 = f32[8,2,8,128,128]{4,0,1,3,2:T(8,128)} copy(f32[8,2,8,128,128]{3,4,1,2,0:T(8,128)} %fusion.2) | data formatting | bytes 16777216 | tf_op jit(solution)/shard_map/rpba,rsbc->rpsac/transpose | solution.py:111
  309.3 7.2 %convolution_bitcast_fusion.1 = f32[4,8,128,128]{3,0,2,1:T(4,128)S(1)} fusion(f32[8,2,8,128,128]{4,0,1,3,2:T(8,128)} %copy.66, s32[8,2]{0,1:T(2,128)S(1)} %get-tuple-element.19), kind=kOutput, calls=%fused_computation.14 | convolution fusion | flops 100663360 | bytes 10485824 | tf_op jit(solution)/shard_map/trp,rpsac->tsac/dot_general | solution.py:116
  316.6 1.0 fusion.27
  318.0 2.0 collective-permute-start.19
  320.1 19.0 %collective-permute-done.19 = f32[2,10,128,128]{3,0,2,1:T(2,128)S(1)} collective-permute-done((f32[2,10,128,128]{3,0,2,1:T(2,128)S(1)}, f32[2,10,128,128]{3,0,2,1:T(2,128)S(1)}, u32[]{:S(2)}, u32[]{:S(2)}) %collective-permute-start.19) | collective-permute-done | bytes 1310752 | tf_op jit(solution)/shard_map/ppermute | solution.py:33
  339.6 1.2 copy.67
  (46 shorter events, 5.6 us)
Async XLA Ops:
  0.8 108.4 %collective-permute-start.1 = (f32[8,2]{0,1:T(2,128)S(1)}, f32[8,2]{0,1:T(2,128)S(1)}, u32[]{:S(2)}, u32[]{:S(2)}) collective-permute-start(f32[8,2]{0,1:T(2,128)S(1)} %get-tuple-element.20), channel_id=1, source_target_pairs={{1,0},{2,1},{3,2},{4,3},{5,4},{6,5},{7,6},{8,7},{9,8},{10,9},{11,1... | collective-permute-start | bytes 200 | tf_op jit(solution)/shard_map/ppermute | solution.py:19
  5.4 105.8 %collective-permute-start = (f32[8,2]{0,1:T(2,128)S(1)}, f32[8,2]{0,1:T(2,128)S(1)}, u32[]{:S(2)}, u32[]{:S(2)}) collective-permute-start(f32[8,2]{0,1:T(2,128)S(1)} %get-tuple-element.20), channel_id=1, source_target_pairs={{0,1},{1,2},{2,3},{3,4},{4,5},{5,6},{6,7},{7,8},{8,9},{9,10},{10,1... | collective-permute-start | bytes 200 | tf_op jit(solution)/shard_map/ppermute | solution.py:18
  8.9 27.7 %collective-permute-start.6 = (f32[2]{0:T(128)S(1)}, f32[2]{0:T(128)S(1)}, u32[]{:S(2)}, u32[]{:S(2)}) collective-permute-start(f32[2]{0:T(128)S(1)} %get-tuple-element.21), channel_id=1, source_target_pairs={{352,0},{384,32},{416,64},{448,96},{480,128},{0,160},{32,192},{64,... | collective-permute-start | bytes 32 | tf_op jit(solution)/shard_map/ppermute | solution.py:27
  19.3 20.6 %collective-permute-start.5 = (f32[2]{0:T(128)S(1)}, f32[2]{0:T(128)S(1)}, u32[]{:S(2)}, u32[]{:S(2)}) collective-permute-start(f32[2]{0:T(128)S(1)} %get-tuple-element.22), channel_id=1, source_target_pairs={{384,0},{416,32},{448,64},{480,96},{0,128},{32,160},{64,192},{96,2... | collective-permute-start | bytes 32 | tf_op jit(solution)/shard_map/ppermute | solution.py:27
  26.6 15.2 %collective-permute-start.4 = (f32[2]{0:T(128)S(1)}, f32[2]{0:T(128)S(1)}, u32[]{:S(2)}, u32[]{:S(2)}) collective-permute-start(f32[2]{0:T(128)S(1)} %get-tuple-element.23), channel_id=1, source_target_pairs={{416,0},{448,32},{480,64},{0,96},{32,128},{64,160},{96,192},{128,2... | collective-permute-start | bytes 32 | tf_op jit(solution)/shard_map/ppermute | solution.py:27
  36.5 9.5 %collective-permute-start.3 = (f32[2]{0:T(128)S(1)}, f32[2]{0:T(128)S(1)}, u32[]{:S(2)}, u32[]{:S(2)}) collective-permute-start(f32[2]{0:T(128)S(1)} %get-tuple-element.24), channel_id=1, source_target_pairs={{448,0},{480,32},{0,64},{32,96},{64,128},{96,160},{128,192},{160,2... | collective-permute-start | bytes 32 | tf_op jit(solution)/shard_map/ppermute | solution.py:27
  39.9 11.3 %collective-permute-start.2 = (f32[2]{0:T(128)S(1)}, f32[2]{0:T(128)S(1)}, u32[]{:S(2)}, u32[]{:S(2)}) collective-permute-start(f32[2]{0:T(128)S(1)} %get-tuple-element.25), channel_id=1, source_target_pairs={{480,0},{0,32},{32,64},{64,96},{96,128},{128,160},{160,192},{192,2... | collective-permute-start | bytes 32 | tf_op jit(solution)/shard_map/ppermute | solution.py:27
  41.9 14.6 %collective-permute-start.11 = (f32[2,4]{1,0:T(2,128)S(1)}, f32[2,4]{1,0:T(2,128)S(1)}, u32[]{:S(2)}, u32[]{:S(2)}) collective-permute-start(f32[2,4]{1,0:T(2,128)S(1)} %get-tuple-element.13), channel_id=1, source_target_pairs={{352,0},{384,32},{416,64},{448,96},{480,128},{0,160},{32,192},{64,... | collective-permute-start | bytes 104 | tf_op jit(solution)/shard_map/ppermute | solution.py:27
  46.1 72.7 %collective-permute-start.15 = (f32[2,4,128,128]{3,2,1,0:T(8,128)}, f32[2,4,128,128]{3,2,1,0:T(8,128)S(1)}, u32[]{:S(2)}, u32[]{:S(2)}) collective-permute-start(f32[2,4,128,128]{3,2,1,0:T(8,128)} %get-tuple-element.8), channel_id=1, source_target_pairs={{448,0},{480,32},{0,64},{32,96},{64,128},{96,160},{128,192},{160,2... | collective-permute-start | bytes 1572872 | tf_op jit(solution)/shard_map/ppermute | solution.py:27
  51.3 73.8 %collective-permute-start.14 = (f32[2,4,128,128]{3,2,1,0:T(8,128)}, f32[2,4,128,128]{3,2,1,0:T(8,128)S(1)}, u32[]{:S(2)}, u32[]{:S(2)}) collective-permute-start(f32[2,4,128,128]{3,2,1,0:T(8,128)} %get-tuple-element.9), channel_id=1, source_target_pairs={{480,0},{0,32},{32,64},{64,96},{96,128},{128,160},{160,192},{192,2... | collective-permute-start | bytes 1572872 | tf_op jit(solution)/shard_map/ppermute | solution.py:27
  56.4 27.9 %collective-permute-start.10 = (f32[2,4]{1,0:T(2,128)S(1)}, f32[2,4]{1,0:T(2,128)S(1)}, u32[]{:S(2)}, u32[]{:S(2)}) collective-permute-start(f32[2,4]{1,0:T(2,128)S(1)} %get-tuple-element.14), channel_id=1, source_target_pairs={{384,0},{416,32},{448,64},{480,96},{0,128},{32,160},{64,192},{96,2... | collective-permute-start | bytes 104 | tf_op jit(solution)/shard_map/ppermute | solution.py:27
  84.3 8.5 %collective-permute-start.9 = (f32[2,4]{1,0:T(2,128)S(1)}, f32[2,4]{1,0:T(2,128)S(1)}, u32[]{:S(2)}, u32[]{:S(2)}) collective-permute-start(f32[2,4]{1,0:T(2,128)S(1)} %get-tuple-element.15), channel_id=1, source_target_pairs={{416,0},{448,32},{480,64},{0,96},{32,128},{64,160},{96,192},{128,2... | collective-permute-start | bytes 104 | tf_op jit(solution)/shard_map/ppermute | solution.py:27
  92.8 7.6 %collective-permute-start.8 = (f32[2,4]{1,0:T(2,128)S(1)}, f32[2,4]{1,0:T(2,128)S(1)}, u32[]{:S(2)}, u32[]{:S(2)}) collective-permute-start(f32[2,4]{1,0:T(2,128)S(1)} %get-tuple-element.16), channel_id=1, source_target_pairs={{448,0},{480,32},{0,64},{32,96},{64,128},{96,160},{128,192},{160,2... | collective-permute-start | bytes 104 | tf_op jit(solution)/shard_map/ppermute | solution.py:27
  100.4 5.5 %collective-permute-start.7 = (f32[2,4]{1,0:T(2,128)S(1)}, f32[2,4]{1,0:T(2,128)S(1)}, u32[]{:S(2)}, u32[]{:S(2)}) collective-permute-start(f32[2,4]{1,0:T(2,128)S(1)} %get-tuple-element.17), channel_id=1, source_target_pairs={{480,0},{0,32},{32,64},{64,96},{96,128},{128,160},{160,192},{192,2... | collective-permute-start | bytes 104 | tf_op jit(solution)/shard_map/ppermute | solution.py:27
  105.8 156.9 %collective-permute-start.13 = (f32[8,2,128,128]{3,2,1,0:T(8,128)}, f32[8,2,128,128]{3,2,1,0:T(8,128)}, u32[]{:S(2)}, u32[]{:S(2)}) collective-permute-start(f32[8,2,128,128]{3,2,1,0:T(8,128)} %param.8), channel_id=1, source_target_pairs={{1,0},{2,1},{3,2},{4,3},{5,4},{6,5},{7,6},{8,7},{9,8},{10,9},{11,1... | collective-permute-start | bytes 3145736 | tf_op jit(solution)/shard_map/ppermute | solution.py:19
  109.1 153.6 %collective-permute-start.12 = (f32[8,2,128,128]{3,2,1,0:T(8,128)}, f32[8,2,128,128]{3,2,1,0:T(8,128)}, u32[]{:S(2)}, u32[]{:S(2)}) collective-permute-start(f32[8,2,128,128]{3,2,1,0:T(8,128)} %param.8), channel_id=1, source_target_pairs={{0,1},{1,2},{2,3},{3,4},{4,5},{5,6},{6,7},{7,8},{8,9},{9,10},{10,1... | collective-permute-start | bytes 3145736 | tf_op jit(solution)/shard_map/ppermute | solution.py:18
  111.2 41.3 %collective-permute-start.16 = (f32[2,4,128,128]{3,2,1,0:T(8,128)}, f32[2,4,128,128]{3,2,1,0:T(8,128)S(1)}, u32[]{:S(2)}, u32[]{:S(2)}) collective-permute-start(f32[2,4,128,128]{3,2,1,0:T(8,128)} %get-tuple-element.7), channel_id=1, source_target_pairs={{416,0},{448,32},{480,64},{0,96},{32,128},{64,160},{96,192},{128,2... | collective-permute-start | bytes 1572872 | tf_op jit(solution)/shard_map/ppermute | solution.py:27
  118.8 138.9 %collective-permute-start.18 = (f32[2,4,128,128]{3,2,1,0:T(8,128)}, f32[2,4,128,128]{3,2,1,0:T(8,128)S(1)}, u32[]{:S(2)}, u32[]{:S(2)}) collective-permute-start(f32[2,4,128,128]{3,2,1,0:T(8,128)} %get-tuple-element.5), channel_id=1, source_target_pairs={{352,0},{384,32},{416,64},{448,96},{480,128},{0,160},{32,192},{64,... | collective-permute-start | bytes 1572872 | tf_op jit(solution)/shard_map/ppermute | solution.py:27
  125.1 131.8 %collective-permute-start.17 = (f32[2,4,128,128]{3,2,1,0:T(8,128)}, f32[2,4,128,128]{3,2,1,0:T(8,128)S(1)}, u32[]{:S(2)}, u32[]{:S(2)}) collective-permute-start(f32[2,4,128,128]{3,2,1,0:T(8,128)} %get-tuple-element.6), channel_id=1, source_target_pairs={{384,0},{416,32},{448,64},{480,96},{0,128},{32,160},{64,192},{96,2... | collective-permute-start | bytes 1572872 | tf_op jit(solution)/shard_map/ppermute | solution.py:27
  258.8 4.0 %copy-start = (f32[8,2,128,128]{3,2,1,0:T(8,128)S(1)}, f32[8,2,128,128]{3,2,1,0:T(8,128)}, u32[]{:S(2)}) copy-start(f32[8,2,128,128]{3,2,1,0:T(8,128)} %param.8) | copy-start | bytes 3145732
  318.0 21.0 %collective-permute-start.19 = (f32[2,10,128,128]{3,0,2,1:T(2,128)S(1)}, f32[2,10,128,128]{3,0,2,1:T(2,128)S(1)}, u32[]{:S(2)}, u32[]{:S(2)}) collective-permute-start(f32[2,10,128,128]{3,0,2,1:T(2,128)S(1)} %concatenate.52), channel_id=1, source_target_pairs={{0,1},{1,2},{2,3},{3,4},{4,5},{5,6},{6,7},{7,8},{8,9},{9,10},{10,1... | collective-permute-start | bytes 3932168 | tf_op jit(solution)/shard_map/ppermute | solution.py:33
where the time goes:
time: 342 us; the launch traced here: 341 us
  waiting for transfers between devices  178 us (52%)
  starting transfers between devices  86.8 us (25%)
  local copies, waits for them, and re-layouts  38.5 us (11%)
  matrix products  31 us (9%)
  other arithmetic  6.51 us (2%)
    ppermute x15, waiting for transfers between devices, from_behind(): return lax.ppermute(block, axis, route)  159 us
    ppermute x15, starting transfers between devices, from_behind(): return lax.ppermute(block, axis, route)  74 us
    ppermute x1, waiting for transfers between devices, shifted(): lax.ppermute(value, axis, [(source, source + steps) for source in range(l...  19 us
    dot_general x1, matrix products, shards(): jnp.einsum('rkab,rkqbc->rkqac', moved, fetched, precision=lax.Precision.H...  10.5 us
    transpose x1, local copies, waits for them, and re-layouts, shards(): jnp.einsum('rpba,rsbc->rpsac', p_tiles, summed, precision=lax.Precision.H...  9.19 us
    dot_general x1, matrix products, shards(): jnp.einsum('rpba,rsbc->rpsac', p_tiles, summed, precision=lax.Precision.H...  9.03 us
    dot_general x1, matrix products, shards(): jnp.einsum('trp,rpsac->tsac', owner_pick, lifted, precision=lax.Precision...  7.22 us
    ppermute x2, starting transfers between devices, with_halo(): after = lax.ppermute(leading, axis, down)  6.91 us
  transfers between devices with their start and end apart: 20, of which 7 were waited for; matrix products, arithmetic and copies ran while one was open for 5% of the time, Pallas kernels for 0%

commit v1 on v0

v1 whole, which is shorter than its diff:
```python
import functools

import jax
import jax.numpy as jnp
from jax import lax
from jax.experimental import pallas as pl
from jax.experimental.pallas import tpu as pltpu
from jax.sharding import PartitionSpec as P

TILE = 128
A_TILES = 4
P_TILES = 2
CAP = 2
SPAN = 6
SLOTS = 10
ROW = A_TILES * TILE
META = 8
WIDTHS = (SLOTS, SLOTS - 2)

BUFFERS = {
    "far": (((10, 0, ROW), (11, 0, ROW - TILE)), True),
    "up": (((11, ROW - TILE, TILE),), False),
    "d4": (((8, 0, ROW), (9, 0, ROW)), True),
    "d3": (((6, 0, ROW), (7, 0, ROW)), True),
    "d2": (((4, 0, ROW), (5, 0, ROW)), True),
    "d1": (((2, 0, ROW), (3, 0, ROW)), True),
    "d0": (((0, 0, ROW), (1, 0, ROW)), True),
}

ANY = pl.BlockSpec(memory_space=pl.ANY)
SMEM = pl.BlockSpec(memory_space=pltpu.SMEM)
VMEM = pl.BlockSpec(memory_space=pltpu.VMEM)


def hop(value, axis, steps):
    count = lax.axis_size(axis)
    return lax.ppermute(value, axis, [(i, (i + steps) % count) for i in range(count)])


def beside(value, steps):
    count = lax.axis_size("gy")
    route = [(i, i + steps) for i in range(count) if 0 <= i + steps < count]
    return lax.ppermute(value, "gy", route)


def bucket_kernel(rows, gx, per_x, layout, new_row, a_cols, my_x, a_hbm, *refs):
    outs = refs[: len(BUFFERS)]
    held, notes, order, in_sem, out_sem, note_sem = refs[len(BUFFERS) :]
    loads = [pltpu.make_async_copy(a_hbm.at[o], held.at[o], in_sem.at[o]) for o in range(rows)]
    for load in loads:
        load.start()
    for s in range(SPAN * CAP):
        order[s] = -1
    gaps = [lax.rem(lax.div(new_row[o], per_x) - my_x[0] + gx, gx) for o in range(rows)]
    for o in range(rows):
        rank = sum([(gaps[e] == gaps[o]).astype(jnp.int32) for e in range(o)], jnp.int32(0))
        order[gaps[o] * CAP + rank] = o
    lane = lax.broadcasted_iota(jnp.int32, (META, TILE), 1)
    line = lax.broadcasted_iota(jnp.int32, (META, TILE), 0)
    note_copies = []
    for b, (pieces, noted) in enumerate(layout):
        if not noted:
            continue
        note = jnp.zeros((META, TILE), jnp.int32)
        for r, (s, _, _) in enumerate(pieces[:CAP]):
            o = order[s]
            here = jnp.maximum(o, 0)
            place = jnp.where(o >= 0, lax.rem(new_row[here], rows) + 1, 0)
            for k in range(A_TILES):
                note = jnp.where((line == r) & (lane == k), a_cols[here * A_TILES + k], note)
            note = jnp.where((line == r) & (lane == A_TILES), place, note)
        notes[b] = note.astype(jnp.float32)
        size = sum(n for _, _, n in pieces)
        copy = pltpu.make_async_copy(notes.at[b], outs[b].at[pl.ds(size, META)], note_sem.at[b])
        copy.start()
        note_copies.append(copy)
    for load in loads:
        load.wait()

    def each(act):
        n = 0
        for out, (pieces, _) in zip(outs, layout):
            to = 0
            for s, frm, size in pieces:
                o = order[s]
                here = jnp.maximum(o, 0)

                @pl.when(o >= 0)
                def _():
                    act(
                        pltpu.make_async_copy(
                            held.at[here, pl.ds(frm, size)], out.at[pl.ds(to, size)], out_sem.at[n]
                        )
                    )

                to += size
                n += 1

    each(lambda copy: copy.start())
    each(lambda copy: copy.wait())
    for copy in note_copies:
        copy.wait()


def buckets(a_tiles, a_cols, new_row, my_x):
    rows = a_tiles.shape[0]
    gx, gy = lax.axis_size("gx"), lax.axis_size("gy")
    layout = list(BUFFERS.values())
    lengths = [sum(n for _, _, n in pieces) + META * noted for pieces, noted in layout]
    outs = pl.pallas_call(
        functools.partial(bucket_kernel, rows, gx, rows * gy, layout),
        out_shape=[jax.ShapeDtypeStruct((n, TILE), jnp.float32) for n in lengths],
        in_specs=[SMEM, SMEM, SMEM, ANY],
        out_specs=[ANY] * len(lengths),
        scratch_shapes=[
            pltpu.VMEM((rows, ROW, TILE), jnp.float32),
            pltpu.VMEM((len(lengths), META, TILE), jnp.float32),
            pltpu.SMEM((SPAN * CAP,), jnp.int32),
            pltpu.SemaphoreType.DMA((rows,)),
            pltpu.SemaphoreType.DMA((sum(len(p) for p, _ in layout),)),
            pltpu.SemaphoreType.DMA((len(lengths),)),
        ],
        compiler_params=pltpu.CompilerParams(vmem_limit_bytes=4 * 2**20),
        name="buckets",
    )(new_row, a_cols.reshape(-1), my_x, a_tiles.reshape(rows, ROW, TILE))
    return dict(zip(BUFFERS, outs))


def halves(x):
    high = x.astype(jnp.bfloat16)
    return high, (x - high.astype(jnp.float32)).astype(jnp.bfloat16)


def split_kernel(rows, *refs):
    sources, (high, low, turned) = refs[:3], refs[3:]
    for n, source in enumerate(sources):

        def body(i, carry):
            for q in range(P_TILES):
                block = source[pl.ds(pl.multiple_of((i * P_TILES + q) * TILE, TILE), TILE), :]
                h, l = halves(block)
                high[n * rows + i, :, q * TILE : (q + 1) * TILE] = h
                low[n * rows + i, :, q * TILE : (q + 1) * TILE] = l
                if n == 1:
                    h, l = halves(block.T)
                    turned[i * P_TILES + q, :TILE, :] = h
                    turned[i * P_TILES + q, TILE:, :] = l
            return carry

        lax.fori_loop(0, rows, body, 0)


def split(sources, rows):
    wide = jax.ShapeDtypeStruct((3 * rows, TILE, P_TILES * TILE), jnp.bfloat16)
    return pl.pallas_call(
        functools.partial(split_kernel, rows),
        out_shape=[wide, wide, jax.ShapeDtypeStruct((rows * P_TILES, 2 * TILE, TILE), jnp.bfloat16)],
        in_specs=[VMEM] * 3,
        out_specs=[VMEM] * 3,
        name="split",
    )(*sources)


def galerkin_kernel(rows, chunks, targets, fresh, slots, first, high, low, turned, *refs):
    count = sum(len(c) for c in chunks)
    buffers, refs = refs[:count], refs[count:]
    if not fresh:
        befores, refs = refs[: len(targets)], refs[len(targets) :]
    accs, refs = refs[: len(targets)], refs[len(targets) :]
    lifted, held, notes, note_sem, sem = refs
    at, note_copies, lines = 0, [], []
    for n, lengths in enumerate(chunks):
        parts = buffers[at : at + len(lengths)]
        at += len(lengths)
        end = lengths[0][0] - META
        copy = pltpu.make_async_copy(parts[0].at[pl.ds(end, META)], notes.at[n], note_sem.at[n])
        copy.start()
        note_copies.append(copy)
        for r in range(CAP):
            size = min(ROW, end - r * ROW)
            pieces = [(parts[0], r * ROW, 0, size)]
            if size < ROW:
                pieces.append((parts[1], lengths[1][1], size, ROW - size))
            lines.append((n, r, pieces))
    for i, acc in enumerate(accs):
        if fresh:
            acc[...] = jnp.zeros_like(acc)
        else:
            acc[...] = befores[i][...]
    for copy in note_copies:
        copy.wait()

    def note(n, r, k):
        return notes[n, r, k].astype(jnp.int32)

    def copies(m):
        return [
            pltpu.make_async_copy(
                part.at[pl.ds(frm, size)], held.at[m, pl.ds(to, size)], sem.at[2 * m + i]
            )
            for i, (part, frm, to, size) in enumerate(lines[m][2])
        ]

    for m, (n, r, _) in enumerate(lines):

        @pl.when(note(n, r, A_TILES) > 0)
        def _():
            for copy in copies(m):
                copy.start()

    for m, (n, r, _) in enumerate(lines):

        @pl.when(note(n, r, A_TILES) > 0)
        def _():
            for copy in copies(m):
                copy.wait()
            row = note(n, r, A_TILES) - 1
            cols = [note(n, r, k) - first[0] for k in range(A_TILES)]
            for k, c in enumerate(cols):
                h, l = halves(held[m, k * TILE : (k + 1) * TILE, :])
                left = jnp.concatenate([h, l], axis=1)
                t = jnp.dot(
                    left, jnp.concatenate([high[c], high[c]], axis=0), preferred_element_type=jnp.float32
                ) + jnp.dot(
                    left, jnp.concatenate([low[c], low[c]], axis=0), preferred_element_type=jnp.float32
                )
                h, l = halves(t)
                span = slice(k * P_TILES * TILE, (k + 1) * P_TILES * TILE)
                lifted[:TILE, span] = h
                lifted[TILE:, span] = l
            for p in range(P_TILES):
                for target, acc in zip(targets, accs):
                    mine = slots[rows + row, p] - 4 - 2 * target

                    @pl.when((mine == 0) | (mine == 1))
                    def _():
                        left = turned[row * P_TILES + p]
                        w = jnp.dot(
                            jnp.concatenate([left, left], axis=1), lifted[...], preferred_element_type=jnp.float32
                        )
                        w = w[:TILE] + w[TILE:]
                        for k, c in enumerate(cols):
                            for q in range(P_TILES):
                                lanes = (k * P_TILES + q) * TILE
                                s = mine * WIDTHS[target] + slots[c, q] - 2 * target
                                acc[s] += w[:, lanes : lanes + TILE]


def galerkin(weight, chunks, targets, first_row, slots, splits, befores, rows, coarse_rows):
    shapes = [tuple((x.shape[0], frm) for x, frm in parts) for parts in chunks]
    buffers = [x for parts in chunks for x, _ in parts]
    out = [jax.ShapeDtypeStruct((coarse_rows * WIDTHS[t], TILE, TILE), jnp.float32) for t in targets]
    befores = befores or []
    operands = [slots, first_row, *splits, *buffers, *befores]
    specs = [SMEM, SMEM] + [VMEM] * len(splits) + [ANY] * len(buffers) + [VMEM] * len(befores)
    lines = CAP * len(chunks)
    return pl.pallas_call(
        functools.partial(galerkin_kernel, rows, shapes, targets, not befores),
        out_shape=out,
        in_specs=specs,
        out_specs=[VMEM] * len(out),
        scratch_shapes=[
            pltpu.VMEM((2 * TILE, A_TILES * P_TILES * TILE), jnp.bfloat16),
            pltpu.VMEM((lines, ROW, TILE), jnp.float32),
            pltpu.SMEM((len(chunks), META, TILE), jnp.float32),
            pltpu.SemaphoreType.DMA((len(chunks),)),
            pltpu.SemaphoreType.DMA((2 * lines,)),
        ],
        input_output_aliases={len(operands) - len(befores) + i: i for i in range(len(befores))},
        compiler_params=pltpu.CompilerParams(vmem_limit_bytes=20 * 2**20),
        cost_estimate=pl.CostEstimate(flops=weight, bytes_accessed=1, transcendentals=0),
        name="galerkin",
    )(*operands)


def after(value, *others):
    return lax.optimization_barrier((value, *others))[0]


def shards(a_tiles, a_cols, new_row, p_tiles, p_cols):
    rows = a_tiles.shape[0]
    coarse_rows = rows // 4
    my_x = lax.axis_index("gx").astype(jnp.int32)
    device = my_x * lax.axis_size("gy") + lax.axis_index("gy").astype(jnp.int32)

    p_notes = jnp.pad(p_cols.astype(jnp.float32), ((0, 0), (0, TILE - P_TILES)))
    p_here = jnp.concatenate([p_tiles.reshape(-1, TILE), p_notes], axis=0)
    sources = [beside(p_here, 1), p_here, beside(p_here, -1)]

    send = buckets(a_tiles, a_cols, new_row, my_x.reshape(1))
    d1 = hop(after(send["d1"], sources[2], sources[0]), "gx", 1)
    d2 = hop(after(send["d2"], sources[0]), "gx", 2)
    d3 = hop(send["d3"], "gx", 3)
    d4 = hop(send["d4"], "gx", 4)
    far = hop(send["far"], "gx", -6)

    slots = jnp.concatenate([x[-rows:, :P_TILES] for x in sources], axis=0).astype(jnp.int32)
    slots = slots - coarse_rows * device + 4
    splits = split(sources, rows)
    first_row = ((device - 1) * rows).reshape(1)

    def add(targets, chunks, befores, weight=1):
        return galerkin(weight, chunks, targets, first_row, slots, splits, befores, rows, coarse_rows)

    both = add((0, 1), [[(send["d0"], 0)]], None, 10**14)
    up = hop(after(send["up"], far, both[0]), "gx", 5)
    far = hop(after(far, both[0]), "gx", -5)
    both = add((0, 1), [[(d4, 0)]], both)
    both = add((0, 1), [[(d3, 0)]], both)
    own, on = add((0, 1), [[(d2, 0)]], both)
    last = [[(d1, 0)], [(far, 0), (up, 0)]]
    (on,) = add((1,), last, [on])
    arrived = beside(on, 1)
    (own,) = add((0,), last, [own])
    own = own.reshape(coarse_rows, SLOTS, TILE, TILE)
    arrived = arrived.reshape(coarse_rows, WIDTHS[1], TILE, TILE)
    return own + jnp.pad(arrived, ((0, 0), (0, SLOTS - WIDTHS[1]), (0, 0), (0, 0)))


def solution(mesh):
    in_specs = (
        P(("gx", "gy"), None, None, None),
        P(("gx", "gy"), None),
        P(("gx", "gy")),
        P(("gx", "gy"), None, None, None),
        P(("gx", "gy"), None),
    )
    out_specs = P(("gx", "gy"), None, None, None)
    return jax.shard_map(shards, mesh=mesh, in_specs=in_specs, out_specs=out_specs, check_vma=False)
```

time: 342 us -> 179 us (0.52)
  the two profiles are of different devices: /device:TPU:38 before, /device:TPU:6 now
where the time goes in v1:
time: 179 us; the launch traced here: 177 us
  waiting for transfers between devices  75.3 us (42%)
  starting transfers between devices  62.6 us (35%)
  Pallas kernels  28.9 us (16%)
  local copies, waits for them, and re-layouts  6.47 us (4%)
  other arithmetic  3.47 us (2%)
    ppermute x7, waiting for transfers between devices, hop(): lax.ppermute(value, axis, [(i, (i + steps) % count) for i in range(count)])  62.2 us
    ppermute x7, starting transfers between devices, hop(): lax.ppermute(value, axis, [(i, (i + steps) % count) for i in range(count)])  54.2 us
    pallas_call x6, Pallas kernels, galerkin(): pl.pallas_call(functools.partial(galerkin_kernel, rows, shapes, targets,...  21.4 us
    ppermute x3, waiting for transfers between devices, beside(): return lax.ppermute(value, 'gy', route)  13 us
    ppermute x3, starting transfers between devices, beside(): return lax.ppermute(value, 'gy', route)  8.46 us
    pallas_call x1, Pallas kernels, split(): pl.pallas_call(functools.partial(split_kernel, rows), out_shape=[wide, wi...  5.05 us
    unnamed x14, local copies, waits for them, and re-layouts  5.04 us
  transfers between devices with their start and end apart: 10, of which 4 were waited for; matrix products, arithmetic and copies ran while one was open for 1% of the time, Pallas kernels for 14%

profile of v1, /device:TPU:6, one launch (start us, length us, event | category | flops | bytes accessed | tf_op | source)
XLA Modules:
  0.0 176.9 jit_solution(13641570241786114604)
XLA Ops:
  0.0 0.0 copy-start.5
  0.0 0.0 copy-start.4
  0.0 0.0 copy-start.3
  0.0 0.9 copy.24
  0.9 2.3 %select_maximum_fusion.refs_1_ = f32[2056,128]{1,0:T(8,128)} fusion(f32[8,2]{1,0:T(8,128)S(1)} %convert_element_type.10, f32[2048,128]{1,0:T(8,128)} %bitcast.9), kind=kLoop, calls=%fused_computation.1 | loop fusion | flops 789504 | bytes 2101312 | tf_op jit(solution)/shard_map/concatenate | solution.py:287
  3.2 4.6 %collective-permute-start.1 = (f32[2056,128]{1,0:T(8,128)}, f32[2056,128]{1,0:T(8,128)}, u32[]{:S(2)}, u32[]{:S(2)}) collective-permute-start(f32[2056,128]{1,0:T(8,128)} %select_maximum_fusion.refs_1_), channel_id=1, source_target_pairs={{1,0},{2,1},{3,2},{4,3},{5,4},{6,5},{7,6},{8,7},{9,8},{10,9},{11,1... | collective-permute-start | bytes 3158024 | tf_op jit(solution)/shard_map/ppermute | solution.py:43
  7.8 1.9 %collective-permute-start = (f32[2056,128]{1,0:T(8,128)}, f32[2056,128]{1,0:T(8,128)}, u32[]{:S(2)}, u32[]{:S(2)}) collective-permute-start(f32[2056,128]{1,0:T(8,128)} %select_maximum_fusion.refs_1_), channel_id=1, source_target_pairs={{0,1},{1,2},{2,3},{3,4},{4,5},{5,6},{6,7},{7,8},{8,9},{9,10},{10,1... | collective-permute-start | bytes 3158024 | tf_op jit(solution)/shard_map/ppermute | solution.py:43
  9.7 0.0 copy-done.5
  9.8 0.1 copy.25
  9.8 0.1 reshape.23.a_cols
  9.9 0.0 copy-done.4
  9.9 0.0 copy-done.3
  9.9 2.5 %buckets.1 = (f32[904,128]{1,0:T(8,128)}, f32[128,128]{1,0:T(8,128)S(1)}, f32[1032,128]{1,0:T(8,128)}, f32[1032,128]{1,0:T(8,128)}, f32[1032,128]{1,0:T(8,128)},...) custom-call(s32[8]{0:T(128)S(1)} %copy-done.4, s32[32]{0:T(128)S(1)} %reshape.23.a_cols, s32[1]{0:T(128)} %bitcast.2.my_x, ...), custom_call_target="tpu_custom_call" | custom-call | tf_op jit(solution)/shard_map/buckets/pallas_call | solution.py:110
  12.4 14.8 %collective-permute-start.3 = (f32[904,128]{1,0:T(8,128)}, f32[904,128]{1,0:T(8,128)}, u32[]{:S(2)}, u32[]{:S(2)}) collective-permute-start(f32[904,128]{1,0:T(8,128)} %get-tuple-element.32), channel_id=1, source_target_pairs={{0,320},{32,352},{64,384},{96,416},{128,448},{160,480},{192,0},{22... | collective-permute-start | bytes 1388552 | tf_op jit(solution)/shard_map/ppermute | solution.py:37
  27.2 2.6 %collective-permute-start.7 = (f32[1032,128]{1,0:T(8,128)}, f32[1032,128]{1,0:T(8,128)}, u32[]{:S(2)}, u32[]{:S(2)}) collective-permute-start(f32[1032,128]{1,0:T(8,128)} %get-tuple-element.40), channel_id=1, source_target_pairs={{0,96},{32,128},{64,160},{96,192},{128,224},{160,256},{192,288},{2... | collective-permute-start | bytes 1585160 | tf_op jit(solution)/shard_map/ppermute | solution.py:37
  29.9 3.6 %collective-permute-start.8 = (f32[1032,128]{1,0:T(8,128)}, f32[1032,128]{1,0:T(8,128)}, u32[]{:S(2)}, u32[]{:S(2)}) collective-permute-start(f32[1032,128]{1,0:T(8,128)} %get-tuple-element.41), channel_id=1, source_target_pairs={{0,128},{32,160},{64,192},{96,224},{128,256},{160,288},{192,320},{... | collective-permute-start | bytes 1585160 | tf_op jit(solution)/shard_map/ppermute | solution.py:37
  33.5 0.0 collective-permute-done.1.refs_2_
  33.5 0.0 collective-permute-done.refs_0_
  33.5 2.9 %collective-permute-start.6 = (f32[1032,128]{1,0:T(8,128)}, f32[1032,128]{1,0:T(8,128)}, u32[]{:S(2)}, u32[]{:S(2)}) collective-permute-start(f32[1032,128]{1,0:T(8,128)} %get-tuple-element.39), channel_id=1, source_target_pairs={{0,64},{32,96},{64,128},{96,160},{128,192},{160,224},{192,256},{22... | collective-permute-start | bytes 1585160 | tf_op jit(solution)/shard_map/ppermute | solution.py:37
  36.4 2.0 %collective-permute-start.2 = (f32[1032,128]{1,0:T(8,128)}, f32[1032,128]{1,0:T(8,128)}, u32[]{:S(2)}, u32[]{:S(2)}) collective-permute-start(f32[1032,128]{1,0:T(8,128)} %get-tuple-element.31), channel_id=1, source_target_pairs={{0,32},{32,64},{64,96},{96,128},{128,160},{160,192},{192,224},{224... | collective-permute-start | bytes 1585160 | tf_op jit(solution)/shard_map/ppermute | solution.py:37
  38.4 0.7 slice.10
  39.1 0.7 slice.9
  39.8 5.0 %split.1 = (bf16[24,128,256]{2,1,0:T(8,128)(2,1)}, bf16[24,128,256]{2,1,0:T(8,128)(2,1)}, bf16[16,256,128]{2,1,0:T(8,128)(2,1)}) custom-call(f32[2056,128]{1,0:T(8,128)} %collective-permute-done.refs_0_, f32[2056,128]{1,0:T(8,128)} %select_maximum_fusion.refs_1_, f32[2056,128]{1,0:T(8,128)} %collective-permute-done.1.refs_2_), custom_call_target="tpu_custom_call" | custom-call | tf_op jit(solution)/shard_map/split/pallas_call | solution.py:155
  44.8 0.0 copy-start
  44.9 1.4 copy-done
  46.3 0.0 copy-start.1
  46.3 1.4 copy-done.1
  47.7 0.0 copy-start.2
  47.7 1.2 copy-done.2
  48.9 1.4 galerkin.6
  50.3 35.6 %collective-permute-done.3 = f32[904,128]{1,0:T(8,128)} collective-permute-done((f32[904,128]{1,0:T(8,128)}, f32[904,128]{1,0:T(8,128)}, u32[]{:S(2)}, u32[]{:S(2)}) %collective-permute-start.3) | collective-permute-done | bytes 462880 | tf_op jit(solution)/shard_map/ppermute | solution.py:37
  85.9 9.4 %collective-permute-start.4 = (f32[904,128]{1,0:T(8,128)}, f32[904,128]{1,0:T(8,128)S(1)}, u32[]{:S(2)}, u32[]{:S(2)}) collective-permute-start(f32[904,128]{1,0:T(8,128)} %collective-permute-done.3), channel_id=1, source_target_pairs={{0,352},{32,384},{64,416},{96,448},{128,480},{160,0},{192,32},{224... | collective-permute-start | bytes 1388552 | tf_op jit(solution)/shard_map/ppermute | solution.py:37
  95.4 12.0 %collective-permute-done.8.refs_0_ = f32[1032,128]{1,0:T(8,128)} collective-permute-done((f32[1032,128]{1,0:T(8,128)}, f32[1032,128]{1,0:T(8,128)}, u32[]{:S(2)}, u32[]{:S(2)}) %collective-permute-start.8) | collective-permute-done | bytes 528416 | tf_op jit(solution)/shard_map/ppermute | solution.py:37
  107.3 18.8 %collective-permute-start.5 = (f32[128,128]{1,0:T(8,128)S(1)}, f32[128,128]{1,0:T(8,128)S(1)}, u32[]{:S(2)}, u32[]{:S(2)}) collective-permute-start(f32[128,128]{1,0:T(8,128)S(1)} %get-tuple-element.37), channel_id=1, source_target_pairs={{0,160},{32,192},{64,224},{96,256},{128,288},{160,320},{192,352},{... | collective-permute-start | bytes 196616 | tf_op jit(solution)/shard_map/ppermute | solution.py:37
  126.1 4.4 %galerkin.7 = (f32[20,128,128]{2,1,0:T(8,128)S(1)}, f32[16,128,128]{2,1,0:T(8,128)S(1)}) custom-call(s32[24,2]{1,0:T(8,128)S(1)} %fusion.1.slots, s32[1]{0:T(128)} %bitcast.1.first, bf16[24,128,256]{2,1,0:T(8,128)(2,1)S(1)} %copy-done, bf16[24,128,256]{2,1,0:T(8,128)(2,1)S(1)} %copy-done.1, ...), custom_call_target="tpu_custom_call", output_to_operand_aliasing={{0}: (6, {}), {1}: (7, {})} | custom-call | flops 1 | bytes 1 | tf_op jit(solution)/shard_map/galerkin/pallas_call | solution.py:257
  130.6 0.0 collective-permute-done.7.refs_0_
  130.6 4.4 %galerkin.8 = (f32[20,128,128]{2,1,0:T(8,128)S(1)}, f32[16,128,128]{2,1,0:T(8,128)S(1)}) custom-call(s32[24,2]{1,0:T(8,128)S(1)} %fusion.1.slots, s32[1]{0:T(128)} %bitcast.1.first, bf16[24,128,256]{2,1,0:T(8,128)(2,1)S(1)} %copy-done, bf16[24,128,256]{2,1,0:T(8,128)(2,1)S(1)} %copy-done.1, ...), custom_call_target="tpu_custom_call", output_to_operand_aliasing={{0}: (6, {}), {1}: (7, {})} | custom-call | flops 1 | bytes 1 | tf_op jit(solution)/shard_map/galerkin/pallas_call | solution.py:257
  135.0 0.0 collective-permute-done.6.refs_0_
  135.0 4.4 %galerkin.9 = (f32[20,128,128]{2,1,0:T(8,128)S(1)}, f32[16,128,128]{2,1,0:T(8,128)S(1)}) custom-call(s32[24,2]{1,0:T(8,128)S(1)} %fusion.1.slots, s32[1]{0:T(128)} %bitcast.1.first, bf16[24,128,256]{2,1,0:T(8,128)(2,1)S(1)} %copy-done, bf16[24,128,256]{2,1,0:T(8,128)(2,1)S(1)} %copy-done.1, ...), custom_call_target="tpu_custom_call", output_to_operand_aliasing={{0}: (6, {}), {1}: (7, {})} | custom-call | flops 1 | bytes 1 | tf_op jit(solution)/shard_map/galerkin/pallas_call | solution.py:257
  139.4 14.6 %collective-permute-done.5.refs_2_ = f32[128,128]{1,0:T(8,128)S(1)} collective-permute-done((f32[128,128]{1,0:T(8,128)S(1)}, f32[128,128]{1,0:T(8,128)S(1)}, u32[]{:S(2)}, u32[]{:S(2)}) %collective-permute-start.5) | collective-permute-done | bytes 65568 | tf_op jit(solution)/shard_map/ppermute | solution.py:37
  154.1 0.0 collective-permute-done.4.refs_1_
  154.1 0.0 collective-permute-done.2.refs_0_
  154.1 3.4 %galerkin.11 = f32[16,128,128]{2,1,0:T(8,128)S(1)} custom-call(s32[24,2]{1,0:T(8,128)S(1)} %fusion.1.slots, s32[1]{0:T(128)} %bitcast.1.first, bf16[24,128,256]{2,1,0:T(8,128)(2,1)S(1)} %copy-done, bf16[24,128,256]{2,1,0:T(8,128)(2,1)S(1)} %copy-done.1, bf16[16,256,128]{2,1,0:T(8,128)(2,1)S(1)} %copy-done.2, ...), custom_call_target="tpu_custom_call", output_to_operand_aliasing={{}: (8, {})} | custom-call | flops 1 | bytes 1 | tf_op jit(solution)/shard_map/galerkin/pallas_call | solution.py:257
  157.5 1.9 %collective-permute-start.9 = (f32[16,128,128]{2,1,0:T(8,128)S(1)}, f32[16,128,128]{2,1,0:T(8,128)S(1)}, u32[]{:S(2)}, u32[]{:S(2)}) collective-permute-start(f32[16,128,128]{2,1,0:T(8,128)S(1)} %galerkin.11), channel_id=1, source_target_pairs={{0,1},{1,2},{2,3},{3,4},{4,5},{5,6},{6,7},{7,8},{8,9},{9,10},{10,1... | collective-permute-start | bytes 3145736 | tf_op jit(solution)/shard_map/ppermute | solution.py:43
  159.4 3.3 %galerkin.10 = f32[20,128,128]{2,1,0:T(8,128)S(1)} custom-call(s32[24,2]{1,0:T(8,128)S(1)} %fusion.1.slots, s32[1]{0:T(128)} %bitcast.1.first, bf16[24,128,256]{2,1,0:T(8,128)(2,1)S(1)} %copy-done, bf16[24,128,256]{2,1,0:T(8,128)(2,1)S(1)} %copy-done.1, bf16[16,256,128]{2,1,0:T(8,128)(2,1)S(1)} %copy-done.2, ...), custom_call_target="tpu_custom_call", output_to_operand_aliasing={{}: (8, {})} | custom-call | flops 1 | bytes 1 | tf_op jit(solution)/shard_map/galerkin/pallas_call | solution.py:257
  162.7 13.0 %collective-permute-done.9 = f32[16,128,128]{2,1,0:T(8,128)S(1)} collective-permute-done((f32[16,128,128]{2,1,0:T(8,128)S(1)}, f32[16,128,128]{2,1,0:T(8,128)S(1)}, u32[]{:S(2)}, u32[]{:S(2)}) %collective-permute-start.9) | collective-permute-done | bytes 1048608 | tf_op jit(solution)/shard_map/ppermute | solution.py:43
  175.7 1.2 pad_add_fusion
  (2 shorter events, 0.0 us)
Async XLA Ops:
  0.0 9.7 %copy-start.5 = (s32[8,4]{0,1:T(4,128)S(1)}, s32[8,4]{0,1:T(4,128)}, u32[]{:S(2)}) copy-start(s32[8,4]{0,1:T(4,128)} %param.6) | copy-start | bytes 388
  0.0 9.9 %copy-start.4 = (s32[8]{0:T(128)S(1)}, s32[8]{0:T(128)}, u32[]{:S(2)}) copy-start(s32[8]{0:T(128)} %new_row.1) | copy-start | bytes 100
  0.0 9.9 %copy-start.3 = (f32[8,4,128,128]{3,2,1,0:T(8,128)S(1)}, f32[8,4,128,128]{3,2,1,0:T(8,128)}, u32[]{:S(2)}) copy-start(f32[8,4,128,128]{3,2,1,0:T(8,128)} %param.5) | copy-start | bytes 6291460
  3.2 30.3 %collective-permute-start.1 = (f32[2056,128]{1,0:T(8,128)}, f32[2056,128]{1,0:T(8,128)}, u32[]{:S(2)}, u32[]{:S(2)}) collective-permute-start(f32[2056,128]{1,0:T(8,128)} %select_maximum_fusion.refs_1_), channel_id=1, source_target_pairs={{1,0},{2,1},{3,2},{4,3},{5,4},{6,5},{7,6},{8,7},{9,8},{10,9},{11,1... | collective-permute-start | bytes 3158024 | tf_op jit(solution)/shard_map/ppermute | solution.py:43
  7.8 25.7 %collective-permute-start = (f32[2056,128]{1,0:T(8,128)}, f32[2056,128]{1,0:T(8,128)}, u32[]{:S(2)}, u32[]{:S(2)}) collective-permute-start(f32[2056,128]{1,0:T(8,128)} %select_maximum_fusion.refs_1_), channel_id=1, source_target_pairs={{0,1},{1,2},{2,3},{3,4},{4,5},{5,6},{6,7},{7,8},{8,9},{9,10},{10,1... | collective-permute-start | bytes 3158024 | tf_op jit(solution)/shard_map/ppermute | solution.py:43
  12.4 73.5 %collective-permute-start.3 = (f32[904,128]{1,0:T(8,128)}, f32[904,128]{1,0:T(8,128)}, u32[]{:S(2)}, u32[]{:S(2)}) collective-permute-start(f32[904,128]{1,0:T(8,128)} %get-tuple-element.32), channel_id=1, source_target_pairs={{0,320},{32,352},{64,384},{96,416},{128,448},{160,480},{192,0},{22... | collective-permute-start | bytes 1388552 | tf_op jit(solution)/shard_map/ppermute | solution.py:37
  27.2 103.3 %collective-permute-start.7 = (f32[1032,128]{1,0:T(8,128)}, f32[1032,128]{1,0:T(8,128)}, u32[]{:S(2)}, u32[]{:S(2)}) collective-permute-start(f32[1032,128]{1,0:T(8,128)} %get-tuple-element.40), channel_id=1, source_target_pairs={{0,96},{32,128},{64,160},{96,192},{128,224},{160,256},{192,288},{2... | collective-permute-start | bytes 1585160 | tf_op jit(solution)/shard_map/ppermute | solution.py:37
  29.9 77.5 %collective-permute-start.8 = (f32[1032,128]{1,0:T(8,128)}, f32[1032,128]{1,0:T(8,128)}, u32[]{:S(2)}, u32[]{:S(2)}) collective-permute-start(f32[1032,128]{1,0:T(8,128)} %get-tuple-element.41), channel_id=1, source_target_pairs={{0,128},{32,160},{64,192},{96,224},{128,256},{160,288},{192,320},{... | collective-permute-start | bytes 1585160 | tf_op jit(solution)/shard_map/ppermute | solution.py:37
  33.5 101.5 %collective-permute-start.6 = (f32[1032,128]{1,0:T(8,128)}, f32[1032,128]{1,0:T(8,128)}, u32[]{:S(2)}, u32[]{:S(2)}) collective-permute-start(f32[1032,128]{1,0:T(8,128)} %get-tuple-element.39), channel_id=1, source_target_pairs={{0,64},{32,96},{64,128},{96,160},{128,192},{160,224},{192,256},{22... | collective-permute-start | bytes 1585160 | tf_op jit(solution)/shard_map/ppermute | solution.py:37
  36.4 117.6 %collective-permute-start.2 = (f32[1032,128]{1,0:T(8,128)}, f32[1032,128]{1,0:T(8,128)}, u32[]{:S(2)}, u32[]{:S(2)}) collective-permute-start(f32[1032,128]{1,0:T(8,128)} %get-tuple-element.31), channel_id=1, source_target_pairs={{0,32},{32,64},{64,96},{96,128},{128,160},{160,192},{192,224},{224... | collective-permute-start | bytes 1585160 | tf_op jit(solution)/shard_map/ppermute | solution.py:37
  44.8 1.4 copy-start
  46.3 1.4 copy-start.1
  47.7 1.2 copy-start.2
  85.9 68.1 %collective-permute-start.4 = (f32[904,128]{1,0:T(8,128)}, f32[904,128]{1,0:T(8,128)S(1)}, u32[]{:S(2)}, u32[]{:S(2)}) collective-permute-start(f32[904,128]{1,0:T(8,128)} %collective-permute-done.3), channel_id=1, source_target_pairs={{0,352},{32,384},{64,416},{96,448},{128,480},{160,0},{192,32},{224... | collective-permute-start | bytes 1388552 | tf_op jit(solution)/shard_map/ppermute | solution.py:37
  107.3 46.7 %collective-permute-start.5 = (f32[128,128]{1,0:T(8,128)S(1)}, f32[128,128]{1,0:T(8,128)S(1)}, u32[]{:S(2)}, u32[]{:S(2)}) collective-permute-start(f32[128,128]{1,0:T(8,128)S(1)} %get-tuple-element.37), channel_id=1, source_target_pairs={{0,160},{32,192},{64,224},{96,256},{128,288},{160,320},{192,352},{... | collective-permute-start | bytes 196616 | tf_op jit(solution)/shard_map/ppermute | solution.py:37
  157.5 18.2 %collective-permute-start.9 = (f32[16,128,128]{2,1,0:T(8,128)S(1)}, f32[16,128,128]{2,1,0:T(8,128)S(1)}, u32[]{:S(2)}, u32[]{:S(2)}) collective-permute-start(f32[16,128,128]{2,1,0:T(8,128)S(1)} %galerkin.11), channel_id=1, source_target_pairs={{0,1},{1,2},{2,3},{3,4},{4,5},{5,6},{6,7},{7,8},{8,9},{9,10},{10,1... | collective-permute-start | bytes 3145736 | tf_op jit(solution)/shard_map/ppermute | solution.py:43

commit v2 on v1

--- a/solution.py
+++ b/solution.py
@@ -18,16 +18,17 @@
 WIDTHS = (SLOTS, SLOTS - 2)
 
 BUFFERS = {
-    "far": (((10, 0, ROW), (11, 0, ROW - TILE)), True),
-    "up": (((11, ROW - TILE, TILE),), False),
-    "d4": (((8, 0, ROW), (9, 0, ROW)), True),
+    "far_a": (((10, 0, ROW),), True),
+    "far_b": (((11, 0, ROW - TILE),), True),
+    "d4": (((8, 0, ROW), (9, 0, ROW), (11, ROW - TILE, TILE)), True),
     "d3": (((6, 0, ROW), (7, 0, ROW)), True),
     "d2": (((4, 0, ROW), (5, 0, ROW)), True),
-    "d1": (((2, 0, ROW), (3, 0, ROW)), True),
+    "d1": (((2, 0, ROW), (3, 0, ROW), (None, 0, TILE)), True),
     "d0": (((0, 0, ROW), (1, 0, ROW)), True),
 }
 
 ANY = pl.BlockSpec(memory_space=pl.ANY)
+HBM = pl.BlockSpec(memory_space=pltpu.MemorySpace.HBM)
 SMEM = pl.BlockSpec(memory_space=pltpu.SMEM)
 VMEM = pl.BlockSpec(memory_space=pltpu.VMEM)
 
@@ -43,9 +44,12 @@
     return lax.ppermute(value, "gy", route)
 
 
-def bucket_kernel(rows, gx, per_x, layout, new_row, a_cols, my_x, a_hbm, *refs):
-    outs = refs[: len(BUFFERS)]
-    held, notes, order, in_sem, out_sem, note_sem = refs[len(BUFFERS) :]
+def bucket_kernel(rows, gx, per_x, layout, new_row, a_cols, p_cols, my_x, a_hbm, p_hbm, *refs):
+    p_out, outs = refs[0], refs[1 : 1 + len(BUFFERS)]
+    held, held_p, notes, order, in_sem, out_sem, note_sem, p_sem = refs[1 + len(BUFFERS) :]
+    p_size = rows * P_TILES * TILE
+    p_load = pltpu.make_async_copy(p_hbm, held_p.at[pl.ds(0, p_size)], p_sem)
+    p_load.start()
     loads = [pltpu.make_async_copy(a_hbm.at[o], held.at[o], in_sem.at[o]) for o in range(rows)]
     for load in loads:
         load.start()
@@ -67,13 +71,21 @@
             here = jnp.maximum(o, 0)
             place = jnp.where(o >= 0, lax.rem(new_row[here], rows) + 1, 0)
             for k in range(A_TILES):
-                note = jnp.where((line == r) & (lane == k), a_cols[here * A_TILES + k], note)
+                note = jnp.where((line == r) & (lane == k), a_cols[here, k], note)
             note = jnp.where((line == r) & (lane == A_TILES), place, note)
         notes[b] = note.astype(jnp.float32)
         size = sum(n for _, _, n in pieces)
         copy = pltpu.make_async_copy(notes.at[b], outs[b].at[pl.ds(size, META)], note_sem.at[b])
         copy.start()
         note_copies.append(copy)
+    note = jnp.zeros((META, TILE), jnp.int32)
+    for i in range(rows):
+        for q in range(P_TILES):
+            note = jnp.where((line == i) & (lane == q), p_cols[i, q], note)
+    held_p[p_size:, :] = note.astype(jnp.float32)
+    p_load.wait()
+    p_copy = pltpu.make_async_copy(held_p, p_out, p_sem)
+    p_copy.start()
     for load in loads:
         load.wait()
 
@@ -82,6 +94,8 @@
         for out, (pieces, _) in zip(outs, layout):
             to = 0
             for s, frm, size in pieces:
+                if s is None:
+                    continue
                 o = order[s]
                 here = jnp.maximum(o, 0)
 
@@ -100,30 +114,34 @@
     each(lambda copy: copy.wait())
     for copy in note_copies:
         copy.wait()
-
-
-def buckets(a_tiles, a_cols, new_row, my_x):
+    p_copy.wait()
+
+
+def buckets(a_tiles, a_cols, new_row, p_tiles, p_cols, my_x):
     rows = a_tiles.shape[0]
     gx, gy = lax.axis_size("gx"), lax.axis_size("gy")
     layout = list(BUFFERS.values())
     lengths = [sum(n for _, _, n in pieces) + META * noted for pieces, noted in layout]
-    outs = pl.pallas_call(
+    p_lines = rows * P_TILES * TILE
+    p_here, *outs = pl.pallas_call(
         functools.partial(bucket_kernel, rows, gx, rows * gy, layout),
-        out_shape=[jax.ShapeDtypeStruct((n, TILE), jnp.float32) for n in lengths],
-        in_specs=[SMEM, SMEM, SMEM, ANY],
-        out_specs=[ANY] * len(lengths),
+        out_shape=[jax.ShapeDtypeStruct((n, TILE), jnp.float32) for n in [p_lines + META] + lengths],
+        in_specs=[SMEM, SMEM, SMEM, SMEM, HBM, HBM],
+        out_specs=[HBM] * (1 + len(lengths)),
         scratch_shapes=[
             pltpu.VMEM((rows, ROW, TILE), jnp.float32),
+            pltpu.VMEM((p_lines + META, TILE), jnp.float32),
             pltpu.VMEM((len(lengths), META, TILE), jnp.float32),
             pltpu.SMEM((SPAN * CAP,), jnp.int32),
             pltpu.SemaphoreType.DMA((rows,)),
             pltpu.SemaphoreType.DMA((sum(len(p) for p, _ in layout),)),
             pltpu.SemaphoreType.DMA((len(lengths),)),
+            pltpu.SemaphoreType.DMA,
         ],
-        compiler_params=pltpu.CompilerParams(vmem_limit_bytes=4 * 2**20),
+        compiler_params=pltpu.CompilerParams(vmem_limit_bytes=5 * 2**20),
         name="buckets",
-    )(new_row, a_cols.reshape(-1), my_x, a_tiles.reshape(rows, ROW, TILE))
-    return dict(zip(BUFFERS, outs))
+    )(new_row, a_cols, p_cols, my_x, a_tiles.reshape(rows, ROW, TILE), p_tiles.reshape(p_lines, TILE))
+    return p_here, dict(zip(BUFFERS, outs))
 
 
 def halves(x):
@@ -157,6 +175,7 @@
         out_shape=[wide, wide, jax.ShapeDtypeStruct((rows * P_TILES, 2 * TILE, TILE), jnp.bfloat16)],
         in_specs=[VMEM] * 3,
         out_specs=[VMEM] * 3,
+        compiler_params=pltpu.CompilerParams(vmem_limit_bytes=12 * 2**20),
         name="split",
     )(*sources)
 
@@ -176,7 +195,7 @@
         copy = pltpu.make_async_copy(parts[0].at[pl.ds(end, META)], notes.at[n], note_sem.at[n])
         copy.start()
         note_copies.append(copy)
-        for r in range(CAP):
+        for r in range(min(CAP, -(-end // ROW))):
             size = min(ROW, end - r * ROW)
             pieces = [(parts[0], r * ROW, 0, size)]
             if size < ROW:
@@ -253,7 +272,7 @@
     befores = befores or []
     operands = [slots, first_row, *splits, *buffers, *befores]
     specs = [SMEM, SMEM] + [VMEM] * len(splits) + [ANY] * len(buffers) + [VMEM] * len(befores)
-    lines = CAP * len(chunks)
+    lines = sum(min(CAP, -(-(parts[0][0] - META) // ROW)) for parts in shapes)
     return pl.pallas_call(
         functools.partial(galerkin_kernel, rows, shapes, targets, not befores),
         out_shape=out,
@@ -283,16 +302,15 @@
     my_x = lax.axis_index("gx").astype(jnp.int32)
     device = my_x * lax.axis_size("gy") + lax.axis_index("gy").astype(jnp.int32)
 
-    p_notes = jnp.pad(p_cols.astype(jnp.float32), ((0, 0), (0, TILE - P_TILES)))
-    p_here = jnp.concatenate([p_tiles.reshape(-1, TILE), p_notes], axis=0)
-    sources = [beside(p_here, 1), p_here, beside(p_here, -1)]
-
-    send = buckets(a_tiles, a_cols, new_row, my_x.reshape(1))
-    d1 = hop(after(send["d1"], sources[2], sources[0]), "gx", 1)
-    d2 = hop(after(send["d2"], sources[0]), "gx", 2)
-    d3 = hop(send["d3"], "gx", 3)
+    p_here, send = buckets(a_tiles, a_cols, new_row, p_tiles, p_cols, my_x.reshape(1))
+    p_before = beside(p_here, 1)
+    p_after = beside(p_here, -1)
+    sources = [p_before, p_here, p_after]
     d4 = hop(send["d4"], "gx", 4)
-    far = hop(send["far"], "gx", -6)
+    far_a = hop(send["far_a"], "gx", -6)
+    d3 = hop(after(send["d3"], p_after), "gx", 3)
+    far_b = hop(after(send["far_b"], p_after), "gx", -6)
+    d2 = hop(after(send["d2"], p_before, p_after), "gx", 2)
 
     slots = jnp.concatenate([x[-rows:, :P_TILES] for x in sources], axis=0).astype(jnp.int32)
     slots = slots - coarse_rows * device + 4
@@ -303,12 +321,15 @@
         return galerkin(weight, chunks, targets, first_row, slots, splits, befores, rows, coarse_rows)
 
     both = add((0, 1), [[(send["d0"], 0)]], None, 10**14)
-    up = hop(after(send["up"], far, both[0]), "gx", 5)
-    far = hop(after(far, both[0]), "gx", -5)
-    both = add((0, 1), [[(d4, 0)]], both)
+    far_a = hop(after(far_a, p_before, p_after), "gx", -5)
+    far_b = hop(after(far_b, both[0]), "gx", -5)
+    end = CAP * ROW
+    d4 = after(d4, both[0])
+    d1 = hop(lax.dynamic_update_slice(send["d1"], d4[end : end + TILE], (end, 0)), "gx", 1)
+    both = add((0, 1), [[(d4, 0)]], both, 10**14)
     both = add((0, 1), [[(d3, 0)]], both)
-    own, on = add((0, 1), [[(d2, 0)]], both)
-    last = [[(d1, 0)], [(far, 0), (up, 0)]]
+    own, on = add((0, 1), [[(d2, 0)], [(far_a, 0)]], both)
+    last = [[(d1, 0)], [(far_b, 0), (d1, end)]]
     (on,) = add((1,), last, [on])
     arrived = beside(on, 1)
     (own,) = add((0,), last, [own])

time: 179 us -> 181 us (1.011)
  waiting for transfers between devices: 75.3 us -> 79.5 us
  Pallas kernels: 28.9 us -> 25.5 us
  local copies, waits for them, and re-layouts: 6.47 us -> 9.54 us
  other arithmetic: 3.47 us -> 1.25 us
  starting transfers between devices: 62.6 us -> 64.6 us
    ppermute x7 -> x8, waiting for transfers between devices: 62.2 us -> 67.2 us  [hop(): lax.ppermute(value, axis, [(i, (i + steps) % count) for i in range(count)])]
    pallas_call x1, Pallas kernels: 5.05 us -> 1.23 us  [split(): pl.pallas_call(functools.partial(split_kernel, rows), out_shape=[wide, wi...]
    unnamed x14 -> x18, local copies, waits for them, and re-layouts: 5.04 us -> 8.06 us
    concatenate x1 -> x0, other arithmetic: 2.26 us -> none  [shards(): p_here = jnp.concatenate([p_tiles.reshape(-1, TILE), p_notes], axis=0)]
    ppermute x7 -> x8, starting transfers between devices: 54.2 us -> 55.8 us  [hop(): lax.ppermute(value, axis, [(i, (i + steps) % count) for i in range(count)])]
  transfers between devices with their start and end apart: 10 -> 11, of which waited for: 4 -> 6; matrix products, arithmetic and copies ran while one was open for 1% -> 1% of each run, Pallas kernels for 14% -> 11%
where the time goes in v2:
time: 181 us
  waiting for transfers between devices  79.5 us (44%)
  starting transfers between devices  64.6 us (36%)
  Pallas kernels  25.5 us (14%)
  local copies, waits for them, and re-layouts  9.54 us (5%)
    ppermute x8, waiting for transfers between devices, hop(): lax.ppermute(value, axis, [(i, (i + steps) % count) for i in range(count)])  67.2 us
    ppermute x8, starting transfers between devices, hop(): lax.ppermute(value, axis, [(i, (i + steps) % count) for i in range(count)])  55.8 us
    pallas_call x6, Pallas kernels, galerkin(): pl.pallas_call(functools.partial(galerkin_kernel, rows, shapes, targets,...  21.8 us
    ppermute x3, waiting for transfers between devices, beside(): return lax.ppermute(value, 'gy', route)  12.3 us
    ppermute x3, starting transfers between devices, beside(): return lax.ppermute(value, 'gy', route)  8.82 us
    unnamed x18, local copies, waits for them, and re-layouts  8.06 us
  transfers between devices with their start and end apart: 11, of which 6 were waited for; matrix products, arithmetic and copies ran while one was open for 1% of the time, Pallas kernels for 11%

profile of v2, /device:TPU:6, one launch (start us, length us, event | category | flops | bytes accessed | tf_op | source)
XLA Modules:
  0.0 180.7 jit_solution(5635134573631881699)
XLA Ops:
  0.0 0.8 copy.22.a_cols
  0.8 0.8 copy.23.p_cols
  1.5 0.0 copy-start
  1.5 1.6 copy-done
  3.1 0.0 copy-start.1
  3.1 1.2 copy-done.1
  4.3 0.0 copy-start.2
  4.3 0.7 copy-done.2
  5.0 2.5 %buckets.1 = (f32[2056,128]{1,0:T(8,128)S(1)}, f32[520,128]{1,0:T(8,128)S(1)}, f32[392,128]{1,0:T(8,128)S(1)}, f32[1160,128]{1,0:T(8,128)}, f32[1032,128]{1,0:T(...) custom-call(s32[8]{0:T(128)S(1)} %copy-done.2, s32[8,4]{1,0:T(8,128)S(1)} %copy.22.a_cols, ...), custom_call_target="tpu_custom_call" | custom-call | tf_op jit(solution)/shard_map/buckets/pallas_call | solution.py:126
  7.5 0.0 copy-start.3
  7.5 0.8 copy-done.3
  8.3 0.0 copy-start.4
  8.3 0.8 copy-done.4
  9.1 0.8 copy-done.5
  9.9 0.7 copy-done.7
  10.5 4.8 %collective-permute-start.1 = (f32[2056,128]{1,0:T(8,128)S(1)}, f32[2056,128]{1,0:T(8,128)S(1)}, u32[]{:S(2)}, u32[]{:S(2)}) collective-permute-start(f32[2056,128]{1,0:T(8,128)S(1)} %get-tuple-element.30.refs_1_), channel_id=1, source_target_pairs={{1,0},{2,1},{3,2},{4,3},{5,4},{6,5},{7,6},{8,7},{9,8},{10,9},{11,1... | collective-permute-start | bytes 3158024 | tf_op jit(solution)/shard_map/ppermute | solution.py:44
  15.4 1.9 %collective-permute-start = (f32[2056,128]{1,0:T(8,128)S(1)}, f32[2056,128]{1,0:T(8,128)S(1)}, u32[]{:S(2)}, u32[]{:S(2)}) collective-permute-start(f32[2056,128]{1,0:T(8,128)S(1)} %get-tuple-element.30.refs_1_), channel_id=1, source_target_pairs={{0,1},{1,2},{2,3},{3,4},{4,5},{5,6},{6,7},{7,8},{8,9},{9,10},{10,1... | collective-permute-start | bytes 3158024 | tf_op jit(solution)/shard_map/ppermute | solution.py:44
  17.3 14.8 %collective-permute-start.7 = (f32[520,128]{1,0:T(8,128)S(1)}, f32[520,128]{1,0:T(8,128)}, u32[]{:S(2)}, u32[]{:S(2)}) collective-permute-start(f32[520,128]{1,0:T(8,128)S(1)} %get-tuple-element.44), channel_id=1, source_target_pairs={{0,320},{32,352},{64,384},{96,416},{128,448},{160,480},{192,0},{22... | collective-permute-start | bytes 798728 | tf_op jit(solution)/shard_map/ppermute | solution.py:38
  32.1 4.3 %collective-permute-start.2 = (f32[1160,128]{1,0:T(8,128)}, f32[1160,128]{1,0:T(8,128)}, u32[]{:S(2)}, u32[]{:S(2)}) collective-permute-start(f32[1160,128]{1,0:T(8,128)} %get-tuple-element.35), channel_id=1, source_target_pairs={{0,128},{32,160},{64,192},{96,224},{128,256},{160,288},{192,320},{... | collective-permute-start | bytes 1781768 | tf_op jit(solution)/shard_map/ppermute | solution.py:38
  36.5 0.0 collective-permute-done.1.refs_2_
  36.5 6.3 %collective-permute-start.4 = (f32[392,128]{1,0:T(8,128)}, f32[392,128]{1,0:T(8,128)}, u32[]{:S(2)}, u32[]{:S(2)}) collective-permute-start(f32[392,128]{1,0:T(8,128)} %copy-done.7), channel_id=1, source_target_pairs={{0,320},{32,352},{64,384},{96,416},{128,448},{160,480},{192,0},{22... | collective-permute-start | bytes 602120 | tf_op jit(solution)/shard_map/ppermute | solution.py:38
  42.8 3.8 %collective-permute-start.9 = (f32[1032,128]{1,0:T(8,128)}, f32[1032,128]{1,0:T(8,128)}, u32[]{:S(2)}, u32[]{:S(2)}) collective-permute-start(f32[1032,128]{1,0:T(8,128)} %copy-done.4), channel_id=1, source_target_pairs={{0,96},{32,128},{64,160},{96,192},{128,224},{160,256},{192,288},{2... | collective-permute-start | bytes 1585160 | tf_op jit(solution)/shard_map/ppermute | solution.py:38
  46.7 26.5 %collective-permute-done.7 = f32[520,128]{1,0:T(8,128)} collective-permute-done((f32[520,128]{1,0:T(8,128)S(1)}, f32[520,128]{1,0:T(8,128)}, u32[]{:S(2)}, u32[]{:S(2)}) %collective-permute-start.7) | collective-permute-done | bytes 266272 | tf_op jit(solution)/shard_map/ppermute | solution.py:38
  73.2 0.0 collective-permute-done.refs_0_
  73.2 1.9 %collective-permute-start.8 = (f32[520,128]{1,0:T(8,128)}, f32[520,128]{1,0:T(8,128)}, u32[]{:S(2)}, u32[]{:S(2)}) collective-permute-start(f32[520,128]{1,0:T(8,128)} %collective-permute-done.7), channel_id=1, source_target_pairs={{0,352},{32,384},{64,416},{96,448},{128,480},{160,0},{192,32},{224... | collective-permute-start | bytes 798728 | tf_op jit(solution)/shard_map/ppermute | solution.py:38
  75.1 5.9 %collective-permute-start.6 = (f32[1032,128]{1,0:T(8,128)}, f32[1032,128]{1,0:T(8,128)}, u32[]{:S(2)}, u32[]{:S(2)}) collective-permute-start(f32[1032,128]{1,0:T(8,128)} %copy-done.3), channel_id=1, source_target_pairs={{0,64},{32,96},{64,128},{96,160},{128,192},{160,224},{192,256},{22... | collective-permute-start | bytes 1585160 | tf_op jit(solution)/shard_map/ppermute | solution.py:38
  81.0 0.0 copy-start.6
  81.0 1.2 split.1
  82.3 0.0 copy-done.6
  82.3 3.4 %galerkin.6 = (f32[20,128,128]{2,1,0:T(8,128)S(1)}, f32[16,128,128]{2,1,0:T(8,128)S(1)}) custom-call(s32[24,2]{1,0:T(8,128)S(1)} %fusion.1.slots, s32[1]{0:T(128)} %bitcast.3.first, bf16[24,128,256]{2,1,0:T(8,128)(2,1)S(1)} %get-tuple-element.31.high, bf16[24,128,256]{2,1,0:T(8,128)(2,1)S(1)} %get-tuple-element.32.low, ...), custom_call_target="tpu_custom_call" | custom-call | flops 100000000376832 | bytes 1 | tf_op jit(solution)/shard_map/galerkin/pallas_call | solution.py:276
  85.7 0.0 collective-permute-done.2.refs_0_
  85.7 1.5 slice_dynamic-update-slice_fusion
  87.2 14.6 %collective-permute-start.3 = (f32[1160,128]{1,0:T(8,128)}, f32[1160,128]{1,0:T(8,128)}, u32[]{:S(2)}, u32[]{:S(2)}) collective-permute-start(f32[1160,128]{1,0:T(8,128)} %slice_dynamic-update-slice_fusion), channel_id=1, source_target_pairs={{0,32},{32,64},{64,96},{96,128},{128,160},{160,192},{192,224},{224... | collective-permute-start | bytes 1781768 | tf_op jit(solution)/shard_map/ppermute | solution.py:38
  101.8 0.0 collective-permute-done.4
  101.8 4.1 %collective-permute-start.5 = (f32[392,128]{1,0:T(8,128)}, f32[392,128]{1,0:T(8,128)}, u32[]{:S(2)}, u32[]{:S(2)}) collective-permute-start(f32[392,128]{1,0:T(8,128)} %collective-permute-done.4), channel_id=1, source_target_pairs={{0,352},{32,384},{64,416},{96,448},{128,480},{160,0},{192,32},{224... | collective-permute-start | bytes 602120 | tf_op jit(solution)/shard_map/ppermute | solution.py:38
  105.9 4.4 %galerkin.7 = (f32[20,128,128]{2,1,0:T(8,128)S(1)}, f32[16,128,128]{2,1,0:T(8,128)S(1)}) custom-call(s32[24,2]{1,0:T(8,128)S(1)} %fusion.1.slots, s32[1]{0:T(128)} %bitcast.3.first, bf16[24,128,256]{2,1,0:T(8,128)(2,1)S(1)} %get-tuple-element.31.high, bf16[24,128,256]{2,1,0:T(8,128)(2,1)S(1)} %get-tuple-element.32.low, ...), custom_call_target="tpu_custom_call", output_to_operand_aliasing={{0}: (6, {}), {1}: (7, {})} | custom-call | flops 100000000376832 | bytes 1 | tf_op jit(solution)/shard_map/galerkin/pallas_call | solution.py:276
  110.4 14.9 %collective-permute-done.9.refs_0_ = f32[1032,128]{1,0:T(8,128)} collective-permute-done((f32[1032,128]{1,0:T(8,128)}, f32[1032,128]{1,0:T(8,128)}, u32[]{:S(2)}, u32[]{:S(2)}) %collective-permute-start.9) | collective-permute-done | bytes 528416 | tf_op jit(solution)/shard_map/ppermute | solution.py:38
  125.2 1.5 galerkin.8
  126.8 1.8 collective-permute-done.8.refs_1_
  128.5 18.1 %collective-permute-done.6.refs_0_ = f32[1032,128]{1,0:T(8,128)} collective-permute-done((f32[1032,128]{1,0:T(8,128)}, f32[1032,128]{1,0:T(8,128)}, u32[]{:S(2)}, u32[]{:S(2)}) %collective-permute-start.6) | collective-permute-done | bytes 528416 | tf_op jit(solution)/shard_map/ppermute | solution.py:38
  146.7 4.7 %galerkin.9 = (f32[20,128,128]{2,1,0:T(8,128)S(1)}, f32[16,128,128]{2,1,0:T(8,128)S(1)}) custom-call(s32[24,2]{1,0:T(8,128)S(1)} %fusion.1.slots, s32[1]{0:T(128)} %bitcast.3.first, bf16[24,128,256]{2,1,0:T(8,128)(2,1)S(1)} %get-tuple-element.31.high, bf16[24,128,256]{2,1,0:T(8,128)(2,1)S(1)} %get-tuple-element.32.low, ...), custom_call_target="tpu_custom_call", output_to_operand_aliasing={{0}: (7, {}), {1}: (8, {})} | custom-call | flops 1 | bytes 1 | tf_op jit(solution)/shard_map/galerkin/pallas_call | solution.py:276
  151.4 0.0 collective-permute-done.5.refs_1_
  151.4 6.0 %collective-permute-done.3.refs_0_.refs_2_ = f32[1160,128]{1,0:T(8,128)} collective-permute-done((f32[1160,128]{1,0:T(8,128)}, f32[1160,128]{1,0:T(8,128)}, u32[]{:S(2)}, u32[]{:S(2)}) %collective-permute-start.3) | collective-permute-done | bytes 593952 | tf_op jit(solution)/shard_map/ppermute | solution.py:38
  157.3 3.9 %galerkin.11 = f32[16,128,128]{2,1,0:T(8,128)S(1)} custom-call(s32[24,2]{1,0:T(8,128)S(1)} %fusion.1.slots, s32[1]{0:T(128)} %bitcast.3.first, bf16[24,128,256]{2,1,0:T(8,128)(2,1)S(1)} %get-tuple-element.31.high, bf16[24,128,256]{2,1,0:T(8,128)(2,1)S(1)} %get-tuple-element.32.low, ...), custom_call_target="tpu_custom_call", output_to_operand_aliasing={{}: (8, {})} | custom-call | flops 1 | bytes 1 | tf_op jit(solution)/shard_map/galerkin/pallas_call | solution.py:276
  161.2 2.1 %collective-permute-start.10 = (f32[16,128,128]{2,1,0:T(8,128)S(1)}, f32[16,128,128]{2,1,0:T(8,128)S(1)}, u32[]{:S(2)}, u32[]{:S(2)}) collective-permute-start(f32[16,128,128]{2,1,0:T(8,128)S(1)} %galerkin.11), channel_id=1, source_target_pairs={{0,1},{1,2},{2,3},{3,4},{4,5},{5,6},{6,7},{7,8},{8,9},{9,10},{10,1... | collective-permute-start | bytes 3145736 | tf_op jit(solution)/shard_map/ppermute | solution.py:44
  163.3 3.9 %galerkin.10 = f32[20,128,128]{2,1,0:T(8,128)S(1)} custom-call(s32[24,2]{1,0:T(8,128)S(1)} %fusion.1.slots, s32[1]{0:T(128)} %bitcast.3.first, bf16[24,128,256]{2,1,0:T(8,128)(2,1)S(1)} %get-tuple-element.31.high, bf16[24,128,256]{2,1,0:T(8,128)(2,1)S(1)} %get-tuple-element.32.low, ...), custom_call_target="tpu_custom_call", output_to_operand_aliasing={{}: (8, {})} | custom-call | flops 1 | bytes 1 | tf_op jit(solution)/shard_map/galerkin/pallas_call | solution.py:276
  167.2 12.3 %collective-permute-done.10 = f32[16,128,128]{2,1,0:T(8,128)S(1)} collective-permute-done((f32[16,128,128]{2,1,0:T(8,128)S(1)}, f32[16,128,128]{2,1,0:T(8,128)S(1)}, u32[]{:S(2)}, u32[]{:S(2)}) %collective-permute-start.10) | collective-permute-done | bytes 1048608 | tf_op jit(solution)/shard_map/ppermute | solution.py:44
  179.4 1.2 pad_add_fusion
  (6 shorter events, 0.0 us)
Async XLA Ops:
  1.5 1.6 copy-start
  3.1 1.2 copy-start.1
  4.3 0.7 copy-start.2
  7.5 0.8 copy-start.3
  8.3 0.8 copy-start.4
  9.1 0.8 copy-start.5
  9.9 0.7 copy-start.7
  10.5 25.9 %collective-permute-start.1 = (f32[2056,128]{1,0:T(8,128)S(1)}, f32[2056,128]{1,0:T(8,128)S(1)}, u32[]{:S(2)}, u32[]{:S(2)}) collective-permute-start(f32[2056,128]{1,0:T(8,128)S(1)} %get-tuple-element.30.refs_1_), channel_id=1, source_target_pairs={{1,0},{2,1},{3,2},{4,3},{5,4},{6,5},{7,6},{8,7},{9,8},{10,9},{11,1... | collective-permute-start | bytes 3158024 | tf_op jit(solution)/shard_map/ppermute | solution.py:44
  15.4 57.8 %collective-permute-start = (f32[2056,128]{1,0:T(8,128)S(1)}, f32[2056,128]{1,0:T(8,128)S(1)}, u32[]{:S(2)}, u32[]{:S(2)}) collective-permute-start(f32[2056,128]{1,0:T(8,128)S(1)} %get-tuple-element.30.refs_1_), channel_id=1, source_target_pairs={{0,1},{1,2},{2,3},{3,4},{4,5},{5,6},{6,7},{7,8},{8,9},{9,10},{10,1... | collective-permute-start | bytes 3158024 | tf_op jit(solution)/shard_map/ppermute | solution.py:44
  17.3 55.9 %collective-permute-start.7 = (f32[520,128]{1,0:T(8,128)S(1)}, f32[520,128]{1,0:T(8,128)}, u32[]{:S(2)}, u32[]{:S(2)}) collective-permute-start(f32[520,128]{1,0:T(8,128)S(1)} %get-tuple-element.44), channel_id=1, source_target_pairs={{0,320},{32,352},{64,384},{96,416},{128,448},{160,480},{192,0},{22... | collective-permute-start | bytes 798728 | tf_op jit(solution)/shard_map/ppermute | solution.py:38
  32.1 53.6 %collective-permute-start.2 = (f32[1160,128]{1,0:T(8,128)}, f32[1160,128]{1,0:T(8,128)}, u32[]{:S(2)}, u32[]{:S(2)}) collective-permute-start(f32[1160,128]{1,0:T(8,128)} %get-tuple-element.35), channel_id=1, source_target_pairs={{0,128},{32,160},{64,192},{96,224},{128,256},{160,288},{192,320},{... | collective-permute-start | bytes 1781768 | tf_op jit(solution)/shard_map/ppermute | solution.py:38
  36.5 65.4 %collective-permute-start.4 = (f32[392,128]{1,0:T(8,128)}, f32[392,128]{1,0:T(8,128)}, u32[]{:S(2)}, u32[]{:S(2)}) collective-permute-start(f32[392,128]{1,0:T(8,128)} %copy-done.7), channel_id=1, source_target_pairs={{0,320},{32,352},{64,384},{96,416},{128,448},{160,480},{192,0},{22... | collective-permute-start | bytes 602120 | tf_op jit(solution)/shard_map/ppermute | solution.py:38
  42.8 82.4 %collective-permute-start.9 = (f32[1032,128]{1,0:T(8,128)}, f32[1032,128]{1,0:T(8,128)}, u32[]{:S(2)}, u32[]{:S(2)}) collective-permute-start(f32[1032,128]{1,0:T(8,128)} %copy-done.4), channel_id=1, source_target_pairs={{0,96},{32,128},{64,160},{96,192},{128,224},{160,256},{192,288},{2... | collective-permute-start | bytes 1585160 | tf_op jit(solution)/shard_map/ppermute | solution.py:38
  73.2 55.4 %collective-permute-start.8 = (f32[520,128]{1,0:T(8,128)}, f32[520,128]{1,0:T(8,128)}, u32[]{:S(2)}, u32[]{:S(2)}) collective-permute-start(f32[520,128]{1,0:T(8,128)} %collective-permute-done.7), channel_id=1, source_target_pairs={{0,352},{32,384},{64,416},{96,448},{128,480},{160,0},{192,32},{224... | collective-permute-start | bytes 798728 | tf_op jit(solution)/shard_map/ppermute | solution.py:38
  75.1 71.6 %collective-permute-start.6 = (f32[1032,128]{1,0:T(8,128)}, f32[1032,128]{1,0:T(8,128)}, u32[]{:S(2)}, u32[]{:S(2)}) collective-permute-start(f32[1032,128]{1,0:T(8,128)} %copy-done.3), channel_id=1, source_target_pairs={{0,64},{32,96},{64,128},{96,160},{128,192},{160,224},{192,256},{22... | collective-permute-start | bytes 1585160 | tf_op jit(solution)/shard_map/ppermute | solution.py:38
  81.0 1.3 copy-start.6
  87.2 70.1 %collective-permute-start.3 = (f32[1160,128]{1,0:T(8,128)}, f32[1160,128]{1,0:T(8,128)}, u32[]{:S(2)}, u32[]{:S(2)}) collective-permute-start(f32[1160,128]{1,0:T(8,128)} %slice_dynamic-update-slice_fusion), channel_id=1, source_target_pairs={{0,32},{32,64},{64,96},{96,128},{128,160},{160,192},{192,224},{224... | collective-permute-start | bytes 1781768 | tf_op jit(solution)/shard_map/ppermute | solution.py:38
  101.8 49.5 %collective-permute-start.5 = (f32[392,128]{1,0:T(8,128)}, f32[392,128]{1,0:T(8,128)}, u32[]{:S(2)}, u32[]{:S(2)}) collective-permute-start(f32[392,128]{1,0:T(8,128)} %collective-permute-done.4), channel_id=1, source_target_pairs={{0,352},{32,384},{64,416},{96,448},{128,480},{160,0},{192,32},{224... | collective-permute-start | bytes 602120 | tf_op jit(solution)/shard_map/ppermute | solution.py:38
  161.2 18.2 %collective-permute-start.10 = (f32[16,128,128]{2,1,0:T(8,128)S(1)}, f32[16,128,128]{2,1,0:T(8,128)S(1)}, u32[]{:S(2)}, u32[]{:S(2)}) collective-permute-start(f32[16,128,128]{2,1,0:T(8,128)S(1)} %galerkin.11), channel_id=1, source_target_pairs={{0,1},{1,2},{2,3},{3,4},{4,5},{5,6},{6,7},{7,8},{8,9},{9,10},{10,1... | collective-permute-start | bytes 3145736 | tf_op jit(solution)/shard_map/ppermute | solution.py:44

commit v3 on v2

--- a/solution.py
+++ b/solution.py
@@ -19,11 +19,11 @@
 
 BUFFERS = {
     "far_a": (((10, 0, ROW),), True),
-    "far_b": (((11, 0, ROW - TILE),), True),
-    "d4": (((8, 0, ROW), (9, 0, ROW), (11, ROW - TILE, TILE)), True),
+    "far_b": (((11, 0, ROW),), True),
+    "d4": (((8, 0, ROW), (9, 0, ROW)), True),
     "d3": (((6, 0, ROW), (7, 0, ROW)), True),
     "d2": (((4, 0, ROW), (5, 0, ROW)), True),
-    "d1": (((2, 0, ROW), (3, 0, ROW), (None, 0, TILE)), True),
+    "d1": (((2, 0, ROW), (3, 0, ROW)), True),
     "d0": (((0, 0, ROW), (1, 0, ROW)), True),
 }
 
@@ -66,12 +66,12 @@
         if not noted:
             continue
         note = jnp.zeros((META, TILE), jnp.int32)
-        for r, (s, _, _) in enumerate(pieces[:CAP]):
+        for r, (s, _, _) in enumerate(pieces):
             o = order[s]
             here = jnp.maximum(o, 0)
             place = jnp.where(o >= 0, lax.rem(new_row[here], rows) + 1, 0)
             for k in range(A_TILES):
-                note = jnp.where((line == r) & (lane == k), a_cols[here, k], note)
+                note = jnp.where((line == r) & (lane == k), a_cols[k, here], note)
             note = jnp.where((line == r) & (lane == A_TILES), place, note)
         notes[b] = note.astype(jnp.float32)
         size = sum(n for _, _, n in pieces)
@@ -81,7 +81,7 @@
     note = jnp.zeros((META, TILE), jnp.int32)
     for i in range(rows):
         for q in range(P_TILES):
-            note = jnp.where((line == i) & (lane == q), p_cols[i, q], note)
+            note = jnp.where((line == i) & (lane == q), p_cols[q, i], note)
     held_p[p_size:, :] = note.astype(jnp.float32)
     p_load.wait()
     p_copy = pltpu.make_async_copy(held_p, p_out, p_sem)
@@ -94,8 +94,6 @@
         for out, (pieces, _) in zip(outs, layout):
             to = 0
             for s, frm, size in pieces:
-                if s is None:
-                    continue
                 o = order[s]
                 here = jnp.maximum(o, 0)
 
@@ -138,9 +136,9 @@
             pltpu.SemaphoreType.DMA((len(lengths),)),
             pltpu.SemaphoreType.DMA,
         ],
-        compiler_params=pltpu.CompilerParams(vmem_limit_bytes=5 * 2**20),
+        compiler_params=pltpu.CompilerParams(vmem_limit_bytes=60 * 2**20),
         name="buckets",
-    )(new_row, a_cols, p_cols, my_x, a_tiles.reshape(rows, ROW, TILE), p_tiles.reshape(p_lines, TILE))
+    )(new_row, a_cols.T, p_cols.T, my_x, a_tiles.reshape(rows, ROW, TILE), p_tiles.reshape(p_lines, TILE))
     return p_here, dict(zip(BUFFERS, outs))
 
 
@@ -323,13 +321,12 @@
     both = add((0, 1), [[(send["d0"], 0)]], None, 10**14)
     far_a = hop(after(far_a, p_before, p_after), "gx", -5)
     far_b = hop(after(far_b, both[0]), "gx", -5)
-    end = CAP * ROW
     d4 = after(d4, both[0])
-    d1 = hop(lax.dynamic_update_slice(send["d1"], d4[end : end + TILE], (end, 0)), "gx", 1)
+    d1 = hop(after(send["d1"], d4), "gx", 1)
     both = add((0, 1), [[(d4, 0)]], both, 10**14)
     both = add((0, 1), [[(d3, 0)]], both)
     own, on = add((0, 1), [[(d2, 0)], [(far_a, 0)]], both)
-    last = [[(d1, 0)], [(far_b, 0), (d1, end)]]
+    last = [[(d1, 0)], [(far_b, 0)]]
     (on,) = add((1,), last, [on])
     arrived = beside(on, 1)
     (own,) = add((0,), last, [own])

time: 181 us -> 176 us (0.972)
  local copies, waits for them, and re-layouts: 9.54 us -> 1.92 us
  waiting for transfers between devices: 79.5 us -> 82 us
  starting transfers between devices: 64.6 us -> 62.5 us
    unnamed x18 -> x4, local copies, waits for them, and re-layouts: 8.06 us -> 1.23 us
    ppermute x8, waiting for transfers between devices: 67.2 us -> 70.2 us  [hop(): lax.ppermute(value, axis, [(i, (i + steps) % count) for i in range(count)])]
    pallas_call x1, Pallas kernels: 2.47 us -> 4.5 us  [buckets(): pl.pallas_call(functools.partial(bucket_kernel, rows, gx, rows * gy, layo...]
  transfers between devices with their start and end apart: 11 -> 11, of which waited for: 6 -> 7; matrix products, arithmetic and copies ran while one was open for 1% -> 0% of each run, Pallas kernels for 11% -> 10%
where the time goes in v3:
time: 176 us; the launch traced here: 175 us
  waiting for transfers between devices  82 us (47%)
  starting transfers between devices  62.5 us (36%)
  Pallas kernels  27 us (15%)
  local copies, waits for them, and re-layouts  1.92 us (1%)
    ppermute x8, waiting for transfers between devices, hop(): lax.ppermute(value, axis, [(i, (i + steps) % count) for i in range(count)])  70.2 us
    ppermute x8, starting transfers between devices, hop(): lax.ppermute(value, axis, [(i, (i + steps) % count) for i in range(count)])  54 us
    pallas_call x6, Pallas kernels, galerkin(): pl.pallas_call(functools.partial(galerkin_kernel, rows, shapes, targets,...  21.2 us
    ppermute x3, waiting for transfers between devices, beside(): return lax.ppermute(value, 'gy', route)  11.8 us
    ppermute x3, starting transfers between devices, beside(): return lax.ppermute(value, 'gy', route)  8.47 us
    pallas_call x1, Pallas kernels, buckets(): pl.pallas_call(functools.partial(bucket_kernel, rows, gx, rows * gy, layo...  4.5 us
  transfers between devices with their start and end apart: 11, of which 7 were waited for; matrix products, arithmetic and copies ran while one was open for 0% of the time, Pallas kernels for 10%

profile of v3, /device:TPU:6, one launch (start us, length us, event | category | flops | bytes accessed | tf_op | source)
XLA Modules:
  0.0 174.8 jit_solution(5033488718782730675)
XLA Ops:
  0.0 4.5 %buckets.1 = (f32[2056,128]{1,0:T(8,128)}, f32[520,128]{1,0:T(8,128)}, f32[520,128]{1,0:T(8,128)}, f32[1032,128]{1,0:T(8,128)}, f32[1032,128]{1,0:T(8,128)}, /*i...) custom-call(s32[8]{0:T(128)} %new_row.1, s32[4,8]{1,0:T(4,128)} %bitcast.12, s32[2,8]{1,0:T(2,128)} %bitcast.13, ...), custom_call_target="tpu_custom_call" | custom-call | tf_op jit(solution)/shard_map/buckets/pallas_call | solution.py:124
  4.5 4.6 %collective-permute-start.1 = (f32[2056,128]{1,0:T(8,128)}, f32[2056,128]{1,0:T(8,128)S(1)}, u32[]{:S(2)}, u32[]{:S(2)}) collective-permute-start(f32[2056,128]{1,0:T(8,128)} %get-tuple-element.31.refs_1_), channel_id=1, source_target_pairs={{1,0},{2,1},{3,2},{4,3},{5,4},{6,5},{7,6},{8,7},{9,8},{10,9},{11,1... | collective-permute-start | bytes 3158024 | tf_op jit(solution)/shard_map/ppermute | solution.py:44
  9.1 1.9 %collective-permute-start = (f32[2056,128]{1,0:T(8,128)}, f32[2056,128]{1,0:T(8,128)S(1)}, u32[]{:S(2)}, u32[]{:S(2)}) collective-permute-start(f32[2056,128]{1,0:T(8,128)} %get-tuple-element.31.refs_1_), channel_id=1, source_target_pairs={{0,1},{1,2},{2,3},{3,4},{4,5},{5,6},{6,7},{7,8},{8,9},{9,10},{10,1... | collective-permute-start | bytes 3158024 | tf_op jit(solution)/shard_map/ppermute | solution.py:44
  11.1 14.8 %collective-permute-start.7 = (f32[520,128]{1,0:T(8,128)}, f32[520,128]{1,0:T(8,128)}, u32[]{:S(2)}, u32[]{:S(2)}) collective-permute-start(f32[520,128]{1,0:T(8,128)} %get-tuple-element.46), channel_id=1, source_target_pairs={{0,320},{32,352},{64,384},{96,416},{128,448},{160,480},{192,0},{22... | collective-permute-start | bytes 798728 | tf_op jit(solution)/shard_map/ppermute | solution.py:38
  25.9 4.3 %collective-permute-start.2 = (f32[1032,128]{1,0:T(8,128)}, f32[1032,128]{1,0:T(8,128)}, u32[]{:S(2)}, u32[]{:S(2)}) collective-permute-start(f32[1032,128]{1,0:T(8,128)} %get-tuple-element.36), channel_id=1, source_target_pairs={{0,128},{32,160},{64,192},{96,224},{128,256},{160,288},{192,320},{... | collective-permute-start | bytes 1585160 | tf_op jit(solution)/shard_map/ppermute | solution.py:38
  30.2 0.7 slice.10
  30.9 0.0 collective-permute-done.1.refs_2_
  30.9 6.3 %collective-permute-start.4 = (f32[520,128]{1,0:T(8,128)}, f32[520,128]{1,0:T(8,128)}, u32[]{:S(2)}, u32[]{:S(2)}) collective-permute-start(f32[520,128]{1,0:T(8,128)} %get-tuple-element.42), channel_id=1, source_target_pairs={{0,320},{32,352},{64,384},{96,416},{128,448},{160,480},{192,0},{22... | collective-permute-start | bytes 798728 | tf_op jit(solution)/shard_map/ppermute | solution.py:38
  37.3 3.8 %collective-permute-start.9 = (f32[1032,128]{1,0:T(8,128)}, f32[1032,128]{1,0:T(8,128)}, u32[]{:S(2)}, u32[]{:S(2)}) collective-permute-start(f32[1032,128]{1,0:T(8,128)} %get-tuple-element.49), channel_id=1, source_target_pairs={{0,96},{32,128},{64,160},{96,192},{128,224},{160,256},{192,288},{2... | collective-permute-start | bytes 1585160 | tf_op jit(solution)/shard_map/ppermute | solution.py:38
  41.1 32.6 %collective-permute-done.7 = f32[520,128]{1,0:T(8,128)} collective-permute-done((f32[520,128]{1,0:T(8,128)}, f32[520,128]{1,0:T(8,128)}, u32[]{:S(2)}, u32[]{:S(2)}) %collective-permute-start.7) | collective-permute-done | bytes 266272 | tf_op jit(solution)/shard_map/ppermute | solution.py:38
  73.7 0.0 collective-permute-done.refs_0_
  73.7 1.9 %collective-permute-start.8 = (f32[520,128]{1,0:T(8,128)}, f32[520,128]{1,0:T(8,128)}, u32[]{:S(2)}, u32[]{:S(2)}) collective-permute-start(f32[520,128]{1,0:T(8,128)} %collective-permute-done.7), channel_id=1, source_target_pairs={{0,352},{32,384},{64,416},{96,448},{128,480},{160,0},{192,32},{224... | collective-permute-start | bytes 798728 | tf_op jit(solution)/shard_map/ppermute | solution.py:38
  75.6 10.0 %collective-permute-start.6 = (f32[1032,128]{1,0:T(8,128)}, f32[1032,128]{1,0:T(8,128)}, u32[]{:S(2)}, u32[]{:S(2)}) collective-permute-start(f32[1032,128]{1,0:T(8,128)} %get-tuple-element.45), channel_id=1, source_target_pairs={{0,64},{32,96},{64,128},{96,160},{128,192},{160,224},{192,256},{22... | collective-permute-start | bytes 1585160 | tf_op jit(solution)/shard_map/ppermute | solution.py:38
  85.6 0.0 copy-start
  85.7 1.2 copy-done
  86.9 0.0 copy-start.1
  86.9 1.2 split.1
  88.1 0.0 copy-done.1
  88.1 3.4 %galerkin.6 = (f32[20,128,128]{2,1,0:T(8,128)S(1)}, f32[16,128,128]{2,1,0:T(8,128)S(1)}) custom-call(s32[24,2]{1,0:T(8,128)S(1)} %fusion.1.slots, s32[1]{0:T(128)} %bitcast.5.first, bf16[24,128,256]{2,1,0:T(8,128)(2,1)S(1)} %get-tuple-element.32.high, bf16[24,128,256]{2,1,0:T(8,128)(2,1)S(1)} %get-tuple-element.33.low, ...), custom_call_target="tpu_custom_call" | custom-call | flops 100000000376832 | bytes 1 | tf_op jit(solution)/shard_map/galerkin/pallas_call | solution.py:274
  91.6 0.0 collective-permute-done.2.refs_0_
  91.6 9.7 %collective-permute-start.3 = (f32[1032,128]{1,0:T(8,128)}, f32[1032,128]{1,0:T(8,128)}, u32[]{:S(2)}, u32[]{:S(2)}) collective-permute-start(f32[1032,128]{1,0:T(8,128)} %get-tuple-element.40), channel_id=1, source_target_pairs={{0,32},{32,64},{64,96},{96,128},{128,160},{160,192},{192,224},{224... | collective-permute-start | bytes 1585160 | tf_op jit(solution)/shard_map/ppermute | solution.py:38
  101.3 0.0 collective-permute-done.4
  101.3 3.1 %collective-permute-start.5 = (f32[520,128]{1,0:T(8,128)}, f32[520,128]{1,0:T(8,128)}, u32[]{:S(2)}, u32[]{:S(2)}) collective-permute-start(f32[520,128]{1,0:T(8,128)} %collective-permute-done.4), channel_id=1, source_target_pairs={{0,352},{32,384},{64,416},{96,448},{128,480},{160,0},{192,32},{224... | collective-permute-start | bytes 798728 | tf_op jit(solution)/shard_map/ppermute | solution.py:38
  104.4 1.5 galerkin.7
  106.0 7.3 %collective-permute-done.9.refs_0_ = f32[1032,128]{1,0:T(8,128)} collective-permute-done((f32[1032,128]{1,0:T(8,128)}, f32[1032,128]{1,0:T(8,128)}, u32[]{:S(2)}, u32[]{:S(2)}) %collective-permute-start.9) | collective-permute-done | bytes 528416 | tf_op jit(solution)/shard_map/ppermute | solution.py:38
  113.3 1.5 galerkin.8
  114.8 16.8 %collective-permute-done.8.refs_1_ = f32[520,128]{1,0:T(8,128)} collective-permute-done((f32[520,128]{1,0:T(8,128)}, f32[520,128]{1,0:T(8,128)}, u32[]{:S(2)}, u32[]{:S(2)}) %collective-permute-start.8) | collective-permute-done | bytes 266272 | tf_op jit(solution)/shard_map/ppermute | solution.py:38
  131.6 3.3 %collective-permute-done.6.refs_0_ = f32[1032,128]{1,0:T(8,128)} collective-permute-done((f32[1032,128]{1,0:T(8,128)}, f32[1032,128]{1,0:T(8,128)}, u32[]{:S(2)}, u32[]{:S(2)}) %collective-permute-start.6) | collective-permute-done | bytes 528416 | tf_op jit(solution)/shard_map/ppermute | solution.py:38
  134.9 5.7 %galerkin.9 = (f32[20,128,128]{2,1,0:T(8,128)S(1)}, f32[16,128,128]{2,1,0:T(8,128)S(1)}) custom-call(s32[24,2]{1,0:T(8,128)S(1)} %fusion.1.slots, s32[1]{0:T(128)} %bitcast.5.first, bf16[24,128,256]{2,1,0:T(8,128)(2,1)S(1)} %get-tuple-element.32.high, bf16[24,128,256]{2,1,0:T(8,128)(2,1)S(1)} %get-tuple-element.33.low, ...), custom_call_target="tpu_custom_call", output_to_operand_aliasing={{0}: (7, {}), {1}: (8, {})} | custom-call | flops 1 | bytes 1 | tf_op jit(solution)/shard_map/galerkin/pallas_call | solution.py:274
  140.6 3.6 %collective-permute-done.3.refs_0_ = f32[1032,128]{1,0:T(8,128)} collective-permute-done((f32[1032,128]{1,0:T(8,128)}, f32[1032,128]{1,0:T(8,128)}, u32[]{:S(2)}, u32[]{:S(2)}) %collective-permute-start.3) | collective-permute-done | bytes 528416 | tf_op jit(solution)/shard_map/ppermute | solution.py:38
  144.1 6.7 %collective-permute-done.5.refs_1_ = f32[520,128]{1,0:T(8,128)} collective-permute-done((f32[520,128]{1,0:T(8,128)}, f32[520,128]{1,0:T(8,128)}, u32[]{:S(2)}, u32[]{:S(2)}) %collective-permute-start.5) | collective-permute-done | bytes 266272 | tf_op jit(solution)/shard_map/ppermute | solution.py:38
  150.8 4.5 %galerkin.11 = f32[16,128,128]{2,1,0:T(8,128)S(1)} custom-call(s32[24,2]{1,0:T(8,128)S(1)} %fusion.1.slots, s32[1]{0:T(128)} %bitcast.5.first, bf16[24,128,256]{2,1,0:T(8,128)(2,1)S(1)} %get-tuple-element.32.high, bf16[24,128,256]{2,1,0:T(8,128)(2,1)S(1)} %get-tuple-element.33.low, ...), custom_call_target="tpu_custom_call", output_to_operand_aliasing={{}: (7, {})} | custom-call | flops 1 | bytes 1 | tf_op jit(solution)/shard_map/galerkin/pallas_call | solution.py:274
  155.3 1.9 %collective-permute-start.10 = (f32[16,128,128]{2,1,0:T(8,128)S(1)}, f32[16,128,128]{2,1,0:T(8,128)S(1)}, u32[]{:S(2)}, u32[]{:S(2)}) collective-permute-start(f32[16,128,128]{2,1,0:T(8,128)S(1)} %galerkin.11), channel_id=1, source_target_pairs={{0,1},{1,2},{2,3},{3,4},{4,5},{5,6},{6,7},{7,8},{8,9},{9,10},{10,1... | collective-permute-start | bytes 3145736 | tf_op jit(solution)/shard_map/ppermute | solution.py:44
  157.3 4.5 %galerkin.10 = f32[20,128,128]{2,1,0:T(8,128)S(1)} custom-call(s32[24,2]{1,0:T(8,128)S(1)} %fusion.1.slots, s32[1]{0:T(128)} %bitcast.5.first, bf16[24,128,256]{2,1,0:T(8,128)(2,1)S(1)} %get-tuple-element.32.high, bf16[24,128,256]{2,1,0:T(8,128)(2,1)S(1)} %get-tuple-element.33.low, ...), custom_call_target="tpu_custom_call", output_to_operand_aliasing={{}: (7, {})} | custom-call | flops 1 | bytes 1 | tf_op jit(solution)/shard_map/galerkin/pallas_call | solution.py:274
  161.8 11.8 %collective-permute-done.10 = f32[16,128,128]{2,1,0:T(8,128)S(1)} collective-permute-done((f32[16,128,128]{2,1,0:T(8,128)S(1)}, f32[16,128,128]{2,1,0:T(8,128)S(1)}, u32[]{:S(2)}, u32[]{:S(2)}) %collective-permute-start.10) | collective-permute-done | bytes 1048608 | tf_op jit(solution)/shard_map/ppermute | solution.py:44
  173.6 1.2 pad_add_fusion
  (3 shorter events, 0.0 us)
Async XLA Ops:
  4.5 26.4 %collective-permute-start.1 = (f32[2056,128]{1,0:T(8,128)}, f32[2056,128]{1,0:T(8,128)S(1)}, u32[]{:S(2)}, u32[]{:S(2)}) collective-permute-start(f32[2056,128]{1,0:T(8,128)} %get-tuple-element.31.refs_1_), channel_id=1, source_target_pairs={{1,0},{2,1},{3,2},{4,3},{5,4},{6,5},{7,6},{8,7},{9,8},{10,9},{11,1... | collective-permute-start | bytes 3158024 | tf_op jit(solution)/shard_map/ppermute | solution.py:44
  9.1 64.6 %collective-permute-start = (f32[2056,128]{1,0:T(8,128)}, f32[2056,128]{1,0:T(8,128)S(1)}, u32[]{:S(2)}, u32[]{:S(2)}) collective-permute-start(f32[2056,128]{1,0:T(8,128)} %get-tuple-element.31.refs_1_), channel_id=1, source_target_pairs={{0,1},{1,2},{2,3},{3,4},{4,5},{5,6},{6,7},{7,8},{8,9},{9,10},{10,1... | collective-permute-start | bytes 3158024 | tf_op jit(solution)/shard_map/ppermute | solution.py:44
  11.1 62.6 %collective-permute-start.7 = (f32[520,128]{1,0:T(8,128)}, f32[520,128]{1,0:T(8,128)}, u32[]{:S(2)}, u32[]{:S(2)}) collective-permute-start(f32[520,128]{1,0:T(8,128)} %get-tuple-element.46), channel_id=1, source_target_pairs={{0,320},{32,352},{64,384},{96,416},{128,448},{160,480},{192,0},{22... | collective-permute-start | bytes 798728 | tf_op jit(solution)/shard_map/ppermute | solution.py:38
  25.9 65.6 %collective-permute-start.2 = (f32[1032,128]{1,0:T(8,128)}, f32[1032,128]{1,0:T(8,128)}, u32[]{:S(2)}, u32[]{:S(2)}) collective-permute-start(f32[1032,128]{1,0:T(8,128)} %get-tuple-element.36), channel_id=1, source_target_pairs={{0,128},{32,160},{64,192},{96,224},{128,256},{160,288},{192,320},{... | collective-permute-start | bytes 1585160 | tf_op jit(solution)/shard_map/ppermute | solution.py:38
  30.9 70.4 %collective-permute-start.4 = (f32[520,128]{1,0:T(8,128)}, f32[520,128]{1,0:T(8,128)}, u32[]{:S(2)}, u32[]{:S(2)}) collective-permute-start(f32[520,128]{1,0:T(8,128)} %get-tuple-element.42), channel_id=1, source_target_pairs={{0,320},{32,352},{64,384},{96,416},{128,448},{160,480},{192,0},{22... | collective-permute-start | bytes 798728 | tf_op jit(solution)/shard_map/ppermute | solution.py:38
  37.3 76.0 %collective-permute-start.9 = (f32[1032,128]{1,0:T(8,128)}, f32[1032,128]{1,0:T(8,128)}, u32[]{:S(2)}, u32[]{:S(2)}) collective-permute-start(f32[1032,128]{1,0:T(8,128)} %get-tuple-element.49), channel_id=1, source_target_pairs={{0,96},{32,128},{64,160},{96,192},{128,224},{160,256},{192,288},{2... | collective-permute-start | bytes 1585160 | tf_op jit(solution)/shard_map/ppermute | solution.py:38
  73.7 57.9 %collective-permute-start.8 = (f32[520,128]{1,0:T(8,128)}, f32[520,128]{1,0:T(8,128)}, u32[]{:S(2)}, u32[]{:S(2)}) collective-permute-start(f32[520,128]{1,0:T(8,128)} %collective-permute-done.7), channel_id=1, source_target_pairs={{0,352},{32,384},{64,416},{96,448},{128,480},{160,0},{192,32},{224... | collective-permute-start | bytes 798728 | tf_op jit(solution)/shard_map/ppermute | solution.py:38
  75.6 59.2 %collective-permute-start.6 = (f32[1032,128]{1,0:T(8,128)}, f32[1032,128]{1,0:T(8,128)}, u32[]{:S(2)}, u32[]{:S(2)}) collective-permute-start(f32[1032,128]{1,0:T(8,128)} %get-tuple-element.45), channel_id=1, source_target_pairs={{0,64},{32,96},{64,128},{96,160},{128,192},{160,224},{192,256},{22... | collective-permute-start | bytes 1585160 | tf_op jit(solution)/shard_map/ppermute | solution.py:38
  85.6 1.2 copy-start
  86.9 1.2 copy-start.1
  91.6 52.5 %collective-permute-start.3 = (f32[1032,128]{1,0:T(8,128)}, f32[1032,128]{1,0:T(8,128)}, u32[]{:S(2)}, u32[]{:S(2)}) collective-permute-start(f32[1032,128]{1,0:T(8,128)} %get-tuple-element.40), channel_id=1, source_target_pairs={{0,32},{32,64},{64,96},{96,128},{128,160},{160,192},{192,224},{224... | collective-permute-start | bytes 1585160 | tf_op jit(solution)/shard_map/ppermute | solution.py:38
  101.3 49.5 %collective-permute-start.5 = (f32[520,128]{1,0:T(8,128)}, f32[520,128]{1,0:T(8,128)}, u32[]{:S(2)}, u32[]{:S(2)}) collective-permute-start(f32[520,128]{1,0:T(8,128)} %collective-permute-done.4), channel_id=1, source_target_pairs={{0,352},{32,384},{64,416},{96,448},{128,480},{160,0},{192,32},{224... | collective-permute-start | bytes 798728 | tf_op jit(solution)/shard_map/ppermute | solution.py:38
  155.3 18.2 %collective-permute-start.10 = (f32[16,128,128]{2,1,0:T(8,128)S(1)}, f32[16,128,128]{2,1,0:T(8,128)S(1)}, u32[]{:S(2)}, u32[]{:S(2)}) collective-permute-start(f32[16,128,128]{2,1,0:T(8,128)S(1)} %galerkin.11), channel_id=1, source_target_pairs={{0,1},{1,2},{2,3},{3,4},{4,5},{5,6},{6,7},{7,8},{8,9},{9,10},{10,1... | collective-permute-start | bytes 3145736 | tf_op jit(solution)/shard_map/ppermute | solution.py:44

commit v4 on v3

--- a/solution.py
+++ b/solution.py
@@ -178,59 +178,50 @@
     )(*sources)
 
 
-def galerkin_kernel(rows, chunks, targets, fresh, slots, first, high, low, turned, *refs):
-    count = sum(len(c) for c in chunks)
-    buffers, refs = refs[:count], refs[count:]
+def galerkin_kernel(rows, chunks, targets, fresh, joined, slots, first, high, low, turned, *refs):
+    buffers, refs = refs[: len(chunks)], refs[len(chunks) :]
     if not fresh:
         befores, refs = refs[: len(targets)], refs[len(targets) :]
+    if joined:
+        arrived, refs = refs[0], refs[1:]
     accs, refs = refs[: len(targets)], refs[len(targets) :]
     lifted, held, notes, note_sem, sem = refs
-    at, note_copies, lines = 0, [], []
-    for n, lengths in enumerate(chunks):
-        parts = buffers[at : at + len(lengths)]
-        at += len(lengths)
-        end = lengths[0][0] - META
-        copy = pltpu.make_async_copy(parts[0].at[pl.ds(end, META)], notes.at[n], note_sem.at[n])
+    note_copies, lines = [], []
+    for n, (buffer, length) in enumerate(zip(buffers, chunks)):
+        copy = pltpu.make_async_copy(buffer.at[pl.ds(length - META, META)], notes.at[n], note_sem.at[n])
         copy.start()
         note_copies.append(copy)
-        for r in range(min(CAP, -(-end // ROW))):
-            size = min(ROW, end - r * ROW)
-            pieces = [(parts[0], r * ROW, 0, size)]
-            if size < ROW:
-                pieces.append((parts[1], lengths[1][1], size, ROW - size))
-            lines.append((n, r, pieces))
+        lines += [(n, r) for r in range(length // ROW)]
     for i, acc in enumerate(accs):
         if fresh:
             acc[...] = jnp.zeros_like(acc)
         else:
             acc[...] = befores[i][...]
+    if joined:
+        for i in range(arrived.shape[0] // WIDTHS[1]):
+            to = i * SLOTS
+            acc[to : to + WIDTHS[1]] += arrived[i * WIDTHS[1] : (i + 1) * WIDTHS[1]]
     for copy in note_copies:
         copy.wait()
 
     def note(n, r, k):
         return notes[n, r, k].astype(jnp.int32)
 
-    def copies(m):
-        return [
-            pltpu.make_async_copy(
-                part.at[pl.ds(frm, size)], held.at[m, pl.ds(to, size)], sem.at[2 * m + i]
-            )
-            for i, (part, frm, to, size) in enumerate(lines[m][2])
-        ]
-
-    for m, (n, r, _) in enumerate(lines):
+    def fetch(m):
+        n, r = lines[m]
+        return pltpu.make_async_copy(buffers[n].at[pl.ds(r * ROW, ROW)], held.at[m], sem.at[m])
+
+    for m, (n, r) in enumerate(lines):
 
         @pl.when(note(n, r, A_TILES) > 0)
         def _():
-            for copy in copies(m):
-                copy.start()
-
-    for m, (n, r, _) in enumerate(lines):
+            fetch(m).start()
+
+    for m, (n, r) in enumerate(lines):
 
         @pl.when(note(n, r, A_TILES) > 0)
         def _():
-            for copy in copies(m):
-                copy.wait()
+            fetch(m).wait()
             row = note(n, r, A_TILES) - 1
             cols = [note(n, r, k) - first[0] for k in range(A_TILES)]
             for k, c in enumerate(cols):
@@ -263,16 +254,15 @@
                                 acc[s] += w[:, lanes : lanes + TILE]
 
 
-def galerkin(weight, chunks, targets, first_row, slots, splits, befores, rows, coarse_rows):
-    shapes = [tuple((x.shape[0], frm) for x, frm in parts) for parts in chunks]
-    buffers = [x for parts in chunks for x, _ in parts]
+def galerkin(weight, chunks, targets, first_row, slots, splits, befores, arrived, rows, coarse_rows):
+    shapes = [x.shape[0] for x in chunks]
     out = [jax.ShapeDtypeStruct((coarse_rows * WIDTHS[t], TILE, TILE), jnp.float32) for t in targets]
-    befores = befores or []
-    operands = [slots, first_row, *splits, *buffers, *befores]
-    specs = [SMEM, SMEM] + [VMEM] * len(splits) + [ANY] * len(buffers) + [VMEM] * len(befores)
-    lines = sum(min(CAP, -(-(parts[0][0] - META) // ROW)) for parts in shapes)
+    befores, joined = list(befores or []), [] if arrived is None else [arrived]
+    operands = [slots, first_row, *splits, *chunks, *befores, *joined]
+    specs = [SMEM, SMEM] + [VMEM] * len(splits) + [ANY] * len(chunks) + [VMEM] * len(befores + joined)
+    lines = sum(n // ROW for n in shapes)
     return pl.pallas_call(
-        functools.partial(galerkin_kernel, rows, shapes, targets, not befores),
+        functools.partial(galerkin_kernel, rows, shapes, targets, not befores, bool(joined)),
         out_shape=out,
         in_specs=specs,
         out_specs=[VMEM] * len(out),
@@ -281,9 +271,9 @@
             pltpu.VMEM((lines, ROW, TILE), jnp.float32),
             pltpu.SMEM((len(chunks), META, TILE), jnp.float32),
             pltpu.SemaphoreType.DMA((len(chunks),)),
-            pltpu.SemaphoreType.DMA((2 * lines,)),
+            pltpu.SemaphoreType.DMA((lines,)),
         ],
-        input_output_aliases={len(operands) - len(befores) + i: i for i in range(len(befores))},
+        input_output_aliases={len(operands) - len(befores + joined) + i: i for i in range(len(befores))},
         compiler_params=pltpu.CompilerParams(vmem_limit_bytes=20 * 2**20),
         cost_estimate=pl.CostEstimate(flops=weight, bytes_accessed=1, transcendentals=0),
         name="galerkin",
@@ -292,6 +282,19 @@
 
 def after(value, *others):
     return lax.optimization_barrier((value, *others))[0]
+
+
+def pause_kernel(value, out):
+    out[...] = value[...]
+
+
+def pause(value):
+    return pl.pallas_call(
+        pause_kernel,
+        out_shape=jax.ShapeDtypeStruct(value.shape, value.dtype),
+        cost_estimate=pl.CostEstimate(flops=10**14, bytes_accessed=1, transcendentals=0),
+        name="pause",
+    )(value)
 
 
 def shards(a_tiles, a_cols, new_row, p_tiles, p_cols):
@@ -306,33 +309,45 @@
     sources = [p_before, p_here, p_after]
     d4 = hop(send["d4"], "gx", 4)
     far_a = hop(send["far_a"], "gx", -6)
+    far_b = hop(after(send["far_b"], p_after), "gx", -6)
+
+
+    def tables(sources, middle):
+        slots = jnp.concatenate([x[-rows:, :P_TILES] for x in sources], axis=0).astype(jnp.int32)
+        slots = slots - coarse_rows * device + 4
+        return ((middle - 1) * rows).reshape(1), slots, split(sources, rows)
+
+    mine = tables([p_before, p_here, p_after], device)
+
+    def add(data, targets, chunks, befores, weight=1, arrived=None):
+        return galerkin(weight, chunks, targets, *data, befores, arrived, rows, coarse_rows)
+
     d3 = hop(after(send["d3"], p_after), "gx", 3)
-    far_b = hop(after(send["far_b"], p_after), "gx", -6)
     d2 = hop(after(send["d2"], p_before, p_after), "gx", 2)
 
-    slots = jnp.concatenate([x[-rows:, :P_TILES] for x in sources], axis=0).astype(jnp.int32)
-    slots = slots - coarse_rows * device + 4
-    splits = split(sources, rows)
-    first_row = ((device - 1) * rows).reshape(1)
-
-    def add(targets, chunks, befores, weight=1):
-        return galerkin(weight, chunks, targets, first_row, slots, splits, befores, rows, coarse_rows)
-
-    both = add((0, 1), [[(send["d0"], 0)]], None, 10**14)
-    far_a = hop(after(far_a, p_before, p_after), "gx", -5)
+    both = add(mine, (0, 1), [send["d0"]], None, 10**14)
+    far_a = hop(after(far_a, both[0]), "gx", -5)
+    p_before_2 = beside(after(p_before, both[0]), 1)
+    theirs = tables([p_before_2, p_before, p_here], device - 1)
+    d4 = after(d4, both[0])
+    both = add(mine, (0, 1), [d4], both, 10**14)
     far_b = hop(after(far_b, both[0]), "gx", -5)
-    d4 = after(d4, both[0])
-    d1 = hop(after(send["d1"], d4), "gx", 1)
-    both = add((0, 1), [[(d4, 0)]], both, 10**14)
-    both = add((0, 1), [[(d3, 0)]], both)
-    own, on = add((0, 1), [[(d2, 0)], [(far_a, 0)]], both)
-    last = [[(d1, 0)], [(far_b, 0)]]
-    (on,) = add((1,), last, [on])
-    arrived = beside(on, 1)
-    (own,) = add((0,), last, [own])
-    own = own.reshape(coarse_rows, SLOTS, TILE, TILE)
-    arrived = arrived.reshape(coarse_rows, WIDTHS[1], TILE, TILE)
-    return own + jnp.pad(arrived, ((0, 0), (0, SLOTS - WIDTHS[1]), (0, 0), (0, 0)))
+    d1 = hop(after(send["d1"], both[0]), "gx", 1)
+    own, on = add(mine, (0, 1), [after(d3, theirs[1], *theirs[2])], both, 10**14)
+    token = pause(on[0, :META])
+    on = beside(on, 1)
+    far_a, d2 = after(far_a, token), after(d2, token)
+
+    f_far_a = beside(far_a, 1)
+    f2 = beside(d2, 1)
+    (own,) = add(mine, (0,), [d2, far_a], [own], 10**14)
+    mid = own
+    (own,) = add(theirs, (0,), [f2, f_far_a], [own], arrived=on)
+    f1 = beside(after(d1, mid), 1)
+    f_far_b = beside(after(far_b, mid), 1)
+    (own,) = add(mine, (0,), [d1, far_b], [own], 10**14)
+    (own,) = add(theirs, (0,), [f1, f_far_b], [own])
+    return own.reshape(coarse_rows, SLOTS, TILE, TILE)
 
 
 def solution(mesh):

time: 176 us -> 176 us (level)
  waiting for transfers between devices: 82 us -> 47.3 us
  Pallas kernels: 27 us -> 48.8 us
  starting transfers between devices: 62.5 us -> 73.2 us
  local copies, waits for them, and re-layouts: 1.92 us -> 3.86 us
    ppermute x8, waiting for transfers between devices: 70.2 us -> 40.3 us  [hop(): lax.ppermute(value, axis, [(i, (i + steps) % count) for i in range(count)])]
    pallas_call x6 -> x7, Pallas kernels: 21.2 us -> 39 us  [galerkin(): pl.pallas_call(functools.partial(galerkin_kernel, rows, shapes, targets,...]
    ppermute x3 -> x8, starting transfers between devices: 8.47 us -> 19.4 us  [beside(): return lax.ppermute(value, 'gy', route)]
    ppermute x3 -> x8, waiting for transfers between devices: 11.8 us -> 7.07 us  [beside(): return lax.ppermute(value, 'gy', route)]
    pallas_call x1 -> x2, Pallas kernels: 1.22 us -> 5.28 us  [split(): pl.pallas_call(functools.partial(split_kernel, rows), out_shape=[wide, wi...]
  transfers between devices with their start and end apart: 11 -> 16, of which waited for: 7 -> 6; matrix products, arithmetic and copies ran while one was open for 0% -> 1% of each run, Pallas kernels for 10% -> 22%
where the time goes in v4:
time: 176 us; the launch traced here: 174 us
  starting transfers between devices  73.2 us (42%)
  Pallas kernels  48.8 us (28%)
  waiting for transfers between devices  47.3 us (27%)
  local copies, waits for them, and re-layouts  3.86 us (2%)
    ppermute x8, starting transfers between devices, hop(): lax.ppermute(value, axis, [(i, (i + steps) % count) for i in range(count)])  53.8 us
    ppermute x8, waiting for transfers between devices, hop(): lax.ppermute(value, axis, [(i, (i + steps) % count) for i in range(count)])  40.3 us
    pallas_call x7, Pallas kernels, galerkin(): pl.pallas_call(functools.partial(galerkin_kernel, rows, shapes, targets,...  39 us
    ppermute x8, starting transfers between devices, beside(): return lax.ppermute(value, 'gy', route)  19.4 us
    ppermute x8, waiting for transfers between devices, beside(): return lax.ppermute(value, 'gy', route)  7.07 us
    pallas_call x2, Pallas kernels, split(): pl.pallas_call(functools.partial(split_kernel, rows), out_shape=[wide, wi...  5.28 us
    pallas_call x1, Pallas kernels, buckets(): pl.pallas_call(functools.partial(bucket_kernel, rows, gx, rows * gy, layo...  4.51 us
  transfers between devices with their start and end apart: 16, of which 6 were waited for; matrix products, arithmetic and copies ran while one was open for 1% of the time, Pallas kernels for 22%

profile of v4, /device:TPU:6, one launch (start us, length us, event | category | flops | bytes accessed | tf_op | source)
XLA Modules:
  0.0 173.7 jit_solution(6415630353908859430)
XLA Ops:
  0.0 4.5 %buckets.1 = (f32[2056,128]{1,0:T(8,128)}, f32[520,128]{1,0:T(8,128)}, f32[520,128]{1,0:T(8,128)}, f32[1032,128]{1,0:T(8,128)}, f32[1032,128]{1,0:T(8,128)}, /*i...) custom-call(s32[8]{0:T(128)} %new_row.1, s32[4,8]{1,0:T(4,128)} %bitcast.12, s32[2,8]{1,0:T(2,128)} %bitcast.13, ...), custom_call_target="tpu_custom_call" | custom-call | tf_op jit(solution)/shard_map/buckets/pallas_call | solution.py:124
  4.5 4.6 %collective-permute-start.1 = (f32[2056,128]{1,0:T(8,128)}, f32[2056,128]{1,0:T(8,128)S(1)}, u32[]{:S(2)}, u32[]{:S(2)}) collective-permute-start(f32[2056,128]{1,0:T(8,128)} %get-tuple-element.38.refs_1_.refs_2_), channel_id=1, source_target_pairs={{1,0},{2,1},{3,2},{4,3},{5,4},{6,5},{7,6},{8,7},{9,8},{10,9},{11,1... | collective-permute-start | bytes 3158024 | tf_op jit(solution)/shard_map/ppermute | solution.py:44
  9.2 1.9 %collective-permute-start = (f32[2056,128]{1,0:T(8,128)}, f32[2056,128]{1,0:T(8,128)}, u32[]{:S(2)}, u32[]{:S(2)}) collective-permute-start(f32[2056,128]{1,0:T(8,128)} %get-tuple-element.38.refs_1_.refs_2_), channel_id=1, source_target_pairs={{0,1},{1,2},{2,3},{3,4},{4,5},{5,6},{6,7},{7,8},{8,9},{9,10},{10,1... | collective-permute-start | bytes 3158024 | tf_op jit(solution)/shard_map/ppermute | solution.py:44
  11.1 14.8 %collective-permute-start.7 = (f32[520,128]{1,0:T(8,128)}, f32[520,128]{1,0:T(8,128)}, u32[]{:S(2)}, u32[]{:S(2)}) collective-permute-start(f32[520,128]{1,0:T(8,128)} %get-tuple-element.62), channel_id=1, source_target_pairs={{0,320},{32,352},{64,384},{96,416},{128,448},{160,480},{192,0},{22... | collective-permute-start | bytes 798728 | tf_op jit(solution)/shard_map/ppermute | solution.py:38
  25.9 4.3 %collective-permute-start.3 = (f32[1032,128]{1,0:T(8,128)}, f32[1032,128]{1,0:T(8,128)}, u32[]{:S(2)}, u32[]{:S(2)}) collective-permute-start(f32[1032,128]{1,0:T(8,128)} %get-tuple-element.49), channel_id=1, source_target_pairs={{0,128},{32,160},{64,192},{96,224},{128,256},{160,288},{192,320},{... | collective-permute-start | bytes 1585160 | tf_op jit(solution)/shard_map/ppermute | solution.py:38
  30.2 0.7 slice.18
  30.9 0.0 collective-permute-done.1.refs_2_
  30.9 6.3 %collective-permute-start.10 = (f32[520,128]{1,0:T(8,128)}, f32[520,128]{1,0:T(8,128)}, u32[]{:S(2)}, u32[]{:S(2)}) collective-permute-start(f32[520,128]{1,0:T(8,128)} %get-tuple-element.68), channel_id=1, source_target_pairs={{0,320},{32,352},{64,384},{96,416},{128,448},{160,480},{192,0},{22... | collective-permute-start | bytes 798728 | tf_op jit(solution)/shard_map/ppermute | solution.py:38
  37.2 3.8 %collective-permute-start.6 = (f32[1032,128]{1,0:T(8,128)}, f32[1032,128]{1,0:T(8,128)}, u32[]{:S(2)}, u32[]{:S(2)}) collective-permute-start(f32[1032,128]{1,0:T(8,128)} %get-tuple-element.57), channel_id=1, source_target_pairs={{0,96},{32,128},{64,160},{96,192},{128,224},{160,256},{192,288},{2... | collective-permute-start | bytes 1585160 | tf_op jit(solution)/shard_map/ppermute | solution.py:38
  41.1 0.0 collective-permute-done.refs_0_.refs_1_
  41.1 3.4 %collective-permute-start.5 = (f32[1032,128]{1,0:T(8,128)}, f32[1032,128]{1,0:T(8,128)}, u32[]{:S(2)}, u32[]{:S(2)}) collective-permute-start(f32[1032,128]{1,0:T(8,128)} %get-tuple-element.55), channel_id=1, source_target_pairs={{0,64},{32,96},{64,128},{96,160},{128,192},{160,224},{192,256},{22... | collective-permute-start | bytes 1585160 | tf_op jit(solution)/shard_map/ppermute | solution.py:38
  44.5 0.7 slice.22
  45.2 0.6 copy-done.5
  45.8 1.2 copy-done
  47.0 2.5 %split.2 = (bf16[24,128,256]{2,1,0:T(8,128)(2,1)S(1)}, bf16[24,128,256]{2,1,0:T(8,128)(2,1)S(1)}, bf16[16,256,128]{2,1,0:T(8,128)(2,1)S(1)}) custom-call(f32[2056,128]{1,0:T(8,128)} %collective-permute-done.refs_0_.refs_1_, f32[2056,128]{1,0:T(8,128)S(1)} %copy-done, f32[2056,128]{1,0:T(8,128)S(1)} %collective-permute-done.1.refs_2_), custom_call_target="tpu_custom_call" | custom-call | tf_op jit(solution)/shard_map/split/pallas_call | solution.py:171
  49.5 0.0 copy-done.3
  49.5 4.8 %galerkin.7 = (f32[20,128,128]{2,1,0:T(8,128)}, f32[16,128,128]{2,1,0:T(8,128)}) custom-call(s32[24,2]{1,0:T(8,128)S(1)} %fusion.1.slots, s32[1]{0:T(128)} %bitcast.5.first, bf16[24,128,256]{2,1,0:T(8,128)(2,1)S(1)} %get-tuple-element.39.high, bf16[24,128,256]{2,1,0:T(8,128)(2,1)S(1)} %get-tuple-element.40.low, ...), custom_call_target="tpu_custom_call" | custom-call | flops 100000000376832 | bytes 1 | tf_op jit(solution)/shard_map/galerkin/pallas_call | solution.py:264
  54.4 20.0 %collective-permute-done.7 = f32[520,128]{1,0:T(8,128)} collective-permute-done((f32[520,128]{1,0:T(8,128)}, f32[520,128]{1,0:T(8,128)}, u32[]{:S(2)}, u32[]{:S(2)}) %collective-permute-start.7) | collective-permute-done | bytes 266272 | tf_op jit(solution)/shard_map/ppermute | solution.py:38
  74.4 0.0 collective-permute-done.3.refs_0_
  74.4 11.9 %collective-permute-start.8 = (f32[520,128]{1,0:T(8,128)}, f32[520,128]{1,0:T(8,128)}, u32[]{:S(2)}, u32[]{:S(2)}) collective-permute-start(f32[520,128]{1,0:T(8,128)} %collective-permute-done.7), channel_id=1, source_target_pairs={{0,352},{32,384},{64,416},{96,448},{128,480},{160,0},{192,32},{224... | collective-permute-start | bytes 798728 | tf_op jit(solution)/shard_map/ppermute | solution.py:38
  86.2 1.9 %collective-permute-start.2 = (f32[2056,128]{1,0:T(8,128)}, f32[2056,128]{1,0:T(8,128)}, u32[]{:S(2)}, u32[]{:S(2)}) collective-permute-start(f32[2056,128]{1,0:T(8,128)} %collective-permute-done.refs_0_.refs_1_), channel_id=1, source_target_pairs={{0,1},{1,2},{2,3},{3,4},{4,5},{5,6},{6,7},{7,8},{8,9},{9,10},{10,1... | collective-permute-start | bytes 3158024 | tf_op jit(solution)/shard_map/ppermute | solution.py:44
  88.2 3.9 %galerkin.8 = (f32[20,128,128]{2,1,0:T(8,128)}, f32[16,128,128]{2,1,0:T(8,128)}) custom-call(s32[24,2]{1,0:T(8,128)S(1)} %fusion.1.slots, s32[1]{0:T(128)} %bitcast.5.first, bf16[24,128,256]{2,1,0:T(8,128)(2,1)S(1)} %get-tuple-element.39.high, bf16[24,128,256]{2,1,0:T(8,128)(2,1)S(1)} %get-tuple-element.40.low, ...), custom_call_target="tpu_custom_call", output_to_operand_aliasing={{0}: (6, {}), {1}: (7, {})} | custom-call | flops 100000000376832 | bytes 1 | tf_op jit(solution)/shard_map/galerkin/pallas_call | solution.py:264
  92.1 2.5 %collective-permute-done.10 = f32[520,128]{1,0:T(8,128)} collective-permute-done((f32[520,128]{1,0:T(8,128)}, f32[520,128]{1,0:T(8,128)}, u32[]{:S(2)}, u32[]{:S(2)}) %collective-permute-start.10) | collective-permute-done | bytes 266272 | tf_op jit(solution)/shard_map/ppermute | solution.py:38
  94.5 3.2 %collective-permute-start.4 = (f32[1032,128]{1,0:T(8,128)}, f32[1032,128]{1,0:T(8,128)}, u32[]{:S(2)}, u32[]{:S(2)}) collective-permute-start(f32[1032,128]{1,0:T(8,128)} %get-tuple-element.53), channel_id=1, source_target_pairs={{0,32},{32,64},{64,96},{96,128},{128,160},{160,192},{192,224},{224... | collective-permute-start | bytes 1585160 | tf_op jit(solution)/shard_map/ppermute | solution.py:38
  97.8 7.1 %collective-permute-done.2.refs_0_ = f32[2056,128]{1,0:T(8,128)} collective-permute-done((f32[2056,128]{1,0:T(8,128)}, f32[2056,128]{1,0:T(8,128)}, u32[]{:S(2)}, u32[]{:S(2)}) %collective-permute-start.2) | collective-permute-done | bytes 1052704 | tf_op jit(solution)/shard_map/ppermute | solution.py:44
  104.8 6.1 %collective-permute-start.11 = (f32[520,128]{1,0:T(8,128)}, f32[520,128]{1,0:T(8,128)}, u32[]{:S(2)}, u32[]{:S(2)}) collective-permute-start(f32[520,128]{1,0:T(8,128)} %collective-permute-done.10), channel_id=1, source_target_pairs={{0,352},{32,384},{64,416},{96,448},{128,480},{160,0},{192,32},{224... | collective-permute-start | bytes 798728 | tf_op jit(solution)/shard_map/ppermute | solution.py:38
  110.9 0.7 slice.24
  111.6 2.8 %split.3 = (bf16[24,128,256]{2,1,0:T(8,128)(2,1)S(1)}, bf16[24,128,256]{2,1,0:T(8,128)(2,1)S(1)}, bf16[16,256,128]{2,1,0:T(8,128)(2,1)S(1)}) custom-call(f32[2056,128]{1,0:T(8,128)} %collective-permute-done.2.refs_0_, f32[2056,128]{1,0:T(8,128)} %collective-permute-done.refs_0_.refs_1_, f32[2056,128]{1,0:T(8,128)S(1)} %copy-done.1), custom_call_target="tpu_custom_call" | custom-call | tf_op jit(solution)/shard_map/split/pallas_call | solution.py:171
  114.4 0.0 collective-permute-done.6.refs_0_
  114.4 6.7 %galerkin.9 = (f32[20,128,128]{2,1,0:T(8,128)}, f32[16,128,128]{2,1,0:T(8,128)}) custom-call(s32[24,2]{1,0:T(8,128)S(1)} %fusion.1.slots, s32[1]{0:T(128)} %bitcast.5.first, bf16[24,128,256]{2,1,0:T(8,128)(2,1)S(1)} %get-tuple-element.39.high, bf16[24,128,256]{2,1,0:T(8,128)(2,1)S(1)} %get-tuple-element.40.low, ...), custom_call_target="tpu_custom_call", output_to_operand_aliasing={{0}: (6, {}), {1}: (7, {})} | custom-call | flops 100000000376832 | bytes 1 | tf_op jit(solution)/shard_map/galerkin/pallas_call | solution.py:264
  121.1 1.9 %collective-permute-start.15 = (f32[16,128,128]{2,1,0:T(8,128)}, f32[16,128,128]{2,1,0:T(8,128)}, u32[]{:S(2)}, u32[]{:S(2)}) collective-permute-start(f32[16,128,128]{2,1,0:T(8,128)} %get-tuple-element.60), channel_id=1, source_target_pairs={{0,1},{1,2},{2,3},{3,4},{4,5},{5,6},{6,7},{7,8},{8,9},{9,10},{10,1... | collective-permute-start | bytes 3145736 | tf_op jit(solution)/shard_map/ppermute | solution.py:44
  123.0 7.1 %collective-permute-done.8.refs_1_ = f32[520,128]{1,0:T(8,128)} collective-permute-done((f32[520,128]{1,0:T(8,128)}, f32[520,128]{1,0:T(8,128)}, u32[]{:S(2)}, u32[]{:S(2)}) %collective-permute-start.8) | collective-permute-done | bytes 266272 | tf_op jit(solution)/shard_map/ppermute | solution.py:38
  130.2 4.7 %collective-permute-done.5.refs_0_ = f32[1032,128]{1,0:T(8,128)} collective-permute-done((f32[1032,128]{1,0:T(8,128)}, f32[1032,128]{1,0:T(8,128)}, u32[]{:S(2)}, u32[]{:S(2)}) %collective-permute-start.5) | collective-permute-done | bytes 528416 | tf_op jit(solution)/shard_map/ppermute | solution.py:38
  134.9 1.9 %collective-permute-start.14 = (f32[520,128]{1,0:T(8,128)}, f32[520,128]{1,0:T(8,128)}, u32[]{:S(2)}, u32[]{:S(2)}) collective-permute-start(f32[520,128]{1,0:T(8,128)} %collective-permute-done.8.refs_1_), channel_id=1, source_target_pairs={{0,1},{1,2},{2,3},{3,4},{4,5},{5,6},{6,7},{7,8},{8,9},{9,10},{10,1... | collective-permute-start | bytes 798728 | tf_op jit(solution)/shard_map/ppermute | solution.py:44
  136.8 1.9 %collective-permute-start.13 = (f32[1032,128]{1,0:T(8,128)}, f32[1032,128]{1,0:T(8,128)}, u32[]{:S(2)}, u32[]{:S(2)}) collective-permute-start(f32[1032,128]{1,0:T(8,128)} %collective-permute-done.5.refs_0_), channel_id=1, source_target_pairs={{0,1},{1,2},{2,3},{3,4},{4,5},{5,6},{6,7},{7,8},{8,9},{9,10},{10,1... | collective-permute-start | bytes 1585160 | tf_op jit(solution)/shard_map/ppermute | solution.py:44
  138.7 6.1 %galerkin.10.refs_2_ = f32[20,128,128]{2,1,0:T(8,128)} custom-call(s32[24,2]{1,0:T(8,128)S(1)} %fusion.1.slots, s32[1]{0:T(128)} %bitcast.5.first, bf16[24,128,256]{2,1,0:T(8,128)(2,1)S(1)} %get-tuple-element.39.high, bf16[24,128,256]{2,1,0:T(8,128)(2,1)S(1)} %get-tuple-element.40.low, ...), custom_call_target="tpu_custom_call", output_to_operand_aliasing={{}: (7, {})} | custom-call | flops 100000000376832 | bytes 1 | tf_op jit(solution)/shard_map/galerkin/pallas_call | solution.py:264
  144.9 6.0 %collective-permute-done.11.refs_1_ = f32[520,128]{1,0:T(8,128)} collective-permute-done((f32[520,128]{1,0:T(8,128)}, f32[520,128]{1,0:T(8,128)}, u32[]{:S(2)}, u32[]{:S(2)}) %collective-permute-start.11) | collective-permute-done | bytes 266272 | tf_op jit(solution)/shard_map/ppermute | solution.py:38
  150.8 0.0 collective-permute-done.4.refs_0_
  150.8 1.9 %collective-permute-start.12 = (f32[520,128]{1,0:T(8,128)}, f32[520,128]{1,0:T(8,128)}, u32[]{:S(2)}, u32[]{:S(2)}) collective-permute-start(f32[520,128]{1,0:T(8,128)} %collective-permute-done.11.refs_1_), channel_id=1, source_target_pairs={{0,1},{1,2},{2,3},{3,4},{4,5},{5,6},{6,7},{7,8},{8,9},{9,10},{10,1... | collective-permute-start | bytes 798728 | tf_op jit(solution)/shard_map/ppermute | solution.py:44
  152.7 3.3 %collective-permute-start.9 = (f32[1032,128]{1,0:T(8,128)}, f32[1032,128]{1,0:T(8,128)}, u32[]{:S(2)}, u32[]{:S(2)}) collective-permute-start(f32[1032,128]{1,0:T(8,128)} %collective-permute-done.4.refs_0_), channel_id=1, source_target_pairs={{0,1},{1,2},{2,3},{3,4},{4,5},{5,6},{6,7},{7,8},{8,9},{9,10},{10,1... | collective-permute-start | bytes 1585160 | tf_op jit(solution)/shard_map/ppermute | solution.py:44
  156.1 0.0 collective-permute-done.14.refs_1_
  156.1 0.0 collective-permute-done.13.refs_0_
  156.1 0.0 collective-permute-done.15.refs_3_
  156.1 6.5 %galerkin.11.refs_2_ = f32[20,128,128]{2,1,0:T(8,128)} custom-call(s32[24,2]{1,0:T(8,128)S(1)} %fusion.3.slots, s32[1]{0:T(128)} %bitcast.6.first, bf16[24,128,256]{2,1,0:T(8,128)(2,1)S(1)} %get-tuple-element.45.high, bf16[24,128,256]{2,1,0:T(8,128)(2,1)S(1)} %get-tuple-element.46.low, ...), custom_call_target="tpu_custom_call", output_to_operand_aliasing={{}: (7, {})} | custom-call | flops 1 | bytes 1 | tf_op jit(solution)/shard_map/galerkin/pallas_call | solution.py:264
  162.5 4.8 %galerkin.12.refs_2_ = f32[20,128,128]{2,1,0:T(8,128)} custom-call(s32[24,2]{1,0:T(8,128)S(1)} %fusion.1.slots, s32[1]{0:T(128)} %bitcast.5.first, bf16[24,128,256]{2,1,0:T(8,128)(2,1)S(1)} %get-tuple-element.39.high, bf16[24,128,256]{2,1,0:T(8,128)(2,1)S(1)} %get-tuple-element.40.low, ...), custom_call_target="tpu_custom_call", output_to_operand_aliasing={{}: (7, {})} | custom-call | flops 100000000376832 | bytes 1 | tf_op jit(solution)/shard_map/galerkin/pallas_call | solution.py:264
  167.4 0.0 collective-permute-done.12.refs_1_
  167.4 0.0 collective-permute-done.9.refs_0_
  167.4 6.2 %galerkin.13 = f32[20,128,128]{2,1,0:T(8,128)} custom-call(s32[24,2]{1,0:T(8,128)S(1)} %fusion.3.slots, s32[1]{0:T(128)} %bitcast.6.first, bf16[24,128,256]{2,1,0:T(8,128)(2,1)S(1)} %get-tuple-element.45.high, bf16[24,128,256]{2,1,0:T(8,128)(2,1)S(1)} %get-tuple-element.46.low, ...), custom_call_target="tpu_custom_call", output_to_operand_aliasing={{}: (7, {})} | custom-call | flops 1 | bytes 1 | tf_op jit(solution)/shard_map/galerkin/pallas_call | solution.py:264
  (14 shorter events, 0.0 us)
Async XLA Ops:
  4.5 26.4 %collective-permute-start.1 = (f32[2056,128]{1,0:T(8,128)}, f32[2056,128]{1,0:T(8,128)S(1)}, u32[]{:S(2)}, u32[]{:S(2)}) collective-permute-start(f32[2056,128]{1,0:T(8,128)} %get-tuple-element.38.refs_1_.refs_2_), channel_id=1, source_target_pairs={{1,0},{2,1},{3,2},{4,3},{5,4},{6,5},{7,6},{8,7},{9,8},{10,9},{11,1... | collective-permute-start | bytes 3158024 | tf_op jit(solution)/shard_map/ppermute | solution.py:44
  9.2 31.9 %collective-permute-start = (f32[2056,128]{1,0:T(8,128)}, f32[2056,128]{1,0:T(8,128)}, u32[]{:S(2)}, u32[]{:S(2)}) collective-permute-start(f32[2056,128]{1,0:T(8,128)} %get-tuple-element.38.refs_1_.refs_2_), channel_id=1, source_target_pairs={{0,1},{1,2},{2,3},{3,4},{4,5},{5,6},{6,7},{7,8},{8,9},{9,10},{10,1... | collective-permute-start | bytes 3158024 | tf_op jit(solution)/shard_map/ppermute | solution.py:44
  11.1 63.3 %collective-permute-start.7 = (f32[520,128]{1,0:T(8,128)}, f32[520,128]{1,0:T(8,128)}, u32[]{:S(2)}, u32[]{:S(2)}) collective-permute-start(f32[520,128]{1,0:T(8,128)} %get-tuple-element.62), channel_id=1, source_target_pairs={{0,320},{32,352},{64,384},{96,416},{128,448},{160,480},{192,0},{22... | collective-permute-start | bytes 798728 | tf_op jit(solution)/shard_map/ppermute | solution.py:38
  25.9 48.5 %collective-permute-start.3 = (f32[1032,128]{1,0:T(8,128)}, f32[1032,128]{1,0:T(8,128)}, u32[]{:S(2)}, u32[]{:S(2)}) collective-permute-start(f32[1032,128]{1,0:T(8,128)} %get-tuple-element.49), channel_id=1, source_target_pairs={{0,128},{32,160},{64,192},{96,224},{128,256},{160,288},{192,320},{... | collective-permute-start | bytes 1585160 | tf_op jit(solution)/shard_map/ppermute | solution.py:38
  30.9 18.6 %copy-start.3 = (f32[8,2]{1,0:T(8,128)}, f32[8,2]{1,0:T(8,128)S(1)}, u32[]{:S(2)}) copy-start(f32[8,2]{1,0:T(8,128)S(1)} %slice.18) | copy-start | bytes 196
  30.9 63.6 %collective-permute-start.10 = (f32[520,128]{1,0:T(8,128)}, f32[520,128]{1,0:T(8,128)}, u32[]{:S(2)}, u32[]{:S(2)}) collective-permute-start(f32[520,128]{1,0:T(8,128)} %get-tuple-element.68), channel_id=1, source_target_pairs={{0,320},{32,352},{64,384},{96,416},{128,448},{160,480},{192,0},{22... | collective-permute-start | bytes 798728 | tf_op jit(solution)/shard_map/ppermute | solution.py:38
  37.2 77.1 %collective-permute-start.6 = (f32[1032,128]{1,0:T(8,128)}, f32[1032,128]{1,0:T(8,128)}, u32[]{:S(2)}, u32[]{:S(2)}) collective-permute-start(f32[1032,128]{1,0:T(8,128)} %get-tuple-element.57), channel_id=1, source_target_pairs={{0,96},{32,128},{64,160},{96,192},{128,224},{160,256},{192,288},{2... | collective-permute-start | bytes 1585160 | tf_op jit(solution)/shard_map/ppermute | solution.py:38
  41.1 93.8 %collective-permute-start.5 = (f32[1032,128]{1,0:T(8,128)}, f32[1032,128]{1,0:T(8,128)}, u32[]{:S(2)}, u32[]{:S(2)}) collective-permute-start(f32[1032,128]{1,0:T(8,128)} %get-tuple-element.55), channel_id=1, source_target_pairs={{0,64},{32,96},{64,128},{96,160},{128,192},{160,224},{192,256},{22... | collective-permute-start | bytes 1585160 | tf_op jit(solution)/shard_map/ppermute | solution.py:38
  45.2 0.6 copy-start.5
  45.8 1.2 copy-start
  47.0 2.5 %copy-start.2 = (f32[1032,128]{1,0:T(8,128)S(1)}, f32[1032,128]{1,0:T(8,128)}, u32[]{:S(2)}) copy-start(f32[1032,128]{1,0:T(8,128)} %get-tuple-element.42.refs_0_) | copy-start | bytes 1585156
  74.4 55.8 %collective-permute-start.8 = (f32[520,128]{1,0:T(8,128)}, f32[520,128]{1,0:T(8,128)}, u32[]{:S(2)}, u32[]{:S(2)}) collective-permute-start(f32[520,128]{1,0:T(8,128)} %collective-permute-done.7), channel_id=1, source_target_pairs={{0,352},{32,384},{64,416},{96,448},{128,480},{160,0},{192,32},{224... | collective-permute-start | bytes 798728 | tf_op jit(solution)/shard_map/ppermute | solution.py:38
  86.2 18.6 %collective-permute-start.2 = (f32[2056,128]{1,0:T(8,128)}, f32[2056,128]{1,0:T(8,128)}, u32[]{:S(2)}, u32[]{:S(2)}) collective-permute-start(f32[2056,128]{1,0:T(8,128)} %collective-permute-done.refs_0_.refs_1_), channel_id=1, source_target_pairs={{0,1},{1,2},{2,3},{3,4},{4,5},{5,6},{6,7},{7,8},{8,9},{9,10},{10,1... | collective-permute-start | bytes 3158024 | tf_op jit(solution)/shard_map/ppermute | solution.py:44
  88.2 23.4 %copy-start.1 = (f32[2056,128]{1,0:T(8,128)S(1)}, f32[2056,128]{1,0:T(8,128)}, u32[]{:S(2)}) copy-start(f32[2056,128]{1,0:T(8,128)} %get-tuple-element.38.refs_1_.refs_2_) | copy-start | bytes 3158020
  92.1 22.3 %copy-start.4 = (f32[8,2]{1,0:T(8,128)S(1)}, f32[8,2]{1,0:T(8,128)}, u32[]{:S(2)}) copy-start(f32[8,2]{1,0:T(8,128)} %copy-done.3) | copy-start | bytes 196
  92.1 22.3 %copy-start.6 = (f32[8,2]{1,0:T(8,128)S(1)}, f32[8,2]{1,0:T(8,128)}, u32[]{:S(2)}) copy-start(f32[8,2]{1,0:T(8,128)} %copy-done.5) | copy-start | bytes 196
  94.5 56.3 %collective-permute-start.4 = (f32[1032,128]{1,0:T(8,128)}, f32[1032,128]{1,0:T(8,128)}, u32[]{:S(2)}, u32[]{:S(2)}) collective-permute-start(f32[1032,128]{1,0:T(8,128)} %get-tuple-element.53), channel_id=1, source_target_pairs={{0,32},{32,64},{64,96},{96,128},{128,160},{160,192},{192,224},{224... | collective-permute-start | bytes 1585160 | tf_op jit(solution)/shard_map/ppermute | solution.py:38
  104.8 46.0 %collective-permute-start.11 = (f32[520,128]{1,0:T(8,128)}, f32[520,128]{1,0:T(8,128)}, u32[]{:S(2)}, u32[]{:S(2)}) collective-permute-start(f32[520,128]{1,0:T(8,128)} %collective-permute-done.10), channel_id=1, source_target_pairs={{0,352},{32,384},{64,416},{96,448},{128,480},{160,0},{192,32},{224... | collective-permute-start | bytes 798728 | tf_op jit(solution)/shard_map/ppermute | solution.py:38
  121.1 35.0 %collective-permute-start.15 = (f32[16,128,128]{2,1,0:T(8,128)}, f32[16,128,128]{2,1,0:T(8,128)}, u32[]{:S(2)}, u32[]{:S(2)}) collective-permute-start(f32[16,128,128]{2,1,0:T(8,128)} %get-tuple-element.60), channel_id=1, source_target_pairs={{0,1},{1,2},{2,3},{3,4},{4,5},{5,6},{6,7},{7,8},{8,9},{9,10},{10,1... | collective-permute-start | bytes 3145736 | tf_op jit(solution)/shard_map/ppermute | solution.py:44
  134.9 21.2 %collective-permute-start.14 = (f32[520,128]{1,0:T(8,128)}, f32[520,128]{1,0:T(8,128)}, u32[]{:S(2)}, u32[]{:S(2)}) collective-permute-start(f32[520,128]{1,0:T(8,128)} %collective-permute-done.8.refs_1_), channel_id=1, source_target_pairs={{0,1},{1,2},{2,3},{3,4},{4,5},{5,6},{6,7},{7,8},{8,9},{9,10},{10,1... | collective-permute-start | bytes 798728 | tf_op jit(solution)/shard_map/ppermute | solution.py:44
  136.8 19.3 %collective-permute-start.13 = (f32[1032,128]{1,0:T(8,128)}, f32[1032,128]{1,0:T(8,128)}, u32[]{:S(2)}, u32[]{:S(2)}) collective-permute-start(f32[1032,128]{1,0:T(8,128)} %collective-permute-done.5.refs_0_), channel_id=1, source_target_pairs={{0,1},{1,2},{2,3},{3,4},{4,5},{5,6},{6,7},{7,8},{8,9},{9,10},{10,1... | collective-permute-start | bytes 1585160 | tf_op jit(solution)/shard_map/ppermute | solution.py:44
  150.8 16.6 %collective-permute-start.12 = (f32[520,128]{1,0:T(8,128)}, f32[520,128]{1,0:T(8,128)}, u32[]{:S(2)}, u32[]{:S(2)}) collective-permute-start(f32[520,128]{1,0:T(8,128)} %collective-permute-done.11.refs_1_), channel_id=1, source_target_pairs={{0,1},{1,2},{2,3},{3,4},{4,5},{5,6},{6,7},{7,8},{8,9},{9,10},{10,1... | collective-permute-start | bytes 798728 | tf_op jit(solution)/shard_map/ppermute | solution.py:44
  152.7 14.6 %collective-permute-start.9 = (f32[1032,128]{1,0:T(8,128)}, f32[1032,128]{1,0:T(8,128)}, u32[]{:S(2)}, u32[]{:S(2)}) collective-permute-start(f32[1032,128]{1,0:T(8,128)} %collective-permute-done.4.refs_0_), channel_id=1, source_target_pairs={{0,1},{1,2},{2,3},{3,4},{4,5},{5,6},{6,7},{7,8},{8,9},{9,10},{10,1... | collective-permute-start | bytes 1585160 | tf_op jit(solution)/shard_map/ppermute | solution.py:44

commit v5 on v4

--- a/solution.py
+++ b/solution.py
@@ -273,7 +273,6 @@
             pltpu.SemaphoreType.DMA((len(chunks),)),
             pltpu.SemaphoreType.DMA((lines,)),
         ],
-        input_output_aliases={len(operands) - len(befores + joined) + i: i for i in range(len(befores))},
         compiler_params=pltpu.CompilerParams(vmem_limit_bytes=20 * 2**20),
         cost_estimate=pl.CostEstimate(flops=weight, bytes_accessed=1, transcendentals=0),
         name="galerkin",
@@ -343,8 +342,8 @@
     (own,) = add(mine, (0,), [d2, far_a], [own], 10**14)
     mid = own
     (own,) = add(theirs, (0,), [f2, f_far_a], [own], arrived=on)
+    f_far_b = beside(after(far_b, own), 1)
     f1 = beside(after(d1, mid), 1)
-    f_far_b = beside(after(far_b, mid), 1)
     (own,) = add(mine, (0,), [d1, far_b], [own], 10**14)
     (own,) = add(theirs, (0,), [f1, f_far_b], [own])
     return own.reshape(coarse_rows, SLOTS, TILE, TILE)

time: 176 us -> 172 us (0.977)
  Pallas kernels: 48.8 us -> 37 us
  waiting for transfers between devices: 47.3 us -> 58.4 us
  starting transfers between devices: 73.2 us -> 70.6 us
    pallas_call x7, Pallas kernels: 39 us -> 27.2 us  [galerkin(): pl.pallas_call(functools.partial(galerkin_kernel, rows, shapes, targets,...]
    ppermute x8, waiting for transfers between devices: 7.07 us -> 16.7 us  [beside(): return lax.ppermute(value, 'gy', route)]
  transfers between devices with their start and end apart: 16 -> 16, of which waited for: 6 -> 8; matrix products, arithmetic and copies ran while one was open for 1% -> 1% of each run, Pallas kernels for 22% -> 16%
where the time goes in v5:
time: 172 us; the launch traced here: 170 us
  starting transfers between devices  70.6 us (41%)
  waiting for transfers between devices  58.4 us (34%)
  Pallas kernels  37 us (22%)
  local copies, waits for them, and re-layouts  3.86 us (2%)
    ppermute x8, starting transfers between devices, hop(): lax.ppermute(value, axis, [(i, (i + steps) % count) for i in range(count)])  52.5 us
    ppermute x8, waiting for transfers between devices, hop(): lax.ppermute(value, axis, [(i, (i + steps) % count) for i in range(count)])  41.6 us
    pallas_call x7, Pallas kernels, galerkin(): pl.pallas_call(functools.partial(galerkin_kernel, rows, shapes, targets,...  27.2 us
    ppermute x8, starting transfers between devices, beside(): return lax.ppermute(value, 'gy', route)  18.1 us
    ppermute x8, waiting for transfers between devices, beside(): return lax.ppermute(value, 'gy', route)  16.7 us
    pallas_call x2, Pallas kernels, split(): pl.pallas_call(functools.partial(split_kernel, rows), out_shape=[wide, wi...  5.28 us
    pallas_call x1, Pallas kernels, buckets(): pl.pallas_call(functools.partial(bucket_kernel, rows, gx, rows * gy, layo...  4.51 us
  transfers between devices with their start and end apart: 16, of which 8 were waited for; matrix products, arithmetic and copies ran while one was open for 1% of the time, Pallas kernels for 16%

profile of v5, /device:TPU:6, one launch (start us, length us, event | category | flops | bytes accessed | tf_op | source)
XLA Modules:
  0.0 170.3 jit_solution(12438029368874998606)
XLA Ops:
  0.0 4.5 %buckets.1 = (f32[2056,128]{1,0:T(8,128)}, f32[520,128]{1,0:T(8,128)}, f32[520,128]{1,0:T(8,128)}, f32[1032,128]{1,0:T(8,128)}, f32[1032,128]{1,0:T(8,128)}, /*i...) custom-call(s32[8]{0:T(128)} %new_row.1, s32[4,8]{1,0:T(4,128)} %bitcast.12, s32[2,8]{1,0:T(2,128)} %bitcast.13, ...), custom_call_target="tpu_custom_call" | custom-call | tf_op jit(solution)/shard_map/buckets/pallas_call | solution.py:124
  4.5 4.6 %collective-permute-start.1 = (f32[2056,128]{1,0:T(8,128)}, f32[2056,128]{1,0:T(8,128)S(1)}, u32[]{:S(2)}, u32[]{:S(2)}) collective-permute-start(f32[2056,128]{1,0:T(8,128)} %get-tuple-element.38.refs_1_.refs_2_), channel_id=1, source_target_pairs={{1,0},{2,1},{3,2},{4,3},{5,4},{6,5},{7,6},{8,7},{9,8},{10,9},{11,1... | collective-permute-start | bytes 3158024 | tf_op jit(solution)/shard_map/ppermute | solution.py:44
  9.2 1.9 %collective-permute-start = (f32[2056,128]{1,0:T(8,128)}, f32[2056,128]{1,0:T(8,128)}, u32[]{:S(2)}, u32[]{:S(2)}) collective-permute-start(f32[2056,128]{1,0:T(8,128)} %get-tuple-element.38.refs_1_.refs_2_), channel_id=1, source_target_pairs={{0,1},{1,2},{2,3},{3,4},{4,5},{5,6},{6,7},{7,8},{8,9},{9,10},{10,1... | collective-permute-start | bytes 3158024 | tf_op jit(solution)/shard_map/ppermute | solution.py:44
  11.1 14.8 %collective-permute-start.7 = (f32[520,128]{1,0:T(8,128)}, f32[520,128]{1,0:T(8,128)}, u32[]{:S(2)}, u32[]{:S(2)}) collective-permute-start(f32[520,128]{1,0:T(8,128)} %get-tuple-element.62), channel_id=1, source_target_pairs={{0,320},{32,352},{64,384},{96,416},{128,448},{160,480},{192,0},{22... | collective-permute-start | bytes 798728 | tf_op jit(solution)/shard_map/ppermute | solution.py:38
  25.9 4.3 %collective-permute-start.3 = (f32[1032,128]{1,0:T(8,128)}, f32[1032,128]{1,0:T(8,128)}, u32[]{:S(2)}, u32[]{:S(2)}) collective-permute-start(f32[1032,128]{1,0:T(8,128)} %get-tuple-element.49), channel_id=1, source_target_pairs={{0,128},{32,160},{64,192},{96,224},{128,256},{160,288},{192,320},{... | collective-permute-start | bytes 1585160 | tf_op jit(solution)/shard_map/ppermute | solution.py:38
  30.2 0.7 slice.18
  30.9 0.0 collective-permute-done.1.refs_2_
  30.9 6.3 %collective-permute-start.10 = (f32[520,128]{1,0:T(8,128)}, f32[520,128]{1,0:T(8,128)}, u32[]{:S(2)}, u32[]{:S(2)}) collective-permute-start(f32[520,128]{1,0:T(8,128)} %get-tuple-element.68), channel_id=1, source_target_pairs={{0,320},{32,352},{64,384},{96,416},{128,448},{160,480},{192,0},{22... | collective-permute-start | bytes 798728 | tf_op jit(solution)/shard_map/ppermute | solution.py:38
  37.3 3.8 %collective-permute-start.6 = (f32[1032,128]{1,0:T(8,128)}, f32[1032,128]{1,0:T(8,128)}, u32[]{:S(2)}, u32[]{:S(2)}) collective-permute-start(f32[1032,128]{1,0:T(8,128)} %get-tuple-element.57), channel_id=1, source_target_pairs={{0,96},{32,128},{64,160},{96,192},{128,224},{160,256},{192,288},{2... | collective-permute-start | bytes 1585160 | tf_op jit(solution)/shard_map/ppermute | solution.py:38
  41.1 0.0 collective-permute-done.refs_0_.refs_1_
  41.1 3.4 %collective-permute-start.5 = (f32[1032,128]{1,0:T(8,128)}, f32[1032,128]{1,0:T(8,128)}, u32[]{:S(2)}, u32[]{:S(2)}) collective-permute-start(f32[1032,128]{1,0:T(8,128)} %get-tuple-element.55), channel_id=1, source_target_pairs={{0,64},{32,96},{64,128},{96,160},{128,192},{160,224},{192,256},{22... | collective-permute-start | bytes 1585160 | tf_op jit(solution)/shard_map/ppermute | solution.py:38
  44.5 0.7 slice.22
  45.2 0.6 copy-done.5
  45.8 1.2 copy-done
  47.0 2.5 %split.2 = (bf16[24,128,256]{2,1,0:T(8,128)(2,1)S(1)}, bf16[24,128,256]{2,1,0:T(8,128)(2,1)S(1)}, bf16[16,256,128]{2,1,0:T(8,128)(2,1)S(1)}) custom-call(f32[2056,128]{1,0:T(8,128)} %collective-permute-done.refs_0_.refs_1_, f32[2056,128]{1,0:T(8,128)S(1)} %copy-done, f32[2056,128]{1,0:T(8,128)S(1)} %collective-permute-done.1.refs_2_), custom_call_target="tpu_custom_call" | custom-call | tf_op jit(solution)/shard_map/split/pallas_call | solution.py:171
  49.6 3.4 %galerkin.7 = (f32[20,128,128]{2,1,0:T(8,128)S(1)}, f32[16,128,128]{2,1,0:T(8,128)S(1)}) custom-call(s32[24,2]{1,0:T(8,128)S(1)} %fusion.1.slots, s32[1]{0:T(128)} %bitcast.5.first, bf16[24,128,256]{2,1,0:T(8,128)(2,1)S(1)} %get-tuple-element.39.high, bf16[24,128,256]{2,1,0:T(8,128)(2,1)S(1)} %get-tuple-element.40.low, ...), custom_call_target="tpu_custom_call" | custom-call | flops 100000000376832 | bytes 1 | tf_op jit(solution)/shard_map/galerkin/pallas_call | solution.py:264
  53.0 21.4 %collective-permute-done.7 = f32[520,128]{1,0:T(8,128)} collective-permute-done((f32[520,128]{1,0:T(8,128)}, f32[520,128]{1,0:T(8,128)}, u32[]{:S(2)}, u32[]{:S(2)}) %collective-permute-start.7) | collective-permute-done | bytes 266272 | tf_op jit(solution)/shard_map/ppermute | solution.py:38
  74.4 0.0 collective-permute-done.3.refs_0_
  74.4 11.9 %collective-permute-start.8 = (f32[520,128]{1,0:T(8,128)}, f32[520,128]{1,0:T(8,128)}, u32[]{:S(2)}, u32[]{:S(2)}) collective-permute-start(f32[520,128]{1,0:T(8,128)} %collective-permute-done.7), channel_id=1, source_target_pairs={{0,352},{32,384},{64,416},{96,448},{128,480},{160,0},{192,32},{224... | collective-permute-start | bytes 798728 | tf_op jit(solution)/shard_map/ppermute | solution.py:38
  86.2 1.9 %collective-permute-start.2 = (f32[2056,128]{1,0:T(8,128)}, f32[2056,128]{1,0:T(8,128)}, u32[]{:S(2)}, u32[]{:S(2)}) collective-permute-start(f32[2056,128]{1,0:T(8,128)} %collective-permute-done.refs_0_.refs_1_), channel_id=1, source_target_pairs={{0,1},{1,2},{2,3},{3,4},{4,5},{5,6},{6,7},{7,8},{8,9},{9,10},{10,1... | collective-permute-start | bytes 3158024 | tf_op jit(solution)/shard_map/ppermute | solution.py:44
  88.2 0.0 copy-start.1
  88.2 1.5 galerkin.8
  89.7 4.8 %collective-permute-done.10 = f32[520,128]{1,0:T(8,128)} collective-permute-done((f32[520,128]{1,0:T(8,128)}, f32[520,128]{1,0:T(8,128)}, u32[]{:S(2)}, u32[]{:S(2)}) %collective-permute-start.10) | collective-permute-done | bytes 266272 | tf_op jit(solution)/shard_map/ppermute | solution.py:38
  94.5 1.9 %collective-permute-start.4 = (f32[1032,128]{1,0:T(8,128)}, f32[1032,128]{1,0:T(8,128)}, u32[]{:S(2)}, u32[]{:S(2)}) collective-permute-start(f32[1032,128]{1,0:T(8,128)} %get-tuple-element.53), channel_id=1, source_target_pairs={{0,32},{32,64},{64,96},{96,128},{128,160},{160,192},{192,224},{224... | collective-permute-start | bytes 1585160 | tf_op jit(solution)/shard_map/ppermute | solution.py:38
  96.5 8.4 %collective-permute-done.2.refs_0_ = f32[2056,128]{1,0:T(8,128)} collective-permute-done((f32[2056,128]{1,0:T(8,128)}, f32[2056,128]{1,0:T(8,128)}, u32[]{:S(2)}, u32[]{:S(2)}) %collective-permute-start.2) | collective-permute-done | bytes 1052704 | tf_op jit(solution)/shard_map/ppermute | solution.py:44
  104.8 6.1 %collective-permute-start.11 = (f32[520,128]{1,0:T(8,128)}, f32[520,128]{1,0:T(8,128)}, u32[]{:S(2)}, u32[]{:S(2)}) collective-permute-start(f32[520,128]{1,0:T(8,128)} %collective-permute-done.10), channel_id=1, source_target_pairs={{0,352},{32,384},{64,416},{96,448},{128,480},{160,0},{192,32},{224... | collective-permute-start | bytes 798728 | tf_op jit(solution)/shard_map/ppermute | solution.py:38
  110.9 0.7 slice.24
  111.6 2.8 %split.3 = (bf16[24,128,256]{2,1,0:T(8,128)(2,1)S(1)}, bf16[24,128,256]{2,1,0:T(8,128)(2,1)S(1)}, bf16[16,256,128]{2,1,0:T(8,128)(2,1)S(1)}) custom-call(f32[2056,128]{1,0:T(8,128)} %collective-permute-done.2.refs_0_, f32[2056,128]{1,0:T(8,128)} %collective-permute-done.refs_0_.refs_1_, f32[2056,128]{1,0:T(8,128)S(1)} %copy-done.1), custom_call_target="tpu_custom_call" | custom-call | tf_op jit(solution)/shard_map/split/pallas_call | solution.py:171
  114.4 0.0 collective-permute-done.6.refs_0_
  114.4 5.4 %galerkin.9 = (f32[20,128,128]{2,1,0:T(8,128)S(1)}, f32[16,128,128]{2,1,0:T(8,128)}) custom-call(s32[24,2]{1,0:T(8,128)S(1)} %fusion.1.slots, s32[1]{0:T(128)} %bitcast.5.first, bf16[24,128,256]{2,1,0:T(8,128)(2,1)S(1)} %get-tuple-element.39.high, bf16[24,128,256]{2,1,0:T(8,128)(2,1)S(1)} %get-tuple-element.40.low, ...), custom_call_target="tpu_custom_call" | custom-call | flops 100000000376832 | bytes 1 | tf_op jit(solution)/shard_map/galerkin/pallas_call | solution.py:264
  119.8 1.9 %collective-permute-start.14 = (f32[16,128,128]{2,1,0:T(8,128)}, f32[16,128,128]{2,1,0:T(8,128)}, u32[]{:S(2)}, u32[]{:S(2)}) collective-permute-start(f32[16,128,128]{2,1,0:T(8,128)} %get-tuple-element.60), channel_id=1, source_target_pairs={{0,1},{1,2},{2,3},{3,4},{4,5},{5,6},{6,7},{7,8},{8,9},{9,10},{10,1... | collective-permute-start | bytes 3145736 | tf_op jit(solution)/shard_map/ppermute | solution.py:44
  121.7 8.5 %collective-permute-done.8.refs_1_ = f32[520,128]{1,0:T(8,128)} collective-permute-done((f32[520,128]{1,0:T(8,128)}, f32[520,128]{1,0:T(8,128)}, u32[]{:S(2)}, u32[]{:S(2)}) %collective-permute-start.8) | collective-permute-done | bytes 266272 | tf_op jit(solution)/shard_map/ppermute | solution.py:38
  130.2 4.7 %collective-permute-done.5.refs_0_ = f32[1032,128]{1,0:T(8,128)} collective-permute-done((f32[1032,128]{1,0:T(8,128)}, f32[1032,128]{1,0:T(8,128)}, u32[]{:S(2)}, u32[]{:S(2)}) %collective-permute-start.5) | collective-permute-done | bytes 528416 | tf_op jit(solution)/shard_map/ppermute | solution.py:38
  134.9 1.9 %collective-permute-start.13 = (f32[520,128]{1,0:T(8,128)}, f32[520,128]{1,0:T(8,128)}, u32[]{:S(2)}, u32[]{:S(2)}) collective-permute-start(f32[520,128]{1,0:T(8,128)} %collective-permute-done.8.refs_1_), channel_id=1, source_target_pairs={{0,1},{1,2},{2,3},{3,4},{4,5},{5,6},{6,7},{7,8},{8,9},{9,10},{10,1... | collective-permute-start | bytes 798728 | tf_op jit(solution)/shard_map/ppermute | solution.py:44
  136.8 1.9 %collective-permute-start.12 = (f32[1032,128]{1,0:T(8,128)}, f32[1032,128]{1,0:T(8,128)}, u32[]{:S(2)}, u32[]{:S(2)}) collective-permute-start(f32[1032,128]{1,0:T(8,128)} %collective-permute-done.5.refs_0_), channel_id=1, source_target_pairs={{0,1},{1,2},{2,3},{3,4},{4,5},{5,6},{6,7},{7,8},{8,9},{9,10},{10,1... | collective-permute-start | bytes 1585160 | tf_op jit(solution)/shard_map/ppermute | solution.py:44
  138.7 3.2 %galerkin.10.refs_2_ = f32[20,128,128]{2,1,0:T(8,128)S(1)} custom-call(s32[24,2]{1,0:T(8,128)S(1)} %fusion.1.slots, s32[1]{0:T(128)} %bitcast.5.first, bf16[24,128,256]{2,1,0:T(8,128)(2,1)S(1)} %get-tuple-element.39.high, bf16[24,128,256]{2,1,0:T(8,128)(2,1)S(1)} %get-tuple-element.40.low, bf16[16,256,128]{2,1,0:T(8,128)(2,1)S(1)} %get-tuple-element.41.turned, ...), custom_call_target="tpu_custom_call" | custom-call | flops 100000000376832 | bytes 1 | tf_op jit(solution)/shard_map/galerkin/pallas_call | solution.py:264
  141.9 2.2 %collective-permute-done.4.refs_0_ = f32[1032,128]{1,0:T(8,128)} collective-permute-done((f32[1032,128]{1,0:T(8,128)}, f32[1032,128]{1,0:T(8,128)}, u32[]{:S(2)}, u32[]{:S(2)}) %collective-permute-start.4) | collective-permute-done | bytes 528416 | tf_op jit(solution)/shard_map/ppermute | solution.py:38
  144.1 1.9 %collective-permute-start.9 = (f32[1032,128]{1,0:T(8,128)}, f32[1032,128]{1,0:T(8,128)}, u32[]{:S(2)}, u32[]{:S(2)}) collective-permute-start(f32[1032,128]{1,0:T(8,128)} %collective-permute-done.4.refs_0_), channel_id=1, source_target_pairs={{0,1},{1,2},{2,3},{3,4},{4,5},{5,6},{6,7},{7,8},{8,9},{9,10},{10,1... | collective-permute-start | bytes 1585160 | tf_op jit(solution)/shard_map/ppermute | solution.py:44
  146.1 0.0 collective-permute-done.13.refs_1_
  146.1 4.6 %collective-permute-done.12.refs_0_ = f32[1032,128]{1,0:T(8,128)} collective-permute-done((f32[1032,128]{1,0:T(8,128)}, f32[1032,128]{1,0:T(8,128)}, u32[]{:S(2)}, u32[]{:S(2)}) %collective-permute-start.12) | collective-permute-done | bytes 528416 | tf_op jit(solution)/shard_map/ppermute | solution.py:44
  150.7 0.0 collective-permute-done.14.refs_3_
  150.7 3.7 %galerkin.11.refs_2_ = f32[20,128,128]{2,1,0:T(8,128)S(1)} custom-call(s32[24,2]{1,0:T(8,128)S(1)} %fusion.3.slots, s32[1]{0:T(128)} %bitcast.6.first, bf16[24,128,256]{2,1,0:T(8,128)(2,1)S(1)} %get-tuple-element.45.high, bf16[24,128,256]{2,1,0:T(8,128)(2,1)S(1)} %get-tuple-element.46.low, bf16[16,256,128]{2,1,0:T(8,128)(2,1)S(1)} %get-tuple-element.47.turned, ...), custom_call_target="tpu_custom_call" | custom-call | flops 1 | bytes 1 | tf_op jit(solution)/shard_map/galerkin/pallas_call | solution.py:264
  154.4 0.0 collective-permute-done.11.refs_1_
  154.4 1.9 %collective-permute-start.15 = (f32[520,128]{1,0:T(8,128)}, f32[520,128]{1,0:T(8,128)}, u32[]{:S(2)}, u32[]{:S(2)}) collective-permute-start(f32[520,128]{1,0:T(8,128)} %collective-permute-done.11.refs_1_), channel_id=1, source_target_pairs={{0,1},{1,2},{2,3},{3,4},{4,5},{5,6},{6,7},{7,8},{8,9},{9,10},{10,1... | collective-permute-start | bytes 798728 | tf_op jit(solution)/shard_map/ppermute | solution.py:44
  156.3 4.5 %galerkin.12.refs_2_ = f32[20,128,128]{2,1,0:T(8,128)S(1)} custom-call(s32[24,2]{1,0:T(8,128)S(1)} %fusion.1.slots, s32[1]{0:T(128)} %bitcast.5.first, bf16[24,128,256]{2,1,0:T(8,128)(2,1)S(1)} %get-tuple-element.39.high, bf16[24,128,256]{2,1,0:T(8,128)(2,1)S(1)} %get-tuple-element.40.low, bf16[16,256,128]{2,1,0:T(8,128)(2,1)S(1)} %get-tuple-element.41.turned, ...), custom_call_target="tpu_custom_call" | custom-call | flops 100000000376832 | bytes 1 | tf_op jit(solution)/shard_map/galerkin/pallas_call | solution.py:264
  160.8 0.0 collective-permute-done.9.refs_0_
  160.8 3.7 %collective-permute-done.15.refs_1_ = f32[520,128]{1,0:T(8,128)} collective-permute-done((f32[520,128]{1,0:T(8,128)}, f32[520,128]{1,0:T(8,128)}, u32[]{:S(2)}, u32[]{:S(2)}) %collective-permute-start.15) | collective-permute-done | bytes 266272 | tf_op jit(solution)/shard_map/ppermute | solution.py:44
  164.5 5.5 %galerkin.13 = f32[20,128,128]{2,1,0:T(8,128)} custom-call(s32[24,2]{1,0:T(8,128)S(1)} %fusion.3.slots, s32[1]{0:T(128)} %bitcast.6.first, bf16[24,128,256]{2,1,0:T(8,128)(2,1)S(1)} %get-tuple-element.45.high, bf16[24,128,256]{2,1,0:T(8,128)(2,1)S(1)} %get-tuple-element.46.low, bf16[16,256,128]{2,1,0:T(8,128)(2,1)S(1)} %get-tuple-element.47.turned, ...), custom_call_target="tpu_custom_call" | custom-call | flops 1 | bytes 1 | tf_op jit(solution)/shard_map/galerkin/pallas_call | solution.py:264
  (14 shorter events, 0.0 us)
Async XLA Ops:
  4.5 26.4 %collective-permute-start.1 = (f32[2056,128]{1,0:T(8,128)}, f32[2056,128]{1,0:T(8,128)S(1)}, u32[]{:S(2)}, u32[]{:S(2)}) collective-permute-start(f32[2056,128]{1,0:T(8,128)} %get-tuple-element.38.refs_1_.refs_2_), channel_id=1, source_target_pairs={{1,0},{2,1},{3,2},{4,3},{5,4},{6,5},{7,6},{8,7},{9,8},{10,9},{11,1... | collective-permute-start | bytes 3158024 | tf_op jit(solution)/shard_map/ppermute | solution.py:44
  9.2 32.0 %collective-permute-start = (f32[2056,128]{1,0:T(8,128)}, f32[2056,128]{1,0:T(8,128)}, u32[]{:S(2)}, u32[]{:S(2)}) collective-permute-start(f32[2056,128]{1,0:T(8,128)} %get-tuple-element.38.refs_1_.refs_2_), channel_id=1, source_target_pairs={{0,1},{1,2},{2,3},{3,4},{4,5},{5,6},{6,7},{7,8},{8,9},{9,10},{10,1... | collective-permute-start | bytes 3158024 | tf_op jit(solution)/shard_map/ppermute | solution.py:44
  11.1 63.3 %collective-permute-start.7 = (f32[520,128]{1,0:T(8,128)}, f32[520,128]{1,0:T(8,128)}, u32[]{:S(2)}, u32[]{:S(2)}) collective-permute-start(f32[520,128]{1,0:T(8,128)} %get-tuple-element.62), channel_id=1, source_target_pairs={{0,320},{32,352},{64,384},{96,416},{128,448},{160,480},{192,0},{22... | collective-permute-start | bytes 798728 | tf_op jit(solution)/shard_map/ppermute | solution.py:38
  25.9 48.5 %collective-permute-start.3 = (f32[1032,128]{1,0:T(8,128)}, f32[1032,128]{1,0:T(8,128)}, u32[]{:S(2)}, u32[]{:S(2)}) collective-permute-start(f32[1032,128]{1,0:T(8,128)} %get-tuple-element.49), channel_id=1, source_target_pairs={{0,128},{32,160},{64,192},{96,224},{128,256},{160,288},{192,320},{... | collective-permute-start | bytes 1585160 | tf_op jit(solution)/shard_map/ppermute | solution.py:38
  30.9 18.6 %copy-start.3 = (f32[8,2]{1,0:T(8,128)}, f32[8,2]{1,0:T(8,128)S(1)}, u32[]{:S(2)}) copy-start(f32[8,2]{1,0:T(8,128)S(1)} %slice.18) | copy-start | bytes 196
  30.9 63.6 %collective-permute-start.10 = (f32[520,128]{1,0:T(8,128)}, f32[520,128]{1,0:T(8,128)}, u32[]{:S(2)}, u32[]{:S(2)}) collective-permute-start(f32[520,128]{1,0:T(8,128)} %get-tuple-element.68), channel_id=1, source_target_pairs={{0,320},{32,352},{64,384},{96,416},{128,448},{160,480},{192,0},{22... | collective-permute-start | bytes 798728 | tf_op jit(solution)/shard_map/ppermute | solution.py:38
  37.3 77.1 %collective-permute-start.6 = (f32[1032,128]{1,0:T(8,128)}, f32[1032,128]{1,0:T(8,128)}, u32[]{:S(2)}, u32[]{:S(2)}) collective-permute-start(f32[1032,128]{1,0:T(8,128)} %get-tuple-element.57), channel_id=1, source_target_pairs={{0,96},{32,128},{64,160},{96,192},{128,224},{160,256},{192,288},{2... | collective-permute-start | bytes 1585160 | tf_op jit(solution)/shard_map/ppermute | solution.py:38
  41.1 93.8 %collective-permute-start.5 = (f32[1032,128]{1,0:T(8,128)}, f32[1032,128]{1,0:T(8,128)}, u32[]{:S(2)}, u32[]{:S(2)}) collective-permute-start(f32[1032,128]{1,0:T(8,128)} %get-tuple-element.55), channel_id=1, source_target_pairs={{0,64},{32,96},{64,128},{96,160},{128,192},{160,224},{192,256},{22... | collective-permute-start | bytes 1585160 | tf_op jit(solution)/shard_map/ppermute | solution.py:38
  45.2 0.6 copy-start.5
  45.8 1.2 copy-start
  47.0 2.5 %copy-start.2 = (f32[1032,128]{1,0:T(8,128)S(1)}, f32[1032,128]{1,0:T(8,128)}, u32[]{:S(2)}) copy-start(f32[1032,128]{1,0:T(8,128)} %get-tuple-element.42.refs_0_) | copy-start | bytes 1585156
  74.4 55.8 %collective-permute-start.8 = (f32[520,128]{1,0:T(8,128)}, f32[520,128]{1,0:T(8,128)}, u32[]{:S(2)}, u32[]{:S(2)}) collective-permute-start(f32[520,128]{1,0:T(8,128)} %collective-permute-done.7), channel_id=1, source_target_pairs={{0,352},{32,384},{64,416},{96,448},{128,480},{160,0},{192,32},{224... | collective-permute-start | bytes 798728 | tf_op jit(solution)/shard_map/ppermute | solution.py:38
  86.2 18.6 %collective-permute-start.2 = (f32[2056,128]{1,0:T(8,128)}, f32[2056,128]{1,0:T(8,128)}, u32[]{:S(2)}, u32[]{:S(2)}) collective-permute-start(f32[2056,128]{1,0:T(8,128)} %collective-permute-done.refs_0_.refs_1_), channel_id=1, source_target_pairs={{0,1},{1,2},{2,3},{3,4},{4,5},{5,6},{6,7},{7,8},{8,9},{9,10},{10,1... | collective-permute-start | bytes 3158024 | tf_op jit(solution)/shard_map/ppermute | solution.py:44
  88.2 23.4 %copy-start.1 = (f32[2056,128]{1,0:T(8,128)S(1)}, f32[2056,128]{1,0:T(8,128)}, u32[]{:S(2)}) copy-start(f32[2056,128]{1,0:T(8,128)} %get-tuple-element.38.refs_1_.refs_2_) | copy-start | bytes 3158020
  89.7 24.6 %copy-start.4 = (f32[8,2]{1,0:T(8,128)S(1)}, f32[8,2]{1,0:T(8,128)}, u32[]{:S(2)}) copy-start(f32[8,2]{1,0:T(8,128)} %copy-done.3) | copy-start | bytes 196
  89.7 24.6 %copy-start.6 = (f32[8,2]{1,0:T(8,128)S(1)}, f32[8,2]{1,0:T(8,128)}, u32[]{:S(2)}) copy-start(f32[8,2]{1,0:T(8,128)} %copy-done.5) | copy-start | bytes 196
  94.5 49.6 %collective-permute-start.4 = (f32[1032,128]{1,0:T(8,128)}, f32[1032,128]{1,0:T(8,128)}, u32[]{:S(2)}, u32[]{:S(2)}) collective-permute-start(f32[1032,128]{1,0:T(8,128)} %get-tuple-element.53), channel_id=1, source_target_pairs={{0,32},{32,64},{64,96},{96,128},{128,160},{160,192},{192,224},{224... | collective-permute-start | bytes 1585160 | tf_op jit(solution)/shard_map/ppermute | solution.py:38
  104.8 49.6 %collective-permute-start.11 = (f32[520,128]{1,0:T(8,128)}, f32[520,128]{1,0:T(8,128)}, u32[]{:S(2)}, u32[]{:S(2)}) collective-permute-start(f32[520,128]{1,0:T(8,128)} %collective-permute-done.10), channel_id=1, source_target_pairs={{0,352},{32,384},{64,416},{96,448},{128,480},{160,0},{192,32},{224... | collective-permute-start | bytes 798728 | tf_op jit(solution)/shard_map/ppermute | solution.py:38
  119.8 30.9 %collective-permute-start.14 = (f32[16,128,128]{2,1,0:T(8,128)}, f32[16,128,128]{2,1,0:T(8,128)}, u32[]{:S(2)}, u32[]{:S(2)}) collective-permute-start(f32[16,128,128]{2,1,0:T(8,128)} %get-tuple-element.60), channel_id=1, source_target_pairs={{0,1},{1,2},{2,3},{3,4},{4,5},{5,6},{6,7},{7,8},{8,9},{9,10},{10,1... | collective-permute-start | bytes 3145736 | tf_op jit(solution)/shard_map/ppermute | solution.py:44
  134.9 11.2 %collective-permute-start.13 = (f32[520,128]{1,0:T(8,128)}, f32[520,128]{1,0:T(8,128)}, u32[]{:S(2)}, u32[]{:S(2)}) collective-permute-start(f32[520,128]{1,0:T(8,128)} %collective-permute-done.8.refs_1_), channel_id=1, source_target_pairs={{0,1},{1,2},{2,3},{3,4},{4,5},{5,6},{6,7},{7,8},{8,9},{9,10},{10,1... | collective-permute-start | bytes 798728 | tf_op jit(solution)/shard_map/ppermute | solution.py:44
  136.8 13.9 %collective-permute-start.12 = (f32[1032,128]{1,0:T(8,128)}, f32[1032,128]{1,0:T(8,128)}, u32[]{:S(2)}, u32[]{:S(2)}) collective-permute-start(f32[1032,128]{1,0:T(8,128)} %collective-permute-done.5.refs_0_), channel_id=1, source_target_pairs={{0,1},{1,2},{2,3},{3,4},{4,5},{5,6},{6,7},{7,8},{8,9},{9,10},{10,1... | collective-permute-start | bytes 1585160 | tf_op jit(solution)/shard_map/ppermute | solution.py:44
  144.1 16.7 %collective-permute-start.9 = (f32[1032,128]{1,0:T(8,128)}, f32[1032,128]{1,0:T(8,128)}, u32[]{:S(2)}, u32[]{:S(2)}) collective-permute-start(f32[1032,128]{1,0:T(8,128)} %collective-permute-done.4.refs_0_), channel_id=1, source_target_pairs={{0,1},{1,2},{2,3},{3,4},{4,5},{5,6},{6,7},{7,8},{8,9},{9,10},{10,1... | collective-permute-start | bytes 1585160 | tf_op jit(solution)/shard_map/ppermute | solution.py:44
  154.4 10.2 %collective-permute-start.15 = (f32[520,128]{1,0:T(8,128)}, f32[520,128]{1,0:T(8,128)}, u32[]{:S(2)}, u32[]{:S(2)}) collective-permute-start(f32[520,128]{1,0:T(8,128)} %collective-permute-done.11.refs_1_), channel_id=1, source_target_pairs={{0,1},{1,2},{2,3},{3,4},{4,5},{5,6},{6,7},{7,8},{8,9},{9,10},{10,1... | collective-permute-start | bytes 798728 | tf_op jit(solution)/shard_map/ppermute | solution.py:44

commit v6 on v5

--- a/solution.py
+++ b/solution.py
@@ -44,21 +44,34 @@
     return lax.ppermute(value, "gy", route)
 
 
-def bucket_kernel(rows, gx, per_x, layout, new_row, a_cols, p_cols, my_x, a_hbm, p_hbm, *refs):
-    p_out, outs = refs[0], refs[1 : 1 + len(BUFFERS)]
-    held, held_p, notes, order, in_sem, out_sem, note_sem, p_sem = refs[1 + len(BUFFERS) :]
+def bucket_kernel(rows, gx, per_x, layout, first, new_row, a_cols, p_cols, my_x, a_hbm, p_hbm, *refs):
+    if first:
+        p_out, refs = refs[0], refs[1:]
+    outs, refs = refs[: len(layout)], refs[len(layout) :]
+    held, held_p, notes, order, in_sem, out_sem, note_sem, p_sem = refs
     p_size = rows * P_TILES * TILE
-    p_load = pltpu.make_async_copy(p_hbm, held_p.at[pl.ds(0, p_size)], p_sem)
-    p_load.start()
+    if first:
+        p_load = pltpu.make_async_copy(p_hbm, held_p.at[pl.ds(0, p_size)], p_sem)
     loads = [pltpu.make_async_copy(a_hbm.at[o], held.at[o], in_sem.at[o]) for o in range(rows)]
-    for load in loads:
-        load.start()
     for s in range(SPAN * CAP):
         order[s] = -1
     gaps = [lax.rem(lax.div(new_row[o], per_x) - my_x[0] + gx, gx) for o in range(rows)]
     for o in range(rows):
         rank = sum([(gaps[e] == gaps[o]).astype(jnp.int32) for e in range(o)], jnp.int32(0))
         order[gaps[o] * CAP + rank] = o
+    places = [s for pieces, _ in layout for s, _, _ in pieces]
+
+    def wanted(o):
+        return sum([(order[s] == o).astype(jnp.int32) for s in places]) > 0
+
+    for o, load in enumerate(loads):
+
+        @pl.when(wanted(o))
+        def _():
+            load.start()
+
+    if first:
+        p_load.start()
     lane = lax.broadcasted_iota(jnp.int32, (META, TILE), 1)
     line = lax.broadcasted_iota(jnp.int32, (META, TILE), 0)
     note_copies = []
@@ -78,16 +91,17 @@
         copy = pltpu.make_async_copy(notes.at[b], outs[b].at[pl.ds(size, META)], note_sem.at[b])
         copy.start()
         note_copies.append(copy)
-    note = jnp.zeros((META, TILE), jnp.int32)
-    for i in range(rows):
-        for q in range(P_TILES):
-            note = jnp.where((line == i) & (lane == q), p_cols[q, i], note)
-    held_p[p_size:, :] = note.astype(jnp.float32)
-    p_load.wait()
-    p_copy = pltpu.make_async_copy(held_p, p_out, p_sem)
-    p_copy.start()
-    for load in loads:
-        load.wait()
+    if first:
+        note = jnp.zeros((META, TILE), jnp.int32)
+        for i in range(rows):
+            for q in range(P_TILES):
+                note = jnp.where((line == i) & (lane == q), p_cols[q, i], note)
+        held_p[p_size:, :] = note.astype(jnp.float32)
+    for o, load in enumerate(loads):
+
+        @pl.when(wanted(o))
+        def _():
+            load.wait()
 
     def each(act):
         n = 0
@@ -109,23 +123,28 @@
                 n += 1
 
     each(lambda copy: copy.start())
+    if first:
+        p_load.wait()
+        p_copy = pltpu.make_async_copy(held_p, p_out, p_sem)
+        p_copy.start()
     each(lambda copy: copy.wait())
     for copy in note_copies:
         copy.wait()
-    p_copy.wait()
-
-
-def buckets(a_tiles, a_cols, new_row, p_tiles, p_cols, my_x):
+    if first:
+        p_copy.wait()
+
+
+def buckets(names, a_tiles, a_cols, new_row, p_tiles, p_cols, my_x, first):
     rows = a_tiles.shape[0]
     gx, gy = lax.axis_size("gx"), lax.axis_size("gy")
-    layout = list(BUFFERS.values())
+    layout = [BUFFERS[name] for name in names]
     lengths = [sum(n for _, _, n in pieces) + META * noted for pieces, noted in layout]
     p_lines = rows * P_TILES * TILE
-    p_here, *outs = pl.pallas_call(
-        functools.partial(bucket_kernel, rows, gx, rows * gy, layout),
-        out_shape=[jax.ShapeDtypeStruct((n, TILE), jnp.float32) for n in [p_lines + META] + lengths],
+    outs = pl.pallas_call(
+        functools.partial(bucket_kernel, rows, gx, rows * gy, layout, first),
+        out_shape=[jax.ShapeDtypeStruct((n, TILE), jnp.float32) for n in [p_lines + META] * first + lengths],
         in_specs=[SMEM, SMEM, SMEM, SMEM, HBM, HBM],
-        out_specs=[HBM] * (1 + len(lengths)),
+        out_specs=[HBM] * (first + len(lengths)),
         scratch_shapes=[
             pltpu.VMEM((rows, ROW, TILE), jnp.float32),
             pltpu.VMEM((p_lines + META, TILE), jnp.float32),
@@ -139,7 +158,7 @@
         compiler_params=pltpu.CompilerParams(vmem_limit_bytes=60 * 2**20),
         name="buckets",
     )(new_row, a_cols.T, p_cols.T, my_x, a_tiles.reshape(rows, ROW, TILE), p_tiles.reshape(p_lines, TILE))
-    return p_here, dict(zip(BUFFERS, outs))
+    return dict(zip(["p"] * first + names, outs))
 
 
 def halves(x):
@@ -192,6 +211,12 @@
         copy.start()
         note_copies.append(copy)
         lines += [(n, r) for r in range(length // ROW)]
+    def fetch(m):
+        n, r = lines[m]
+        return pltpu.make_async_copy(buffers[n].at[pl.ds(r * ROW, ROW)], held.at[m], sem.at[m])
+
+    for m in range(len(lines)):
+        fetch(m).start()
     for i, acc in enumerate(accs):
         if fresh:
             acc[...] = jnp.zeros_like(acc)
@@ -207,21 +232,12 @@
     def note(n, r, k):
         return notes[n, r, k].astype(jnp.int32)
 
-    def fetch(m):
-        n, r = lines[m]
-        return pltpu.make_async_copy(buffers[n].at[pl.ds(r * ROW, ROW)], held.at[m], sem.at[m])
-
     for m, (n, r) in enumerate(lines):
+
+        fetch(m).wait()
 
         @pl.when(note(n, r, A_TILES) > 0)
         def _():
-            fetch(m).start()
-
-    for m, (n, r) in enumerate(lines):
-
-        @pl.when(note(n, r, A_TILES) > 0)
-        def _():
-            fetch(m).wait()
             row = note(n, r, A_TILES) - 1
             cols = [note(n, r, k) - first[0] for k in range(A_TILES)]
             for k, c in enumerate(cols):
@@ -302,12 +318,15 @@
     my_x = lax.axis_index("gx").astype(jnp.int32)
     device = my_x * lax.axis_size("gy") + lax.axis_index("gy").astype(jnp.int32)
 
-    p_here, send = buckets(a_tiles, a_cols, new_row, p_tiles, p_cols, my_x.reshape(1))
+    operands = (a_cols, new_row, p_tiles, p_cols, my_x.reshape(1))
+    send = buckets(["far_a", "d4"], a_tiles, *operands, True)
+    p_here = send["p"]
     p_before = beside(p_here, 1)
     p_after = beside(p_here, -1)
     sources = [p_before, p_here, p_after]
     d4 = hop(send["d4"], "gx", 4)
     far_a = hop(send["far_a"], "gx", -6)
+    send |= buckets(["far_b", "d3", "d2", "d1", "d0"], after(a_tiles, p_after), *operands, False)
     far_b = hop(after(send["far_b"], p_after), "gx", -6)
 
 

time: 172 us -> 170 us (0.988)
  waiting for transfers between devices: 58.4 us -> 53.9 us
  starting transfers between devices: 70.6 us -> 74.3 us
    ppermute x8, waiting for transfers between devices: 41.6 us -> 36.2 us  [hop(): lax.ppermute(value, axis, [(i, (i + steps) % count) for i in range(count)])]
    pallas_call x7, Pallas kernels: 27.2 us -> 23.8 us  [galerkin(): pl.pallas_call(functools.partial(galerkin_kernel, rows, shapes, targets,...]
    ppermute x8, starting transfers between devices: 52.5 us -> 55.8 us  [hop(): lax.ppermute(value, axis, [(i, (i + steps) % count) for i in range(count)])]
    pallas_call x1 -> x2, Pallas kernels: 4.51 us -> 7.01 us  [buckets(): pl.pallas_call(functools.partial(bucket_kernel, rows, gx, rows * gy, layo...]
  transfers between devices with their start and end apart: 16 -> 16, of which waited for: 8 -> 9; matrix products, arithmetic and copies ran while one was open for 1% -> 1% of each run, Pallas kernels for 16% -> 17%
where the time goes in v6:
time: 170 us; the launch traced here: 167 us
  starting transfers between devices  74.3 us (44%)
  waiting for transfers between devices  53.9 us (32%)
  Pallas kernels  36.1 us (21%)
  local copies, waits for them, and re-layouts  2.64 us (2%)
    ppermute x8, starting transfers between devices, hop(): lax.ppermute(value, axis, [(i, (i + steps) % count) for i in range(count)])  55.8 us
    ppermute x8, waiting for transfers between devices, hop(): lax.ppermute(value, axis, [(i, (i + steps) % count) for i in range(count)])  36.2 us
    pallas_call x7, Pallas kernels, galerkin(): pl.pallas_call(functools.partial(galerkin_kernel, rows, shapes, targets,...  23.8 us
    ppermute x8, starting transfers between devices, beside(): return lax.ppermute(value, 'gy', route)  18.4 us
    ppermute x8, waiting for transfers between devices, beside(): return lax.ppermute(value, 'gy', route)  17.7 us
    pallas_call x2, Pallas kernels, buckets(): pl.pallas_call(functools.partial(bucket_kernel, rows, gx, rows * gy, layo...  7.01 us
    pallas_call x2, Pallas kernels, split(): pl.pallas_call(functools.partial(split_kernel, rows), out_shape=[wide, wi...  5.28 us
  transfers between devices with their start and end apart: 16, of which 9 were waited for; matrix products, arithmetic and copies ran while one was open for 1% of the time, Pallas kernels for 17%

profile of v6, /device:TPU:6, one launch (start us, length us, event | category | flops | bytes accessed | tf_op | source)
XLA Modules:
  0.0 167.4 jit_solution(14343838891854157533)
XLA Ops:
  0.0 3.4 %buckets.2 = (f32[2056,128]{1,0:T(8,128)}, f32[520,128]{1,0:T(8,128)}, f32[1032,128]{1,0:T(8,128)}) custom-call(s32[8]{0:T(128)} %new_row.3, s32[4,8]{1,0:T(4,128)} %bitcast.15, s32[2,8]{1,0:T(2,128)} %bitcast.17, s32[1]{0:T(128)} %bitcast.2.my_x, f32[8,512,128]{2,1,0:T(8,128)} %bitcast.11, f32[2048,128]{1,0:T(8,128)} %bitcast.13), custom_call_target="tpu_custom_call" | custom-call | tf_op jit(solution)/shard_map/buckets/pallas_call | solution.py:143
  3.4 4.8 %collective-permute-start.1 = (f32[2056,128]{1,0:T(8,128)}, f32[2056,128]{1,0:T(8,128)S(1)}, u32[]{:S(2)}, u32[]{:S(2)}) collective-permute-start(f32[2056,128]{1,0:T(8,128)} %get-tuple-element.39.refs_1_.refs_2_), channel_id=1, source_target_pairs={{1,0},{2,1},{3,2},{4,3},{5,4},{6,5},{7,6},{8,7},{9,8},{10,9},{11,1... | collective-permute-start | bytes 3158024 | tf_op jit(solution)/shard_map/ppermute | solution.py:44
  8.2 1.9 %collective-permute-start = (f32[2056,128]{1,0:T(8,128)}, f32[2056,128]{1,0:T(8,128)}, u32[]{:S(2)}, u32[]{:S(2)}) collective-permute-start(f32[2056,128]{1,0:T(8,128)} %get-tuple-element.39.refs_1_.refs_2_), channel_id=1, source_target_pairs={{0,1},{1,2},{2,3},{3,4},{4,5},{5,6},{6,7},{7,8},{8,9},{9,10},{10,1... | collective-permute-start | bytes 3158024 | tf_op jit(solution)/shard_map/ppermute | solution.py:44
  10.2 14.8 %collective-permute-start.7 = (f32[520,128]{1,0:T(8,128)}, f32[520,128]{1,0:T(8,128)}, u32[]{:S(2)}, u32[]{:S(2)}) collective-permute-start(f32[520,128]{1,0:T(8,128)} %get-tuple-element.64), channel_id=1, source_target_pairs={{0,320},{32,352},{64,384},{96,416},{128,448},{160,480},{192,0},{22... | collective-permute-start | bytes 798728 | tf_op jit(solution)/shard_map/ppermute | solution.py:38
  25.0 4.1 %collective-permute-start.3 = (f32[1032,128]{1,0:T(8,128)}, f32[1032,128]{1,0:T(8,128)}, u32[]{:S(2)}, u32[]{:S(2)}) collective-permute-start(f32[1032,128]{1,0:T(8,128)} %get-tuple-element.51), channel_id=1, source_target_pairs={{0,128},{32,160},{64,192},{96,224},{128,256},{160,288},{192,320},{... | collective-permute-start | bytes 1585160 | tf_op jit(solution)/shard_map/ppermute | solution.py:38
  29.1 0.7 slice.18
  29.8 0.0 collective-permute-done.1.refs_2_
  29.8 3.6 %buckets.3 = (f32[520,128]{1,0:T(8,128)}, f32[1032,128]{1,0:T(8,128)}, f32[1032,128]{1,0:T(8,128)}, f32[1032,128]{1,0:T(8,128)}, f32[1032,128]{1,0:T(8,128)}) custom-call(s32[8]{0:T(128)} %new_row.3, s32[4,8]{1,0:T(4,128)} %bitcast.16, s32[2,8]{1,0:T(2,128)} %bitcast.18, s32[1]{0:T(128)} %bitcast.2.my_x, f32[8,512,128]{2,1,0:T(8,128)} %bitcast.12, ...), custom_call_target="tpu_custom_call" | custom-call | tf_op jit(solution)/shard_map/buckets/pallas_call | solution.py:143
  33.4 0.0 collective-permute-done.refs_0_.refs_1_
  33.4 8.2 %collective-permute-start.10 = (f32[520,128]{1,0:T(8,128)}, f32[520,128]{1,0:T(8,128)}, u32[]{:S(2)}, u32[]{:S(2)}) collective-permute-start(f32[520,128]{1,0:T(8,128)} %get-tuple-element.70), channel_id=1, source_target_pairs={{0,320},{32,352},{64,384},{96,416},{128,448},{160,480},{192,0},{22... | collective-permute-start | bytes 798728 | tf_op jit(solution)/shard_map/ppermute | solution.py:38
  41.7 2.6 %collective-permute-start.6 = (f32[1032,128]{1,0:T(8,128)}, f32[1032,128]{1,0:T(8,128)}, u32[]{:S(2)}, u32[]{:S(2)}) collective-permute-start(f32[1032,128]{1,0:T(8,128)} %get-tuple-element.59), channel_id=1, source_target_pairs={{0,96},{32,128},{64,160},{96,192},{128,224},{160,256},{192,288},{2... | collective-permute-start | bytes 1585160 | tf_op jit(solution)/shard_map/ppermute | solution.py:38
  44.3 4.6 %collective-permute-start.5 = (f32[1032,128]{1,0:T(8,128)}, f32[1032,128]{1,0:T(8,128)}, u32[]{:S(2)}, u32[]{:S(2)}) collective-permute-start(f32[1032,128]{1,0:T(8,128)} %get-tuple-element.57), channel_id=1, source_target_pairs={{0,64},{32,96},{64,128},{96,160},{128,192},{160,224},{192,256},{22... | collective-permute-start | bytes 1585160 | tf_op jit(solution)/shard_map/ppermute | solution.py:38
  48.9 0.7 slice.22
  49.6 0.6 copy-done.4
  50.2 0.0 copy-done
  50.2 2.5 %split.2 = (bf16[24,128,256]{2,1,0:T(8,128)(2,1)S(1)}, bf16[24,128,256]{2,1,0:T(8,128)(2,1)S(1)}, bf16[16,256,128]{2,1,0:T(8,128)(2,1)S(1)}) custom-call(f32[2056,128]{1,0:T(8,128)} %collective-permute-done.refs_0_.refs_1_, f32[2056,128]{1,0:T(8,128)S(1)} %copy-done, f32[2056,128]{1,0:T(8,128)S(1)} %collective-permute-done.1.refs_2_), custom_call_target="tpu_custom_call" | custom-call | tf_op jit(solution)/shard_map/split/pallas_call | solution.py:190
  52.7 3.4 %galerkin.7 = (f32[20,128,128]{2,1,0:T(8,128)S(1)}, f32[16,128,128]{2,1,0:T(8,128)S(1)}) custom-call(s32[24,2]{1,0:T(8,128)S(1)} %fusion.1.slots, s32[1]{0:T(128)} %bitcast.5.first, bf16[24,128,256]{2,1,0:T(8,128)(2,1)S(1)} %get-tuple-element.40.high, bf16[24,128,256]{2,1,0:T(8,128)(2,1)S(1)} %get-tuple-element.41.low, ...), custom_call_target="tpu_custom_call" | custom-call | flops 100000000376832 | bytes 1 | tf_op jit(solution)/shard_map/galerkin/pallas_call | solution.py:280
  56.1 14.9 %collective-permute-done.7 = f32[520,128]{1,0:T(8,128)} collective-permute-done((f32[520,128]{1,0:T(8,128)}, f32[520,128]{1,0:T(8,128)}, u32[]{:S(2)}, u32[]{:S(2)}) %collective-permute-start.7) | collective-permute-done | bytes 266272 | tf_op jit(solution)/shard_map/ppermute | solution.py:38
  71.0 2.0 %collective-permute-done.3.refs_0_ = f32[1032,128]{1,0:T(8,128)} collective-permute-done((f32[1032,128]{1,0:T(8,128)}, f32[1032,128]{1,0:T(8,128)}, u32[]{:S(2)}, u32[]{:S(2)}) %collective-permute-start.3) | collective-permute-done | bytes 528416 | tf_op jit(solution)/shard_map/ppermute | solution.py:38
  72.9 11.3 %collective-permute-start.8 = (f32[520,128]{1,0:T(8,128)}, f32[520,128]{1,0:T(8,128)}, u32[]{:S(2)}, u32[]{:S(2)}) collective-permute-start(f32[520,128]{1,0:T(8,128)} %collective-permute-done.7), channel_id=1, source_target_pairs={{0,352},{32,384},{64,416},{96,448},{128,480},{160,0},{192,32},{224... | collective-permute-start | bytes 798728 | tf_op jit(solution)/shard_map/ppermute | solution.py:38
  84.3 1.9 %collective-permute-start.2 = (f32[2056,128]{1,0:T(8,128)}, f32[2056,128]{1,0:T(8,128)}, u32[]{:S(2)}, u32[]{:S(2)}) collective-permute-start(f32[2056,128]{1,0:T(8,128)} %collective-permute-done.refs_0_.refs_1_), channel_id=1, source_target_pairs={{0,1},{1,2},{2,3},{3,4},{4,5},{5,6},{6,7},{7,8},{8,9},{9,10},{10,1... | collective-permute-start | bytes 3158024 | tf_op jit(solution)/shard_map/ppermute | solution.py:44
  86.2 3.7 %galerkin.8 = (f32[20,128,128]{2,1,0:T(8,128)S(1)}, f32[16,128,128]{2,1,0:T(8,128)S(1)}) custom-call(s32[24,2]{1,0:T(8,128)S(1)} %fusion.1.slots, s32[1]{0:T(128)} %bitcast.5.first, bf16[24,128,256]{2,1,0:T(8,128)(2,1)S(1)} %get-tuple-element.40.high, bf16[24,128,256]{2,1,0:T(8,128)(2,1)S(1)} %get-tuple-element.41.low, ...), custom_call_target="tpu_custom_call" | custom-call | flops 100000000376832 | bytes 1 | tf_op jit(solution)/shard_map/galerkin/pallas_call | solution.py:280
  89.9 1.8 %collective-permute-done.10 = f32[520,128]{1,0:T(8,128)} collective-permute-done((f32[520,128]{1,0:T(8,128)}, f32[520,128]{1,0:T(8,128)}, u32[]{:S(2)}, u32[]{:S(2)}) %collective-permute-start.10) | collective-permute-done | bytes 266272 | tf_op jit(solution)/shard_map/ppermute | solution.py:38
  91.7 2.2 %collective-permute-start.4 = (f32[1032,128]{1,0:T(8,128)}, f32[1032,128]{1,0:T(8,128)}, u32[]{:S(2)}, u32[]{:S(2)}) collective-permute-start(f32[1032,128]{1,0:T(8,128)} %get-tuple-element.55), channel_id=1, source_target_pairs={{0,32},{32,64},{64,96},{96,128},{128,160},{160,192},{192,224},{224... | collective-permute-start | bytes 1585160 | tf_op jit(solution)/shard_map/ppermute | solution.py:38
  93.9 9.0 %collective-permute-done.2.refs_0_ = f32[2056,128]{1,0:T(8,128)} collective-permute-done((f32[2056,128]{1,0:T(8,128)}, f32[2056,128]{1,0:T(8,128)}, u32[]{:S(2)}, u32[]{:S(2)}) %collective-permute-start.2) | collective-permute-done | bytes 1052704 | tf_op jit(solution)/shard_map/ppermute | solution.py:44
  102.9 8.0 %collective-permute-start.11 = (f32[520,128]{1,0:T(8,128)}, f32[520,128]{1,0:T(8,128)}, u32[]{:S(2)}, u32[]{:S(2)}) collective-permute-start(f32[520,128]{1,0:T(8,128)} %collective-permute-done.10), channel_id=1, source_target_pairs={{0,352},{32,384},{64,416},{96,448},{128,480},{160,0},{192,32},{224... | collective-permute-start | bytes 798728 | tf_op jit(solution)/shard_map/ppermute | solution.py:38
  110.8 0.7 slice.24
  111.5 2.8 %split.3 = (bf16[24,128,256]{2,1,0:T(8,128)(2,1)S(1)}, bf16[24,128,256]{2,1,0:T(8,128)(2,1)S(1)}, bf16[16,256,128]{2,1,0:T(8,128)(2,1)S(1)}) custom-call(f32[2056,128]{1,0:T(8,128)} %collective-permute-done.2.refs_0_, f32[2056,128]{1,0:T(8,128)} %collective-permute-done.refs_0_.refs_1_, f32[2056,128]{1,0:T(8,128)S(1)} %copy-done), custom_call_target="tpu_custom_call" | custom-call | tf_op jit(solution)/shard_map/split/pallas_call | solution.py:190
  114.3 0.0 collective-permute-done.6.refs_0_
  114.3 2.8 %galerkin.9 = (f32[20,128,128]{2,1,0:T(8,128)S(1)}, f32[16,128,128]{2,1,0:T(8,128)}) custom-call(s32[24,2]{1,0:T(8,128)S(1)} %fusion.1.slots, s32[1]{0:T(128)} %bitcast.5.first, bf16[24,128,256]{2,1,0:T(8,128)(2,1)S(1)} %get-tuple-element.40.high, bf16[24,128,256]{2,1,0:T(8,128)(2,1)S(1)} %get-tuple-element.41.low, ...), custom_call_target="tpu_custom_call" | custom-call | flops 100000000376832 | bytes 1 | tf_op jit(solution)/shard_map/galerkin/pallas_call | solution.py:280
  117.1 1.9 %collective-permute-start.14 = (f32[16,128,128]{2,1,0:T(8,128)}, f32[16,128,128]{2,1,0:T(8,128)}, u32[]{:S(2)}, u32[]{:S(2)}) collective-permute-start(f32[16,128,128]{2,1,0:T(8,128)} %get-tuple-element.62), channel_id=1, source_target_pairs={{0,1},{1,2},{2,3},{3,4},{4,5},{5,6},{6,7},{7,8},{8,9},{9,10},{10,1... | collective-permute-start | bytes 3145736 | tf_op jit(solution)/shard_map/ppermute | solution.py:44
  119.0 11.4 %collective-permute-done.8.refs_1_ = f32[520,128]{1,0:T(8,128)} collective-permute-done((f32[520,128]{1,0:T(8,128)}, f32[520,128]{1,0:T(8,128)}, u32[]{:S(2)}, u32[]{:S(2)}) %collective-permute-start.8) | collective-permute-done | bytes 266272 | tf_op jit(solution)/shard_map/ppermute | solution.py:38
  130.5 3.0 %collective-permute-done.5.refs_0_ = f32[1032,128]{1,0:T(8,128)} collective-permute-done((f32[1032,128]{1,0:T(8,128)}, f32[1032,128]{1,0:T(8,128)}, u32[]{:S(2)}, u32[]{:S(2)}) %collective-permute-start.5) | collective-permute-done | bytes 528416 | tf_op jit(solution)/shard_map/ppermute | solution.py:38
  133.5 1.9 %collective-permute-start.13 = (f32[520,128]{1,0:T(8,128)}, f32[520,128]{1,0:T(8,128)}, u32[]{:S(2)}, u32[]{:S(2)}) collective-permute-start(f32[520,128]{1,0:T(8,128)} %collective-permute-done.8.refs_1_), channel_id=1, source_target_pairs={{0,1},{1,2},{2,3},{3,4},{4,5},{5,6},{6,7},{7,8},{8,9},{9,10},{10,1... | collective-permute-start | bytes 798728 | tf_op jit(solution)/shard_map/ppermute | solution.py:44
  135.4 1.9 %collective-permute-start.12 = (f32[1032,128]{1,0:T(8,128)}, f32[1032,128]{1,0:T(8,128)}, u32[]{:S(2)}, u32[]{:S(2)}) collective-permute-start(f32[1032,128]{1,0:T(8,128)} %collective-permute-done.5.refs_0_), channel_id=1, source_target_pairs={{0,1},{1,2},{2,3},{3,4},{4,5},{5,6},{6,7},{7,8},{8,9},{9,10},{10,1... | collective-permute-start | bytes 1585160 | tf_op jit(solution)/shard_map/ppermute | solution.py:44
  137.3 2.5 %galerkin.10.refs_2_ = f32[20,128,128]{2,1,0:T(8,128)S(1)} custom-call(s32[24,2]{1,0:T(8,128)S(1)} %fusion.1.slots, s32[1]{0:T(128)} %bitcast.5.first, bf16[24,128,256]{2,1,0:T(8,128)(2,1)S(1)} %get-tuple-element.40.high, bf16[24,128,256]{2,1,0:T(8,128)(2,1)S(1)} %get-tuple-element.41.low, bf16[16,256,128]{2,1,0:T(8,128)(2,1)S(1)} %get-tuple-element.42.turned, ...), custom_call_target="tpu_custom_call" | custom-call | flops 100000000376832 | bytes 1 | tf_op jit(solution)/shard_map/galerkin/pallas_call | solution.py:280
  139.9 3.2 %collective-permute-done.4.refs_0_ = f32[1032,128]{1,0:T(8,128)} collective-permute-done((f32[1032,128]{1,0:T(8,128)}, f32[1032,128]{1,0:T(8,128)}, u32[]{:S(2)}, u32[]{:S(2)}) %collective-permute-start.4) | collective-permute-done | bytes 528416 | tf_op jit(solution)/shard_map/ppermute | solution.py:38
  143.0 2.1 %collective-permute-start.9 = (f32[1032,128]{1,0:T(8,128)}, f32[1032,128]{1,0:T(8,128)}, u32[]{:S(2)}, u32[]{:S(2)}) collective-permute-start(f32[1032,128]{1,0:T(8,128)} %collective-permute-done.4.refs_0_), channel_id=1, source_target_pairs={{0,1},{1,2},{2,3},{3,4},{4,5},{5,6},{6,7},{7,8},{8,9},{9,10},{10,1... | collective-permute-start | bytes 1585160 | tf_op jit(solution)/shard_map/ppermute | solution.py:44
  145.1 0.0 collective-permute-done.13.refs_1_
  145.2 4.1 %collective-permute-done.12.refs_0_ = f32[1032,128]{1,0:T(8,128)} collective-permute-done((f32[1032,128]{1,0:T(8,128)}, f32[1032,128]{1,0:T(8,128)}, u32[]{:S(2)}, u32[]{:S(2)}) %collective-permute-start.12) | collective-permute-done | bytes 528416 | tf_op jit(solution)/shard_map/ppermute | solution.py:44
  149.3 0.0 collective-permute-done.14.refs_3_
  149.3 4.2 %galerkin.11.refs_2_ = f32[20,128,128]{2,1,0:T(8,128)S(1)} custom-call(s32[24,2]{1,0:T(8,128)S(1)} %fusion.3.slots, s32[1]{0:T(128)} %bitcast.7.first, bf16[24,128,256]{2,1,0:T(8,128)(2,1)S(1)} %get-tuple-element.47.high, bf16[24,128,256]{2,1,0:T(8,128)(2,1)S(1)} %get-tuple-element.48.low, bf16[16,256,128]{2,1,0:T(8,128)(2,1)S(1)} %get-tuple-element.49.turned, ...), custom_call_target="tpu_custom_call" | custom-call | flops 1 | bytes 1 | tf_op jit(solution)/shard_map/galerkin/pallas_call | solution.py:280
  153.5 0.0 collective-permute-done.11.refs_1_
  153.5 1.9 %collective-permute-start.15 = (f32[520,128]{1,0:T(8,128)}, f32[520,128]{1,0:T(8,128)}, u32[]{:S(2)}, u32[]{:S(2)}) collective-permute-start(f32[520,128]{1,0:T(8,128)} %collective-permute-done.11.refs_1_), channel_id=1, source_target_pairs={{0,1},{1,2},{2,3},{3,4},{4,5},{5,6},{6,7},{7,8},{8,9},{9,10},{10,1... | collective-permute-start | bytes 798728 | tf_op jit(solution)/shard_map/ppermute | solution.py:44
  155.4 3.7 %galerkin.12.refs_2_ = f32[20,128,128]{2,1,0:T(8,128)S(1)} custom-call(s32[24,2]{1,0:T(8,128)S(1)} %fusion.1.slots, s32[1]{0:T(128)} %bitcast.5.first, bf16[24,128,256]{2,1,0:T(8,128)(2,1)S(1)} %get-tuple-element.40.high, bf16[24,128,256]{2,1,0:T(8,128)(2,1)S(1)} %get-tuple-element.41.low, bf16[16,256,128]{2,1,0:T(8,128)(2,1)S(1)} %get-tuple-element.42.turned, ...), custom_call_target="tpu_custom_call" | custom-call | flops 100000000376832 | bytes 1 | tf_op jit(solution)/shard_map/galerkin/pallas_call | solution.py:280
  159.1 0.0 collective-permute-done.9.refs_0_
  159.2 4.5 %collective-permute-done.15.refs_1_ = f32[520,128]{1,0:T(8,128)} collective-permute-done((f32[520,128]{1,0:T(8,128)}, f32[520,128]{1,0:T(8,128)}, u32[]{:S(2)}, u32[]{:S(2)}) %collective-permute-start.15) | collective-permute-done | bytes 266272 | tf_op jit(solution)/shard_map/ppermute | solution.py:44
  163.7 3.6 %galerkin.13 = f32[20,128,128]{2,1,0:T(8,128)} custom-call(s32[24,2]{1,0:T(8,128)S(1)} %fusion.3.slots, s32[1]{0:T(128)} %bitcast.7.first, bf16[24,128,256]{2,1,0:T(8,128)(2,1)S(1)} %get-tuple-element.47.high, bf16[24,128,256]{2,1,0:T(8,128)(2,1)S(1)} %get-tuple-element.48.low, bf16[16,256,128]{2,1,0:T(8,128)(2,1)S(1)} %get-tuple-element.49.turned, ...), custom_call_target="tpu_custom_call" | custom-call | flops 1 | bytes 1 | tf_op jit(solution)/shard_map/galerkin/pallas_call | solution.py:280
  (13 shorter events, 0.0 us)
Async XLA Ops:
  3.4 26.4 %collective-permute-start.1 = (f32[2056,128]{1,0:T(8,128)}, f32[2056,128]{1,0:T(8,128)S(1)}, u32[]{:S(2)}, u32[]{:S(2)}) collective-permute-start(f32[2056,128]{1,0:T(8,128)} %get-tuple-element.39.refs_1_.refs_2_), channel_id=1, source_target_pairs={{1,0},{2,1},{3,2},{4,3},{5,4},{6,5},{7,6},{8,7},{9,8},{10,9},{11,1... | collective-permute-start | bytes 3158024 | tf_op jit(solution)/shard_map/ppermute | solution.py:44
  8.2 25.2 %collective-permute-start = (f32[2056,128]{1,0:T(8,128)}, f32[2056,128]{1,0:T(8,128)}, u32[]{:S(2)}, u32[]{:S(2)}) collective-permute-start(f32[2056,128]{1,0:T(8,128)} %get-tuple-element.39.refs_1_.refs_2_), channel_id=1, source_target_pairs={{0,1},{1,2},{2,3},{3,4},{4,5},{5,6},{6,7},{7,8},{8,9},{9,10},{10,1... | collective-permute-start | bytes 3158024 | tf_op jit(solution)/shard_map/ppermute | solution.py:44
  10.2 60.8 %collective-permute-start.7 = (f32[520,128]{1,0:T(8,128)}, f32[520,128]{1,0:T(8,128)}, u32[]{:S(2)}, u32[]{:S(2)}) collective-permute-start(f32[520,128]{1,0:T(8,128)} %get-tuple-element.64), channel_id=1, source_target_pairs={{0,320},{32,352},{64,384},{96,416},{128,448},{160,480},{192,0},{22... | collective-permute-start | bytes 798728 | tf_op jit(solution)/shard_map/ppermute | solution.py:38
  25.0 47.9 %collective-permute-start.3 = (f32[1032,128]{1,0:T(8,128)}, f32[1032,128]{1,0:T(8,128)}, u32[]{:S(2)}, u32[]{:S(2)}) collective-permute-start(f32[1032,128]{1,0:T(8,128)} %get-tuple-element.51), channel_id=1, source_target_pairs={{0,128},{32,160},{64,192},{96,224},{128,256},{160,288},{192,320},{... | collective-permute-start | bytes 1585160 | tf_op jit(solution)/shard_map/ppermute | solution.py:38
  29.8 19.8 %copy-start.2 = (f32[8,2]{1,0:T(8,128)}, f32[8,2]{1,0:T(8,128)S(1)}, u32[]{:S(2)}) copy-start(f32[8,2]{1,0:T(8,128)S(1)} %slice.18) | copy-start | bytes 196
  29.8 20.4 %copy-start = (f32[2056,128]{1,0:T(8,128)S(1)}, f32[2056,128]{1,0:T(8,128)}, u32[]{:S(2)}) copy-start(f32[2056,128]{1,0:T(8,128)} %get-tuple-element.39.refs_1_.refs_2_) | copy-start | bytes 3158020
  33.4 58.2 %collective-permute-start.10 = (f32[520,128]{1,0:T(8,128)}, f32[520,128]{1,0:T(8,128)}, u32[]{:S(2)}, u32[]{:S(2)}) collective-permute-start(f32[520,128]{1,0:T(8,128)} %get-tuple-element.70), channel_id=1, source_target_pairs={{0,320},{32,352},{64,384},{96,416},{128,448},{160,480},{192,0},{22... | collective-permute-start | bytes 798728 | tf_op jit(solution)/shard_map/ppermute | solution.py:38
  41.7 72.7 %collective-permute-start.6 = (f32[1032,128]{1,0:T(8,128)}, f32[1032,128]{1,0:T(8,128)}, u32[]{:S(2)}, u32[]{:S(2)}) collective-permute-start(f32[1032,128]{1,0:T(8,128)} %get-tuple-element.59), channel_id=1, source_target_pairs={{0,96},{32,128},{64,160},{96,192},{128,224},{160,256},{192,288},{2... | collective-permute-start | bytes 1585160 | tf_op jit(solution)/shard_map/ppermute | solution.py:38
  44.3 89.2 %collective-permute-start.5 = (f32[1032,128]{1,0:T(8,128)}, f32[1032,128]{1,0:T(8,128)}, u32[]{:S(2)}, u32[]{:S(2)}) collective-permute-start(f32[1032,128]{1,0:T(8,128)} %get-tuple-element.57), channel_id=1, source_target_pairs={{0,64},{32,96},{64,128},{96,160},{128,192},{160,224},{192,256},{22... | collective-permute-start | bytes 1585160 | tf_op jit(solution)/shard_map/ppermute | solution.py:38
  49.6 0.6 copy-start.4
  50.2 2.5 %copy-start.1 = (f32[1032,128]{1,0:T(8,128)S(1)}, f32[1032,128]{1,0:T(8,128)}, u32[]{:S(2)}) copy-start(f32[1032,128]{1,0:T(8,128)} %get-tuple-element.44.refs_0_) | copy-start | bytes 1585156
  72.9 57.5 %collective-permute-start.8 = (f32[520,128]{1,0:T(8,128)}, f32[520,128]{1,0:T(8,128)}, u32[]{:S(2)}, u32[]{:S(2)}) collective-permute-start(f32[520,128]{1,0:T(8,128)} %collective-permute-done.7), channel_id=1, source_target_pairs={{0,352},{32,384},{64,416},{96,448},{128,480},{160,0},{192,32},{224... | collective-permute-start | bytes 798728 | tf_op jit(solution)/shard_map/ppermute | solution.py:38
  84.3 18.6 %collective-permute-start.2 = (f32[2056,128]{1,0:T(8,128)}, f32[2056,128]{1,0:T(8,128)}, u32[]{:S(2)}, u32[]{:S(2)}) collective-permute-start(f32[2056,128]{1,0:T(8,128)} %collective-permute-done.refs_0_.refs_1_), channel_id=1, source_target_pairs={{0,1},{1,2},{2,3},{3,4},{4,5},{5,6},{6,7},{7,8},{8,9},{9,10},{10,1... | collective-permute-start | bytes 3158024 | tf_op jit(solution)/shard_map/ppermute | solution.py:44
  89.9 24.4 %copy-start.3 = (f32[8,2]{1,0:T(8,128)S(1)}, f32[8,2]{1,0:T(8,128)}, u32[]{:S(2)}) copy-start(f32[8,2]{1,0:T(8,128)} %copy-done.2) | copy-start | bytes 196
  89.9 24.4 %copy-start.5 = (f32[8,2]{1,0:T(8,128)S(1)}, f32[8,2]{1,0:T(8,128)}, u32[]{:S(2)}) copy-start(f32[8,2]{1,0:T(8,128)} %copy-done.4) | copy-start | bytes 196
  91.7 51.4 %collective-permute-start.4 = (f32[1032,128]{1,0:T(8,128)}, f32[1032,128]{1,0:T(8,128)}, u32[]{:S(2)}, u32[]{:S(2)}) collective-permute-start(f32[1032,128]{1,0:T(8,128)} %get-tuple-element.55), channel_id=1, source_target_pairs={{0,32},{32,64},{64,96},{96,128},{128,160},{160,192},{192,224},{224... | collective-permute-start | bytes 1585160 | tf_op jit(solution)/shard_map/ppermute | solution.py:38
  102.9 50.6 %collective-permute-start.11 = (f32[520,128]{1,0:T(8,128)}, f32[520,128]{1,0:T(8,128)}, u32[]{:S(2)}, u32[]{:S(2)}) collective-permute-start(f32[520,128]{1,0:T(8,128)} %collective-permute-done.10), channel_id=1, source_target_pairs={{0,352},{32,384},{64,416},{96,448},{128,480},{160,0},{192,32},{224... | collective-permute-start | bytes 798728 | tf_op jit(solution)/shard_map/ppermute | solution.py:38
  117.1 32.2 %collective-permute-start.14 = (f32[16,128,128]{2,1,0:T(8,128)}, f32[16,128,128]{2,1,0:T(8,128)}, u32[]{:S(2)}, u32[]{:S(2)}) collective-permute-start(f32[16,128,128]{2,1,0:T(8,128)} %get-tuple-element.62), channel_id=1, source_target_pairs={{0,1},{1,2},{2,3},{3,4},{4,5},{5,6},{6,7},{7,8},{8,9},{9,10},{10,1... | collective-permute-start | bytes 3145736 | tf_op jit(solution)/shard_map/ppermute | solution.py:44
  133.5 11.7 %collective-permute-start.13 = (f32[520,128]{1,0:T(8,128)}, f32[520,128]{1,0:T(8,128)}, u32[]{:S(2)}, u32[]{:S(2)}) collective-permute-start(f32[520,128]{1,0:T(8,128)} %collective-permute-done.8.refs_1_), channel_id=1, source_target_pairs={{0,1},{1,2},{2,3},{3,4},{4,5},{5,6},{6,7},{7,8},{8,9},{9,10},{10,1... | collective-permute-start | bytes 798728 | tf_op jit(solution)/shard_map/ppermute | solution.py:44
  135.4 13.9 %collective-permute-start.12 = (f32[1032,128]{1,0:T(8,128)}, f32[1032,128]{1,0:T(8,128)}, u32[]{:S(2)}, u32[]{:S(2)}) collective-permute-start(f32[1032,128]{1,0:T(8,128)} %collective-permute-done.5.refs_0_), channel_id=1, source_target_pairs={{0,1},{1,2},{2,3},{3,4},{4,5},{5,6},{6,7},{7,8},{8,9},{9,10},{10,1... | collective-permute-start | bytes 1585160 | tf_op jit(solution)/shard_map/ppermute | solution.py:44
  143.0 16.1 %collective-permute-start.9 = (f32[1032,128]{1,0:T(8,128)}, f32[1032,128]{1,0:T(8,128)}, u32[]{:S(2)}, u32[]{:S(2)}) collective-permute-start(f32[1032,128]{1,0:T(8,128)} %collective-permute-done.4.refs_0_), channel_id=1, source_target_pairs={{0,1},{1,2},{2,3},{3,4},{4,5},{5,6},{6,7},{7,8},{8,9},{9,10},{10,1... | collective-permute-start | bytes 1585160 | tf_op jit(solution)/shard_map/ppermute | solution.py:44
  153.5 10.2 %collective-permute-start.15 = (f32[520,128]{1,0:T(8,128)}, f32[520,128]{1,0:T(8,128)}, u32[]{:S(2)}, u32[]{:S(2)}) collective-permute-start(f32[520,128]{1,0:T(8,128)} %collective-permute-done.11.refs_1_), channel_id=1, source_target_pairs={{0,1},{1,2},{2,3},{3,4},{4,5},{5,6},{6,7},{7,8},{8,9},{9,10},{10,1... | collective-permute-start | bytes 798728 | tf_op jit(solution)/shard_map/ppermute | solution.py:44

commit v7 on v6

--- a/solution.py
+++ b/solution.py
@@ -360,10 +360,12 @@
     f2 = beside(d2, 1)
     (own,) = add(mine, (0,), [d2, far_a], [own], 10**14)
     mid = own
-    (own,) = add(theirs, (0,), [f2, f_far_a], [own], arrived=on)
-    f_far_b = beside(after(far_b, own), 1)
+    token = pause(mid[0, :META])
+    far_b = after(far_b, token)
+    (own,) = add(theirs, (0,), [after(f2, token), f_far_a], [own], arrived=on)
     f1 = beside(after(d1, mid), 1)
-    (own,) = add(mine, (0,), [d1, far_b], [own], 10**14)
+    f_far_b = beside(far_b, 1)
+    (own,) = add(mine, (0,), [d1, far_b], [own])
     (own,) = add(theirs, (0,), [f1, f_far_b], [own])
     return own.reshape(coarse_rows, SLOTS, TILE, TILE)
 

time: 170 us -> 170 us (level)
  the two profiles are of different devices: /device:TPU:6 before, /device:TPU:1 now
where the time goes in v7:
time: 170 us; the launch traced here: 169 us
  starting transfers between devices  82.9 us (49%)
  waiting for transfers between devices  41.5 us (24%)
  Pallas kernels  36.9 us (22%)
  local copies, waits for them, and re-layouts  6.71 us (4%)
    ppermute x8, starting transfers between devices, hop(): lax.ppermute(value, axis, [(i, (i + steps) % count) for i in range(count)])  46.1 us
    ppermute x8, starting transfers between devices, beside(): return lax.ppermute(value, 'gy', route)  36.8 us
    ppermute x8, waiting for transfers between devices, hop(): lax.ppermute(value, axis, [(i, (i + steps) % count) for i in range(count)])  34.1 us
    pallas_call x7, Pallas kernels, galerkin(): pl.pallas_call(functools.partial(galerkin_kernel, rows, shapes, targets,...  24.3 us
    ppermute x8, waiting for transfers between devices, beside(): return lax.ppermute(value, 'gy', route)  7.41 us
    pallas_call x2, Pallas kernels, buckets(): pl.pallas_call(functools.partial(bucket_kernel, rows, gx, rows * gy, layo...  7.27 us
    pallas_call x2, Pallas kernels, split(): pl.pallas_call(functools.partial(split_kernel, rows), out_shape=[wide, wi...  5.28 us
    unnamed x36, local copies, waits for them, and re-layouts  4.64 us
  transfers between devices with their start and end apart: 16, of which 4 were waited for; matrix products, arithmetic and copies ran while one was open for 1% of the time, Pallas kernels for 18%

profile of v7, /device:TPU:1, one launch (start us, length us, event | category | flops | bytes accessed | tf_op | source)
XLA Modules:
  0.0 168.6 jit_solution(11932571419824635553)
XLA Ops:
  0.0 3.3 %buckets.2 = (f32[2056,128]{1,0:T(8,128)}, f32[520,128]{1,0:T(8,128)}, f32[1032,128]{1,0:T(8,128)}) custom-call(s32[8]{0:T(128)} %new_row.3, s32[4,8]{1,0:T(4,128)} %bitcast.17, s32[2,8]{1,0:T(2,128)} %bitcast.19, s32[1]{0:T(128)} %bitcast.2.my_x, f32[8,512,128]{2,1,0:T(8,128)} %bitcast.13, f32[2048,128]{1,0:T(8,128)} %bitcast.15), custom_call_target="tpu_custom_call" | custom-call | tf_op jit(solution)/shard_map/buckets/pallas_call | solution.py:143
  3.3 8.9 %collective-permute-start.1 = (f32[2056,128]{1,0:T(8,128)}, f32[2056,128]{1,0:T(8,128)S(1)}, u32[]{:S(2)}, u32[]{:S(2)}) collective-permute-start(f32[2056,128]{1,0:T(8,128)} %get-tuple-element.40.refs_1_.refs_2_), channel_id=1, source_target_pairs={{1,0},{2,1},{3,2},{4,3},{5,4},{6,5},{7,6},{8,7},{9,8},{10,9},{11,1... | collective-permute-start | bytes 3158024 | tf_op jit(solution)/shard_map/ppermute | solution.py:44
  12.2 1.9 %collective-permute-start = (f32[2056,128]{1,0:T(8,128)}, f32[2056,128]{1,0:T(8,128)}, u32[]{:S(2)}, u32[]{:S(2)}) collective-permute-start(f32[2056,128]{1,0:T(8,128)} %get-tuple-element.40.refs_1_.refs_2_), channel_id=1, source_target_pairs={{0,1},{1,2},{2,3},{3,4},{4,5},{5,6},{6,7},{7,8},{8,9},{9,10},{10,1... | collective-permute-start | bytes 3158024 | tf_op jit(solution)/shard_map/ppermute | solution.py:44
  14.1 10.4 %collective-permute-start.7 = (f32[520,128]{1,0:T(8,128)}, f32[520,128]{1,0:T(8,128)}, u32[]{:S(2)}, u32[]{:S(2)}) collective-permute-start(f32[520,128]{1,0:T(8,128)} %get-tuple-element.65), channel_id=1, source_target_pairs={{0,320},{32,352},{64,384},{96,416},{128,448},{160,480},{192,0},{22... | collective-permute-start | bytes 798728 | tf_op jit(solution)/shard_map/ppermute | solution.py:38
  24.5 4.2 %collective-permute-start.3 = (f32[1032,128]{1,0:T(8,128)}, f32[1032,128]{1,0:T(8,128)}, u32[]{:S(2)}, u32[]{:S(2)}) collective-permute-start(f32[1032,128]{1,0:T(8,128)} %get-tuple-element.52), channel_id=1, source_target_pairs={{0,128},{32,160},{64,192},{96,224},{128,256},{160,288},{192,320},{... | collective-permute-start | bytes 1585160 | tf_op jit(solution)/shard_map/ppermute | solution.py:38
  28.7 0.7 slice.21
  29.4 0.0 collective-permute-done.1.refs_2_
  29.4 4.0 %buckets.3 = (f32[520,128]{1,0:T(8,128)}, f32[1032,128]{1,0:T(8,128)}, f32[1032,128]{1,0:T(8,128)}, f32[1032,128]{1,0:T(8,128)}, f32[1032,128]{1,0:T(8,128)}) custom-call(s32[8]{0:T(128)} %new_row.3, s32[4,8]{1,0:T(4,128)} %bitcast.18, s32[2,8]{1,0:T(2,128)} %bitcast.20, s32[1]{0:T(128)} %bitcast.2.my_x, f32[8,512,128]{2,1,0:T(8,128)} %bitcast.14, ...), custom_call_target="tpu_custom_call" | custom-call | tf_op jit(solution)/shard_map/buckets/pallas_call | solution.py:143
  33.4 0.0 collective-permute-done.refs_0_.refs_1_
  33.4 6.0 %collective-permute-start.10 = (f32[520,128]{1,0:T(8,128)}, f32[520,128]{1,0:T(8,128)}, u32[]{:S(2)}, u32[]{:S(2)}) collective-permute-start(f32[520,128]{1,0:T(8,128)} %get-tuple-element.71), channel_id=1, source_target_pairs={{0,320},{32,352},{64,384},{96,416},{128,448},{160,480},{192,0},{22... | collective-permute-start | bytes 798728 | tf_op jit(solution)/shard_map/ppermute | solution.py:38
  39.5 3.6 %collective-permute-start.6 = (f32[1032,128]{1,0:T(8,128)}, f32[1032,128]{1,0:T(8,128)}, u32[]{:S(2)}, u32[]{:S(2)}) collective-permute-start(f32[1032,128]{1,0:T(8,128)} %get-tuple-element.60), channel_id=1, source_target_pairs={{0,96},{32,128},{64,160},{96,192},{128,224},{160,256},{192,288},{2... | collective-permute-start | bytes 1585160 | tf_op jit(solution)/shard_map/ppermute | solution.py:38
  43.1 2.9 %collective-permute-start.5 = (f32[1032,128]{1,0:T(8,128)}, f32[1032,128]{1,0:T(8,128)}, u32[]{:S(2)}, u32[]{:S(2)}) collective-permute-start(f32[1032,128]{1,0:T(8,128)} %get-tuple-element.58), channel_id=1, source_target_pairs={{0,64},{32,96},{64,128},{96,160},{128,192},{160,224},{192,256},{22... | collective-permute-start | bytes 1585160 | tf_op jit(solution)/shard_map/ppermute | solution.py:38
  46.0 0.7 slice.26
  46.7 2.5 %split.2 = (bf16[24,128,256]{2,1,0:T(8,128)(2,1)S(1)}, bf16[24,128,256]{2,1,0:T(8,128)(2,1)S(1)}, bf16[16,256,128]{2,1,0:T(8,128)(2,1)S(1)}) custom-call(f32[2056,128]{1,0:T(8,128)} %collective-permute-done.refs_0_.refs_1_, f32[2056,128]{1,0:T(8,128)S(1)} %copy-done, f32[2056,128]{1,0:T(8,128)S(1)} %collective-permute-done.1.refs_2_), custom_call_target="tpu_custom_call" | custom-call | tf_op jit(solution)/shard_map/split/pallas_call | solution.py:190
  49.2 3.4 %galerkin.7 = (f32[20,128,128]{2,1,0:T(8,128)S(1)}, f32[16,128,128]{2,1,0:T(8,128)S(1)}) custom-call(s32[24,2]{1,0:T(8,128)S(1)} %fusion.1.slots, s32[1]{0:T(128)} %bitcast.5.first, bf16[24,128,256]{2,1,0:T(8,128)(2,1)S(1)} %get-tuple-element.41.high, bf16[24,128,256]{2,1,0:T(8,128)(2,1)S(1)} %get-tuple-element.42.low, ...), custom_call_target="tpu_custom_call" | custom-call | flops 100000000376832 | bytes 1 | tf_op jit(solution)/shard_map/galerkin/pallas_call | solution.py:280
  52.6 22.1 %collective-permute-done.7 = f32[520,128]{1,0:T(8,128)} collective-permute-done((f32[520,128]{1,0:T(8,128)}, f32[520,128]{1,0:T(8,128)}, u32[]{:S(2)}, u32[]{:S(2)}) %collective-permute-start.7) | collective-permute-done | bytes 266272 | tf_op jit(solution)/shard_map/ppermute | solution.py:38
  74.7 0.0 collective-permute-done.3.refs_0_
  74.8 11.2 %collective-permute-start.8 = (f32[520,128]{1,0:T(8,128)}, f32[520,128]{1,0:T(8,128)}, u32[]{:S(2)}, u32[]{:S(2)}) collective-permute-start(f32[520,128]{1,0:T(8,128)} %collective-permute-done.7), channel_id=1, source_target_pairs={{0,352},{32,384},{64,416},{96,448},{128,480},{160,0},{192,32},{224... | collective-permute-start | bytes 798728 | tf_op jit(solution)/shard_map/ppermute | solution.py:38
  85.9 4.2 %collective-permute-start.2 = (f32[2056,128]{1,0:T(8,128)}, f32[2056,128]{1,0:T(8,128)}, u32[]{:S(2)}, u32[]{:S(2)}) collective-permute-start(f32[2056,128]{1,0:T(8,128)} %collective-permute-done.refs_0_.refs_1_), channel_id=1, source_target_pairs={{0,1},{1,2},{2,3},{3,4},{4,5},{5,6},{6,7},{7,8},{8,9},{9,10},{10,1... | collective-permute-start | bytes 3158024 | tf_op jit(solution)/shard_map/ppermute | solution.py:44
  90.2 0.0 copy-start.1
  90.2 1.8 %galerkin.8 = (f32[20,128,128]{2,1,0:T(8,128)S(1)}, f32[16,128,128]{2,1,0:T(8,128)S(1)}) custom-call(s32[24,2]{1,0:T(8,128)S(1)} %fusion.1.slots, s32[1]{0:T(128)} %bitcast.5.first, bf16[24,128,256]{2,1,0:T(8,128)(2,1)S(1)} %get-tuple-element.41.high, bf16[24,128,256]{2,1,0:T(8,128)(2,1)S(1)} %get-tuple-element.42.low, ...), custom_call_target="tpu_custom_call" | custom-call | flops 100000000376832 | bytes 1 | tf_op jit(solution)/shard_map/galerkin/pallas_call | solution.py:280
  92.0 0.0 collective-permute-done.10
  92.0 2.8 %collective-permute-start.4 = (f32[1032,128]{1,0:T(8,128)}, f32[1032,128]{1,0:T(8,128)}, u32[]{:S(2)}, u32[]{:S(2)}) collective-permute-start(f32[1032,128]{1,0:T(8,128)} %get-tuple-element.56), channel_id=1, source_target_pairs={{0,32},{32,64},{64,96},{96,128},{128,160},{160,192},{192,224},{224... | collective-permute-start | bytes 1585160 | tf_op jit(solution)/shard_map/ppermute | solution.py:38
  94.8 7.4 %collective-permute-done.2.refs_0_ = f32[2056,128]{1,0:T(8,128)} collective-permute-done((f32[2056,128]{1,0:T(8,128)}, f32[2056,128]{1,0:T(8,128)}, u32[]{:S(2)}, u32[]{:S(2)}) %collective-permute-start.2) | collective-permute-done | bytes 1052704 | tf_op jit(solution)/shard_map/ppermute | solution.py:44
  102.2 5.0 %collective-permute-start.11 = (f32[520,128]{1,0:T(8,128)}, f32[520,128]{1,0:T(8,128)}, u32[]{:S(2)}, u32[]{:S(2)}) collective-permute-start(f32[520,128]{1,0:T(8,128)} %collective-permute-done.10), channel_id=1, source_target_pairs={{0,352},{32,384},{64,416},{96,448},{128,480},{160,0},{192,32},{224... | collective-permute-start | bytes 798728 | tf_op jit(solution)/shard_map/ppermute | solution.py:38
  107.2 0.7 slice.28
  107.9 2.8 %split.3 = (bf16[24,128,256]{2,1,0:T(8,128)(2,1)S(1)}, bf16[24,128,256]{2,1,0:T(8,128)(2,1)S(1)}, bf16[16,256,128]{2,1,0:T(8,128)(2,1)S(1)}) custom-call(f32[2056,128]{1,0:T(8,128)} %collective-permute-done.2.refs_0_, f32[2056,128]{1,0:T(8,128)} %collective-permute-done.refs_0_.refs_1_, f32[2056,128]{1,0:T(8,128)S(1)} %copy-done.1), custom_call_target="tpu_custom_call" | custom-call | tf_op jit(solution)/shard_map/split/pallas_call | solution.py:190
  110.7 1.0 copy-done.2
  111.7 0.4 collective-permute-done.6.refs_0_
  112.1 4.7 %galerkin.9 = (f32[20,128,128]{2,1,0:T(8,128)S(1)}, f32[16,128,128]{2,1,0:T(8,128)}) custom-call(s32[24,2]{1,0:T(8,128)S(1)} %fusion.1.slots, s32[1]{0:T(128)} %bitcast.5.first, bf16[24,128,256]{2,1,0:T(8,128)(2,1)S(1)} %get-tuple-element.41.high, bf16[24,128,256]{2,1,0:T(8,128)(2,1)S(1)} %get-tuple-element.42.low, ...), custom_call_target="tpu_custom_call" | custom-call | flops 100000000376832 | bytes 1 | tf_op jit(solution)/shard_map/galerkin/pallas_call | solution.py:280
  116.8 4.5 %collective-permute-start.15 = (f32[16,128,128]{2,1,0:T(8,128)}, f32[16,128,128]{2,1,0:T(8,128)}, u32[]{:S(2)}, u32[]{:S(2)}) collective-permute-start(f32[16,128,128]{2,1,0:T(8,128)} %get-tuple-element.63), channel_id=1, source_target_pairs={{0,1},{1,2},{2,3},{3,4},{4,5},{5,6},{6,7},{7,8},{8,9},{9,10},{10,1... | collective-permute-start | bytes 3145736 | tf_op jit(solution)/shard_map/ppermute | solution.py:44
  121.3 11.6 %collective-permute-done.8.refs_1_ = f32[520,128]{1,0:T(8,128)} collective-permute-done((f32[520,128]{1,0:T(8,128)}, f32[520,128]{1,0:T(8,128)}, u32[]{:S(2)}, u32[]{:S(2)}) %collective-permute-start.8) | collective-permute-done | bytes 266272 | tf_op jit(solution)/shard_map/ppermute | solution.py:38
  132.8 1.9 %collective-permute-start.14 = (f32[520,128]{1,0:T(8,128)}, f32[520,128]{1,0:T(8,128)}, u32[]{:S(2)}, u32[]{:S(2)}) collective-permute-start(f32[520,128]{1,0:T(8,128)} %collective-permute-done.8.refs_1_), channel_id=1, source_target_pairs={{0,1},{1,2},{2,3},{3,4},{4,5},{5,6},{6,7},{7,8},{8,9},{9,10},{10,1... | collective-permute-start | bytes 798728 | tf_op jit(solution)/shard_map/ppermute | solution.py:44
  134.7 9.4 %collective-permute-start.13 = (f32[1032,128]{1,0:T(8,128)}, f32[1032,128]{1,0:T(8,128)}, u32[]{:S(2)}, u32[]{:S(2)}) collective-permute-start(f32[1032,128]{1,0:T(8,128)} %collective-permute-done.5.refs_0_), channel_id=1, source_target_pairs={{0,1},{1,2},{2,3},{3,4},{4,5},{5,6},{6,7},{7,8},{8,9},{9,10},{10,1... | collective-permute-start | bytes 1585160 | tf_op jit(solution)/shard_map/ppermute | solution.py:44
  144.2 2.7 %galerkin.10.refs_2_ = f32[20,128,128]{2,1,0:T(8,128)S(1)} custom-call(s32[24,2]{1,0:T(8,128)S(1)} %fusion.1.slots, s32[1]{0:T(128)} %bitcast.5.first, bf16[24,128,256]{2,1,0:T(8,128)(2,1)S(1)} %get-tuple-element.41.high, bf16[24,128,256]{2,1,0:T(8,128)(2,1)S(1)} %get-tuple-element.42.low, bf16[16,256,128]{2,1,0:T(8,128)(2,1)S(1)} %get-tuple-element.43.turned, ...), custom_call_target="tpu_custom_call" | custom-call | flops 100000000376832 | bytes 1 | tf_op jit(solution)/shard_map/galerkin/pallas_call | solution.py:280
  147.0 0.0 copy-start.9
  147.0 1.0 copy-done.9
  148.0 3.1 %collective-permute-start.9 = (f32[1032,128]{1,0:T(8,128)}, f32[1032,128]{1,0:T(8,128)}, u32[]{:S(2)}, u32[]{:S(2)}) collective-permute-start(f32[1032,128]{1,0:T(8,128)} %collective-permute-done.4.refs_0_), channel_id=1, source_target_pairs={{0,1},{1,2},{2,3},{3,4},{4,5},{5,6},{6,7},{7,8},{8,9},{9,10},{10,1... | collective-permute-start | bytes 1585160 | tf_op jit(solution)/shard_map/ppermute | solution.py:44
  151.1 0.0 collective-permute-done.11.refs_1_
  151.1 2.9 %collective-permute-start.12 = (f32[520,128]{1,0:T(8,128)}, f32[520,128]{1,0:T(8,128)S(1)}, u32[]{:S(2)}, u32[]{:S(2)}) collective-permute-start(f32[520,128]{1,0:T(8,128)} %collective-permute-done.11.refs_1_), channel_id=1, source_target_pairs={{0,1},{1,2},{2,3},{3,4},{4,5},{5,6},{6,7},{7,8},{8,9},{9,10},{10,1... | collective-permute-start | bytes 798728 | tf_op jit(solution)/shard_map/ppermute | solution.py:44
  154.0 0.0 collective-permute-done.14.refs_1_
  154.1 0.0 collective-permute-done.15.refs_3_
  154.1 1.2 copy-done.3
  155.3 1.3 copy-done.10
  156.6 4.5 %galerkin.11.refs_2_ = f32[20,128,128]{2,1,0:T(8,128)S(1)} custom-call(s32[24,2]{1,0:T(8,128)S(1)} %fusion.3.slots, s32[1]{0:T(128)} %bitcast.7.first, bf16[24,128,256]{2,1,0:T(8,128)(2,1)S(1)} %get-tuple-element.48.high, bf16[24,128,256]{2,1,0:T(8,128)(2,1)S(1)} %get-tuple-element.49.low, bf16[16,256,128]{2,1,0:T(8,128)(2,1)S(1)} %copy-done.3, ...), custom_call_target="tpu_custom_call" | custom-call | flops 1 | bytes 1 | tf_op jit(solution)/shard_map/galerkin/pallas_call | solution.py:280
  161.2 3.7 %galerkin.12.refs_2_ = f32[20,128,128]{2,1,0:T(8,128)S(1)} custom-call(s32[24,2]{1,0:T(8,128)S(1)} %fusion.1.slots, s32[1]{0:T(128)} %bitcast.5.first, bf16[24,128,256]{2,1,0:T(8,128)(2,1)S(1)} %copy-done.6, bf16[24,128,256]{2,1,0:T(8,128)(2,1)S(1)} %copy-done.8, bf16[16,256,128]{2,1,0:T(8,128)(2,1)S(1)} %copy-done.12, ...), custom_call_target="tpu_custom_call" | custom-call | flops 1 | bytes 1 | tf_op jit(solution)/shard_map/galerkin/pallas_call | solution.py:280
  164.9 0.0 collective-permute-done.12.refs_1_
  164.9 3.5 %galerkin.13 = f32[20,128,128]{2,1,0:T(8,128)} custom-call(s32[24,2]{1,0:T(8,128)S(1)} %fusion.3.slots, s32[1]{0:T(128)} %bitcast.7.first, bf16[24,128,256]{2,1,0:T(8,128)(2,1)S(1)} %get-tuple-element.48.high, bf16[24,128,256]{2,1,0:T(8,128)(2,1)S(1)} %get-tuple-element.49.low, bf16[16,256,128]{2,1,0:T(8,128)(2,1)S(1)} %copy-done.4, ...), custom_call_target="tpu_custom_call" | custom-call | flops 1 | bytes 1 | tf_op jit(solution)/shard_map/galerkin/pallas_call | solution.py:280
  (37 shorter events, 0.1 us)
Async XLA Ops:
  3.3 26.1 %collective-permute-start.1 = (f32[2056,128]{1,0:T(8,128)}, f32[2056,128]{1,0:T(8,128)S(1)}, u32[]{:S(2)}, u32[]{:S(2)}) collective-permute-start(f32[2056,128]{1,0:T(8,128)} %get-tuple-element.40.refs_1_.refs_2_), channel_id=1, source_target_pairs={{1,0},{2,1},{3,2},{4,3},{5,4},{6,5},{7,6},{8,7},{9,8},{10,9},{11,1... | collective-permute-start | bytes 3158024 | tf_op jit(solution)/shard_map/ppermute | solution.py:44
  12.2 21.2 %collective-permute-start = (f32[2056,128]{1,0:T(8,128)}, f32[2056,128]{1,0:T(8,128)}, u32[]{:S(2)}, u32[]{:S(2)}) collective-permute-start(f32[2056,128]{1,0:T(8,128)} %get-tuple-element.40.refs_1_.refs_2_), channel_id=1, source_target_pairs={{0,1},{1,2},{2,3},{3,4},{4,5},{5,6},{6,7},{7,8},{8,9},{9,10},{10,1... | collective-permute-start | bytes 3158024 | tf_op jit(solution)/shard_map/ppermute | solution.py:44
  14.1 60.6 %collective-permute-start.7 = (f32[520,128]{1,0:T(8,128)}, f32[520,128]{1,0:T(8,128)}, u32[]{:S(2)}, u32[]{:S(2)}) collective-permute-start(f32[520,128]{1,0:T(8,128)} %get-tuple-element.65), channel_id=1, source_target_pairs={{0,320},{32,352},{64,384},{96,416},{128,448},{160,480},{192,0},{22... | collective-permute-start | bytes 798728 | tf_op jit(solution)/shard_map/ppermute | solution.py:38
  24.5 50.3 %collective-permute-start.3 = (f32[1032,128]{1,0:T(8,128)}, f32[1032,128]{1,0:T(8,128)}, u32[]{:S(2)}, u32[]{:S(2)}) collective-permute-start(f32[1032,128]{1,0:T(8,128)} %get-tuple-element.52), channel_id=1, source_target_pairs={{0,128},{32,160},{64,192},{96,224},{128,256},{160,288},{192,320},{... | collective-permute-start | bytes 1585160 | tf_op jit(solution)/shard_map/ppermute | solution.py:38
  29.4 17.2 %copy-start.14 = (f32[8,2]{1,0:T(8,128)}, f32[8,2]{1,0:T(8,128)S(1)}, u32[]{:S(2)}) copy-start(f32[8,2]{1,0:T(8,128)S(1)} %slice.21) | copy-start | bytes 196
  29.4 17.2 %copy-start = (f32[2056,128]{1,0:T(8,128)S(1)}, f32[2056,128]{1,0:T(8,128)}, u32[]{:S(2)}) copy-start(f32[2056,128]{1,0:T(8,128)} %get-tuple-element.40.refs_1_.refs_2_) | copy-start | bytes 3158020
  33.4 58.6 %collective-permute-start.10 = (f32[520,128]{1,0:T(8,128)}, f32[520,128]{1,0:T(8,128)}, u32[]{:S(2)}, u32[]{:S(2)}) collective-permute-start(f32[520,128]{1,0:T(8,128)} %get-tuple-element.71), channel_id=1, source_target_pairs={{0,320},{32,352},{64,384},{96,416},{128,448},{160,480},{192,0},{22... | collective-permute-start | bytes 798728 | tf_op jit(solution)/shard_map/ppermute | solution.py:38
  39.5 72.6 %collective-permute-start.6 = (f32[1032,128]{1,0:T(8,128)}, f32[1032,128]{1,0:T(8,128)}, u32[]{:S(2)}, u32[]{:S(2)}) collective-permute-start(f32[1032,128]{1,0:T(8,128)} %get-tuple-element.60), channel_id=1, source_target_pairs={{0,96},{32,128},{64,160},{96,192},{128,224},{160,256},{192,288},{2... | collective-permute-start | bytes 1585160 | tf_op jit(solution)/shard_map/ppermute | solution.py:38
  43.1 89.7 %collective-permute-start.5 = (f32[1032,128]{1,0:T(8,128)}, f32[1032,128]{1,0:T(8,128)}, u32[]{:S(2)}, u32[]{:S(2)}) collective-permute-start(f32[1032,128]{1,0:T(8,128)} %get-tuple-element.58), channel_id=1, source_target_pairs={{0,64},{32,96},{64,128},{96,160},{128,192},{160,224},{192,256},{22... | collective-permute-start | bytes 1585160 | tf_op jit(solution)/shard_map/ppermute | solution.py:38
  46.6 2.6 %copy-start.16 = (f32[8,2]{1,0:T(8,128)}, f32[8,2]{1,0:T(8,128)S(1)}, u32[]{:S(2)}) copy-start(f32[8,2]{1,0:T(8,128)S(1)} %slice.26) | copy-start | bytes 196
  46.7 2.6 %copy-start.13 = (f32[1032,128]{1,0:T(8,128)S(1)}, f32[1032,128]{1,0:T(8,128)}, u32[]{:S(2)}) copy-start(f32[1032,128]{1,0:T(8,128)} %get-tuple-element.45.refs_0_) | copy-start | bytes 1585156
  49.2 95.0 %copy-start.5 = (bf16[24,128,256]{2,1,0:T(8,128)(2,1)}, bf16[24,128,256]{2,1,0:T(8,128)(2,1)S(1)}, u32[]{:S(2)}) copy-start(bf16[24,128,256]{2,1,0:T(8,128)(2,1)S(1)} %get-tuple-element.41.high) | copy-start | bytes 4718596
  49.2 95.0 %copy-start.7 = (bf16[24,128,256]{2,1,0:T(8,128)(2,1)}, bf16[24,128,256]{2,1,0:T(8,128)(2,1)S(1)}, u32[]{:S(2)}) copy-start(bf16[24,128,256]{2,1,0:T(8,128)(2,1)S(1)} %get-tuple-element.42.low) | copy-start | bytes 4718596
  49.2 95.0 %copy-start.11 = (bf16[16,256,128]{2,1,0:T(8,128)(2,1)}, bf16[16,256,128]{2,1,0:T(8,128)(2,1)S(1)}, u32[]{:S(2)}) copy-start(bf16[16,256,128]{2,1,0:T(8,128)(2,1)S(1)} %get-tuple-element.43.turned) | copy-start | bytes 3145732
  74.8 58.1 %collective-permute-start.8 = (f32[520,128]{1,0:T(8,128)}, f32[520,128]{1,0:T(8,128)}, u32[]{:S(2)}, u32[]{:S(2)}) collective-permute-start(f32[520,128]{1,0:T(8,128)} %collective-permute-done.7), channel_id=1, source_target_pairs={{0,352},{32,384},{64,416},{96,448},{128,480},{160,0},{192,32},{224... | collective-permute-start | bytes 798728 | tf_op jit(solution)/shard_map/ppermute | solution.py:38
  85.9 16.3 %collective-permute-start.2 = (f32[2056,128]{1,0:T(8,128)}, f32[2056,128]{1,0:T(8,128)}, u32[]{:S(2)}, u32[]{:S(2)}) collective-permute-start(f32[2056,128]{1,0:T(8,128)} %collective-permute-done.refs_0_.refs_1_), channel_id=1, source_target_pairs={{0,1},{1,2},{2,3},{3,4},{4,5},{5,6},{6,7},{7,8},{8,9},{9,10},{10,1... | collective-permute-start | bytes 3158024 | tf_op jit(solution)/shard_map/ppermute | solution.py:44
  90.2 17.7 %copy-start.1 = (f32[2056,128]{1,0:T(8,128)S(1)}, f32[2056,128]{1,0:T(8,128)}, u32[]{:S(2)}) copy-start(f32[2056,128]{1,0:T(8,128)} %get-tuple-element.40.refs_1_.refs_2_) | copy-start | bytes 3158020
  92.0 19.7 %copy-start.15 = (f32[8,2]{1,0:T(8,128)S(1)}, f32[8,2]{1,0:T(8,128)}, u32[]{:S(2)}) copy-start(f32[8,2]{1,0:T(8,128)} %copy-done.14) | copy-start | bytes 196
  92.0 19.7 %copy-start.17 = (f32[8,2]{1,0:T(8,128)S(1)}, f32[8,2]{1,0:T(8,128)}, u32[]{:S(2)}) copy-start(f32[8,2]{1,0:T(8,128)} %copy-done.16) | copy-start | bytes 196
  92.0 56.0 %collective-permute-start.4 = (f32[1032,128]{1,0:T(8,128)}, f32[1032,128]{1,0:T(8,128)}, u32[]{:S(2)}, u32[]{:S(2)}) collective-permute-start(f32[1032,128]{1,0:T(8,128)} %get-tuple-element.56), channel_id=1, source_target_pairs={{0,32},{32,64},{64,96},{96,128},{128,160},{160,192},{192,224},{224... | collective-permute-start | bytes 1585160 | tf_op jit(solution)/shard_map/ppermute | solution.py:38
  102.2 48.9 %collective-permute-start.11 = (f32[520,128]{1,0:T(8,128)}, f32[520,128]{1,0:T(8,128)}, u32[]{:S(2)}, u32[]{:S(2)}) collective-permute-start(f32[520,128]{1,0:T(8,128)} %collective-permute-done.10), channel_id=1, source_target_pairs={{0,352},{32,384},{64,416},{96,448},{128,480},{160,0},{192,32},{224... | collective-permute-start | bytes 798728 | tf_op jit(solution)/shard_map/ppermute | solution.py:38
  110.7 1.0 copy-start.2
  116.8 37.3 %collective-permute-start.15 = (f32[16,128,128]{2,1,0:T(8,128)}, f32[16,128,128]{2,1,0:T(8,128)}, u32[]{:S(2)}, u32[]{:S(2)}) collective-permute-start(f32[16,128,128]{2,1,0:T(8,128)} %get-tuple-element.63), channel_id=1, source_target_pairs={{0,1},{1,2},{2,3},{3,4},{4,5},{5,6},{6,7},{7,8},{8,9},{9,10},{10,1... | collective-permute-start | bytes 3145736 | tf_op jit(solution)/shard_map/ppermute | solution.py:44
  132.8 21.2 %collective-permute-start.14 = (f32[520,128]{1,0:T(8,128)}, f32[520,128]{1,0:T(8,128)}, u32[]{:S(2)}, u32[]{:S(2)}) collective-permute-start(f32[520,128]{1,0:T(8,128)} %collective-permute-done.8.refs_1_), channel_id=1, source_target_pairs={{0,1},{1,2},{2,3},{3,4},{4,5},{5,6},{6,7},{7,8},{8,9},{9,10},{10,1... | collective-permute-start | bytes 798728 | tf_op jit(solution)/shard_map/ppermute | solution.py:44
  134.7 19.3 %collective-permute-start.13 = (f32[1032,128]{1,0:T(8,128)}, f32[1032,128]{1,0:T(8,128)}, u32[]{:S(2)}, u32[]{:S(2)}) collective-permute-start(f32[1032,128]{1,0:T(8,128)} %collective-permute-done.5.refs_0_), channel_id=1, source_target_pairs={{0,1},{1,2},{2,3},{3,4},{4,5},{5,6},{6,7},{7,8},{8,9},{9,10},{10,1... | collective-permute-start | bytes 1585160 | tf_op jit(solution)/shard_map/ppermute | solution.py:44
  147.0 1.1 copy-start.9
  148.0 16.9 %collective-permute-start.9 = (f32[1032,128]{1,0:T(8,128)}, f32[1032,128]{1,0:T(8,128)}, u32[]{:S(2)}, u32[]{:S(2)}) collective-permute-start(f32[1032,128]{1,0:T(8,128)} %collective-permute-done.4.refs_0_), channel_id=1, source_target_pairs={{0,1},{1,2},{2,3},{3,4},{4,5},{5,6},{6,7},{7,8},{8,9},{9,10},{10,1... | collective-permute-start | bytes 1585160 | tf_op jit(solution)/shard_map/ppermute | solution.py:44
  151.1 13.8 %collective-permute-start.12 = (f32[520,128]{1,0:T(8,128)}, f32[520,128]{1,0:T(8,128)S(1)}, u32[]{:S(2)}, u32[]{:S(2)}) collective-permute-start(f32[520,128]{1,0:T(8,128)} %collective-permute-done.11.refs_1_), channel_id=1, source_target_pairs={{0,1},{1,2},{2,3},{3,4},{4,5},{5,6},{6,7},{7,8},{8,9},{9,10},{10,1... | collective-permute-start | bytes 798728 | tf_op jit(solution)/shard_map/ppermute | solution.py:44
  154.1 1.2 copy-start.3
  155.3 1.3 copy-start.10
  156.6 4.5 %copy-start.6 = (bf16[24,128,256]{2,1,0:T(8,128)(2,1)S(1)}, bf16[24,128,256]{2,1,0:T(8,128)(2,1)}, u32[]{:S(2)}) copy-start(bf16[24,128,256]{2,1,0:T(8,128)(2,1)} %copy-done.5) | copy-start | bytes 4718596
  156.6 4.5 %copy-start.8 = (bf16[24,128,256]{2,1,0:T(8,128)(2,1)S(1)}, bf16[24,128,256]{2,1,0:T(8,128)(2,1)}, u32[]{:S(2)}) copy-start(bf16[24,128,256]{2,1,0:T(8,128)(2,1)} %copy-done.7) | copy-start | bytes 4718596
  156.6 4.6 %copy-start.12 = (bf16[16,256,128]{2,1,0:T(8,128)(2,1)S(1)}, bf16[16,256,128]{2,1,0:T(8,128)(2,1)}, u32[]{:S(2)}) copy-start(bf16[16,256,128]{2,1,0:T(8,128)(2,1)} %copy-done.11) | copy-start | bytes 3145732
  161.2 3.7 %copy-start.4 = (bf16[16,256,128]{2,1,0:T(8,128)(2,1)S(1)}, bf16[16,256,128]{2,1,0:T(8,128)(2,1)}, u32[]{:S(2)}) copy-start(bf16[16,256,128]{2,1,0:T(8,128)(2,1)} %copy-done.2) | copy-start | bytes 3145732

commit v8 on v6

--- a/solution.py
+++ b/solution.py
@@ -361,9 +361,9 @@
     (own,) = add(mine, (0,), [d2, far_a], [own], 10**14)
     mid = own
     (own,) = add(theirs, (0,), [f2, f_far_a], [own], arrived=on)
-    f_far_b = beside(after(far_b, own), 1)
     f1 = beside(after(d1, mid), 1)
-    (own,) = add(mine, (0,), [d1, far_b], [own], 10**14)
+    f_far_b = beside(after(far_b, mid, d1), 1)
+    (own,) = add(mine, (0,), [d1, far_b], [own])
     (own,) = add(theirs, (0,), [f1, f_far_b], [own])
     return own.reshape(coarse_rows, SLOTS, TILE, TILE)
 

time: 170 us -> 174 us (1.024)
  local copies, waits for them, and re-layouts: 2.64 us -> 6.71 us
  starting transfers between devices: 74.3 us -> 77.4 us
  waiting for transfers between devices: 53.9 us -> 52 us
    unnamed x12 -> x36, local copies, waits for them, and re-layouts: 0.6 us -> 4.65 us
    ppermute x8, waiting for transfers between devices: 17.7 us -> 14 us  [beside(): return lax.ppermute(value, 'gy', route)]
    ppermute x8, starting transfers between devices: 55.8 us -> 58.1 us  [hop(): lax.ppermute(value, axis, [(i, (i + steps) % count) for i in range(count)])]
    ppermute x8, waiting for transfers between devices: 36.2 us -> 38 us  [hop(): lax.ppermute(value, axis, [(i, (i + steps) % count) for i in range(count)])]
  transfers between devices with their start and end apart: 16 -> 16, of which waited for: 9 -> 8; matrix products, arithmetic and copies ran while one was open for 1% -> 1% of each run, Pallas kernels for 17% -> 17%
where the time goes in v8:
time: 174 us; the launch traced here: 172 us
  starting transfers between devices  77.4 us (44%)
  waiting for transfers between devices  52 us (30%)
  Pallas kernels  35.2 us (20%)
  local copies, waits for them, and re-layouts  6.71 us (4%)
    ppermute x8, starting transfers between devices, hop(): lax.ppermute(value, axis, [(i, (i + steps) % count) for i in range(count)])  58.1 us
    ppermute x8, waiting for transfers between devices, hop(): lax.ppermute(value, axis, [(i, (i + steps) % count) for i in range(count)])  38 us
    pallas_call x7, Pallas kernels, galerkin(): pl.pallas_call(functools.partial(galerkin_kernel, rows, shapes, targets,...  22.8 us
    ppermute x8, starting transfers between devices, beside(): return lax.ppermute(value, 'gy', route)  19.3 us
    ppermute x8, waiting for transfers between devices, beside(): return lax.ppermute(value, 'gy', route)  14 us
    pallas_call x2, Pallas kernels, buckets(): pl.pallas_call(functools.partial(bucket_kernel, rows, gx, rows * gy, layo...  7.2 us
    pallas_call x2, Pallas kernels, split(): pl.pallas_call(functools.partial(split_kernel, rows), out_shape=[wide, wi...  5.28 us
    unnamed x36, local copies, waits for them, and re-layouts  4.65 us
  transfers between devices with their start and end apart: 16, of which 8 were waited for; matrix products, arithmetic and copies ran while one was open for 1% of the time, Pallas kernels for 17%

profile of v8, /device:TPU:6, one launch (start us, length us, event | category | flops | bytes accessed | tf_op | source)
XLA Modules:
  0.0 172.0 jit_solution(5354539690917237067)
XLA Ops:
  0.0 3.6 %buckets.2 = (f32[2056,128]{1,0:T(8,128)}, f32[520,128]{1,0:T(8,128)}, f32[1032,128]{1,0:T(8,128)}) custom-call(s32[8]{0:T(128)} %new_row.3, s32[4,8]{1,0:T(4,128)} %bitcast.15, s32[2,8]{1,0:T(2,128)} %bitcast.17, s32[1]{0:T(128)} %bitcast.2.my_x, f32[8,512,128]{2,1,0:T(8,128)} %bitcast.11, f32[2048,128]{1,0:T(8,128)} %bitcast.13), custom_call_target="tpu_custom_call" | custom-call | tf_op jit(solution)/shard_map/buckets/pallas_call | solution.py:143
  3.6 4.3 %collective-permute-start.1 = (f32[2056,128]{1,0:T(8,128)}, f32[2056,128]{1,0:T(8,128)S(1)}, u32[]{:S(2)}, u32[]{:S(2)}) collective-permute-start(f32[2056,128]{1,0:T(8,128)} %get-tuple-element.39.refs_1_.refs_2_), channel_id=1, source_target_pairs={{1,0},{2,1},{3,2},{4,3},{5,4},{6,5},{7,6},{8,7},{9,8},{10,9},{11,1... | collective-permute-start | bytes 3158024 | tf_op jit(solution)/shard_map/ppermute | solution.py:44
  8.0 1.9 %collective-permute-start = (f32[2056,128]{1,0:T(8,128)}, f32[2056,128]{1,0:T(8,128)}, u32[]{:S(2)}, u32[]{:S(2)}) collective-permute-start(f32[2056,128]{1,0:T(8,128)} %get-tuple-element.39.refs_1_.refs_2_), channel_id=1, source_target_pairs={{0,1},{1,2},{2,3},{3,4},{4,5},{5,6},{6,7},{7,8},{8,9},{9,10},{10,1... | collective-permute-start | bytes 3158024 | tf_op jit(solution)/shard_map/ppermute | solution.py:44
  9.9 14.8 %collective-permute-start.7 = (f32[520,128]{1,0:T(8,128)}, f32[520,128]{1,0:T(8,128)}, u32[]{:S(2)}, u32[]{:S(2)}) collective-permute-start(f32[520,128]{1,0:T(8,128)} %get-tuple-element.64), channel_id=1, source_target_pairs={{0,320},{32,352},{64,384},{96,416},{128,448},{160,480},{192,0},{22... | collective-permute-start | bytes 798728 | tf_op jit(solution)/shard_map/ppermute | solution.py:38
  24.7 4.3 %collective-permute-start.3 = (f32[1032,128]{1,0:T(8,128)}, f32[1032,128]{1,0:T(8,128)}, u32[]{:S(2)}, u32[]{:S(2)}) collective-permute-start(f32[1032,128]{1,0:T(8,128)} %get-tuple-element.51), channel_id=1, source_target_pairs={{0,128},{32,160},{64,192},{96,224},{128,256},{160,288},{192,320},{... | collective-permute-start | bytes 1585160 | tf_op jit(solution)/shard_map/ppermute | solution.py:38
  29.0 0.7 slice.18
  29.7 0.0 collective-permute-done.1.refs_2_
  29.7 3.6 %buckets.3 = (f32[520,128]{1,0:T(8,128)}, f32[1032,128]{1,0:T(8,128)}, f32[1032,128]{1,0:T(8,128)}, f32[1032,128]{1,0:T(8,128)}, f32[1032,128]{1,0:T(8,128)}) custom-call(s32[8]{0:T(128)} %new_row.3, s32[4,8]{1,0:T(4,128)} %bitcast.16, s32[2,8]{1,0:T(2,128)} %bitcast.18, s32[1]{0:T(128)} %bitcast.2.my_x, f32[8,512,128]{2,1,0:T(8,128)} %bitcast.12, ...), custom_call_target="tpu_custom_call" | custom-call | tf_op jit(solution)/shard_map/buckets/pallas_call | solution.py:143
  33.3 0.0 collective-permute-done.refs_0_.refs_1_
  33.3 8.0 %collective-permute-start.10 = (f32[520,128]{1,0:T(8,128)}, f32[520,128]{1,0:T(8,128)}, u32[]{:S(2)}, u32[]{:S(2)}) collective-permute-start(f32[520,128]{1,0:T(8,128)} %get-tuple-element.70), channel_id=1, source_target_pairs={{0,320},{32,352},{64,384},{96,416},{128,448},{160,480},{192,0},{22... | collective-permute-start | bytes 798728 | tf_op jit(solution)/shard_map/ppermute | solution.py:38
  41.4 2.8 %collective-permute-start.6 = (f32[1032,128]{1,0:T(8,128)}, f32[1032,128]{1,0:T(8,128)}, u32[]{:S(2)}, u32[]{:S(2)}) collective-permute-start(f32[1032,128]{1,0:T(8,128)} %get-tuple-element.59), channel_id=1, source_target_pairs={{0,96},{32,128},{64,160},{96,192},{128,224},{160,256},{192,288},{2... | collective-permute-start | bytes 1585160 | tf_op jit(solution)/shard_map/ppermute | solution.py:38
  44.1 4.6 %collective-permute-start.5 = (f32[1032,128]{1,0:T(8,128)}, f32[1032,128]{1,0:T(8,128)}, u32[]{:S(2)}, u32[]{:S(2)}) collective-permute-start(f32[1032,128]{1,0:T(8,128)} %get-tuple-element.57), channel_id=1, source_target_pairs={{0,64},{32,96},{64,128},{96,160},{128,192},{160,224},{192,256},{22... | collective-permute-start | bytes 1585160 | tf_op jit(solution)/shard_map/ppermute | solution.py:38
  48.8 0.7 slice.22
  49.5 2.5 %split.2 = (bf16[24,128,256]{2,1,0:T(8,128)(2,1)S(1)}, bf16[24,128,256]{2,1,0:T(8,128)(2,1)S(1)}, bf16[16,256,128]{2,1,0:T(8,128)(2,1)S(1)}) custom-call(f32[2056,128]{1,0:T(8,128)} %collective-permute-done.refs_0_.refs_1_, f32[2056,128]{1,0:T(8,128)S(1)} %copy-done, f32[2056,128]{1,0:T(8,128)S(1)} %collective-permute-done.1.refs_2_), custom_call_target="tpu_custom_call" | custom-call | tf_op jit(solution)/shard_map/split/pallas_call | solution.py:190
  52.0 1.4 galerkin.7
  53.4 20.2 %collective-permute-done.7 = f32[520,128]{1,0:T(8,128)} collective-permute-done((f32[520,128]{1,0:T(8,128)}, f32[520,128]{1,0:T(8,128)}, u32[]{:S(2)}, u32[]{:S(2)}) %collective-permute-start.7) | collective-permute-done | bytes 266272 | tf_op jit(solution)/shard_map/ppermute | solution.py:38
  73.6 0.0 collective-permute-done.3.refs_0_
  73.6 11.3 %collective-permute-start.8 = (f32[520,128]{1,0:T(8,128)}, f32[520,128]{1,0:T(8,128)}, u32[]{:S(2)}, u32[]{:S(2)}) collective-permute-start(f32[520,128]{1,0:T(8,128)} %collective-permute-done.7), channel_id=1, source_target_pairs={{0,352},{32,384},{64,416},{96,448},{128,480},{160,0},{192,32},{224... | collective-permute-start | bytes 798728 | tf_op jit(solution)/shard_map/ppermute | solution.py:38
  84.9 1.9 %collective-permute-start.2 = (f32[2056,128]{1,0:T(8,128)}, f32[2056,128]{1,0:T(8,128)}, u32[]{:S(2)}, u32[]{:S(2)}) collective-permute-start(f32[2056,128]{1,0:T(8,128)} %collective-permute-done.refs_0_.refs_1_), channel_id=1, source_target_pairs={{0,1},{1,2},{2,3},{3,4},{4,5},{5,6},{6,7},{7,8},{8,9},{9,10},{10,1... | collective-permute-start | bytes 3158024 | tf_op jit(solution)/shard_map/ppermute | solution.py:44
  86.9 0.0 copy-start.1
  86.9 3.7 %galerkin.8 = (f32[20,128,128]{2,1,0:T(8,128)S(1)}, f32[16,128,128]{2,1,0:T(8,128)S(1)}) custom-call(s32[24,2]{1,0:T(8,128)S(1)} %fusion.1.slots, s32[1]{0:T(128)} %bitcast.5.first, bf16[24,128,256]{2,1,0:T(8,128)(2,1)S(1)} %get-tuple-element.40.high, bf16[24,128,256]{2,1,0:T(8,128)(2,1)S(1)} %get-tuple-element.41.low, ...), custom_call_target="tpu_custom_call" | custom-call | flops 100000000376832 | bytes 1 | tf_op jit(solution)/shard_map/galerkin/pallas_call | solution.py:280
  90.6 0.6 collective-permute-done.10
  91.2 5.6 %collective-permute-start.4 = (f32[1032,128]{1,0:T(8,128)}, f32[1032,128]{1,0:T(8,128)}, u32[]{:S(2)}, u32[]{:S(2)}) collective-permute-start(f32[1032,128]{1,0:T(8,128)} %get-tuple-element.55), channel_id=1, source_target_pairs={{0,32},{32,64},{64,96},{96,128},{128,160},{160,192},{192,224},{224... | collective-permute-start | bytes 1585160 | tf_op jit(solution)/shard_map/ppermute | solution.py:38
  96.8 6.7 %collective-permute-done.2.refs_0_ = f32[2056,128]{1,0:T(8,128)} collective-permute-done((f32[2056,128]{1,0:T(8,128)}, f32[2056,128]{1,0:T(8,128)}, u32[]{:S(2)}, u32[]{:S(2)}) %collective-permute-start.2) | collective-permute-done | bytes 1052704 | tf_op jit(solution)/shard_map/ppermute | solution.py:44
  103.5 6.7 %collective-permute-start.11 = (f32[520,128]{1,0:T(8,128)}, f32[520,128]{1,0:T(8,128)}, u32[]{:S(2)}, u32[]{:S(2)}) collective-permute-start(f32[520,128]{1,0:T(8,128)} %collective-permute-done.10), channel_id=1, source_target_pairs={{0,352},{32,384},{64,416},{96,448},{128,480},{160,0},{192,32},{224... | collective-permute-start | bytes 798728 | tf_op jit(solution)/shard_map/ppermute | solution.py:38
  110.2 0.7 slice.24
  110.9 2.8 %split.3 = (bf16[24,128,256]{2,1,0:T(8,128)(2,1)S(1)}, bf16[24,128,256]{2,1,0:T(8,128)(2,1)S(1)}, bf16[16,256,128]{2,1,0:T(8,128)(2,1)S(1)}) custom-call(f32[2056,128]{1,0:T(8,128)} %collective-permute-done.2.refs_0_, f32[2056,128]{1,0:T(8,128)} %collective-permute-done.refs_0_.refs_1_, f32[2056,128]{1,0:T(8,128)S(1)} %copy-done.1), custom_call_target="tpu_custom_call" | custom-call | tf_op jit(solution)/shard_map/split/pallas_call | solution.py:190
  113.7 1.0 copy-done.2
  114.7 4.7 %galerkin.9 = (f32[20,128,128]{2,1,0:T(8,128)S(1)}, f32[16,128,128]{2,1,0:T(8,128)}) custom-call(s32[24,2]{1,0:T(8,128)S(1)} %fusion.1.slots, s32[1]{0:T(128)} %bitcast.5.first, bf16[24,128,256]{2,1,0:T(8,128)(2,1)S(1)} %get-tuple-element.40.high, bf16[24,128,256]{2,1,0:T(8,128)(2,1)S(1)} %get-tuple-element.41.low, ...), custom_call_target="tpu_custom_call" | custom-call | flops 100000000376832 | bytes 1 | tf_op jit(solution)/shard_map/galerkin/pallas_call | solution.py:280
  119.4 1.9 %collective-permute-start.15 = (f32[16,128,128]{2,1,0:T(8,128)}, f32[16,128,128]{2,1,0:T(8,128)}, u32[]{:S(2)}, u32[]{:S(2)}) collective-permute-start(f32[16,128,128]{2,1,0:T(8,128)} %get-tuple-element.62), channel_id=1, source_target_pairs={{0,1},{1,2},{2,3},{3,4},{4,5},{5,6},{6,7},{7,8},{8,9},{9,10},{10,1... | collective-permute-start | bytes 3145736 | tf_op jit(solution)/shard_map/ppermute | solution.py:44
  121.3 2.8 %collective-permute-done.8.refs_1_ = f32[520,128]{1,0:T(8,128)} collective-permute-done((f32[520,128]{1,0:T(8,128)}, f32[520,128]{1,0:T(8,128)}, u32[]{:S(2)}, u32[]{:S(2)}) %collective-permute-start.8) | collective-permute-done | bytes 266272 | tf_op jit(solution)/shard_map/ppermute | solution.py:38
  124.2 9.4 %collective-permute-done.5.refs_0_ = f32[1032,128]{1,0:T(8,128)} collective-permute-done((f32[1032,128]{1,0:T(8,128)}, f32[1032,128]{1,0:T(8,128)}, u32[]{:S(2)}, u32[]{:S(2)}) %collective-permute-start.5) | collective-permute-done | bytes 528416 | tf_op jit(solution)/shard_map/ppermute | solution.py:38
  133.6 1.9 %collective-permute-start.13 = (f32[1032,128]{1,0:T(8,128)}, f32[1032,128]{1,0:T(8,128)}, u32[]{:S(2)}, u32[]{:S(2)}) collective-permute-start(f32[1032,128]{1,0:T(8,128)} %collective-permute-done.5.refs_0_), channel_id=1, source_target_pairs={{0,1},{1,2},{2,3},{3,4},{4,5},{5,6},{6,7},{7,8},{8,9},{9,10},{10,1... | collective-permute-start | bytes 1585160 | tf_op jit(solution)/shard_map/ppermute | solution.py:44
  135.6 2.5 %galerkin.10.refs_2_ = f32[20,128,128]{2,1,0:T(8,128)S(1)} custom-call(s32[24,2]{1,0:T(8,128)S(1)} %fusion.1.slots, s32[1]{0:T(128)} %bitcast.5.first, bf16[24,128,256]{2,1,0:T(8,128)(2,1)S(1)} %get-tuple-element.40.high, bf16[24,128,256]{2,1,0:T(8,128)(2,1)S(1)} %get-tuple-element.41.low, bf16[16,256,128]{2,1,0:T(8,128)(2,1)S(1)} %get-tuple-element.42.turned, ...), custom_call_target="tpu_custom_call" | custom-call | flops 100000000376832 | bytes 1 | tf_op jit(solution)/shard_map/galerkin/pallas_call | solution.py:280
  138.1 0.0 copy-start.9
  138.1 1.0 copy-done.9
  139.2 3.7 %collective-permute-done.4.refs_0_ = f32[1032,128]{1,0:T(8,128)} collective-permute-done((f32[1032,128]{1,0:T(8,128)}, f32[1032,128]{1,0:T(8,128)}, u32[]{:S(2)}, u32[]{:S(2)}) %collective-permute-start.4) | collective-permute-done | bytes 528416 | tf_op jit(solution)/shard_map/ppermute | solution.py:38
  142.9 2.1 %collective-permute-start.9 = (f32[1032,128]{1,0:T(8,128)}, f32[1032,128]{1,0:T(8,128)}, u32[]{:S(2)}, u32[]{:S(2)}) collective-permute-start(f32[1032,128]{1,0:T(8,128)} %collective-permute-done.4.refs_0_), channel_id=1, source_target_pairs={{0,1},{1,2},{2,3},{3,4},{4,5},{5,6},{6,7},{7,8},{8,9},{9,10},{10,1... | collective-permute-start | bytes 1585160 | tf_op jit(solution)/shard_map/ppermute | solution.py:44
  145.0 3.3 %collective-permute-start.14 = (f32[520,128]{1,0:T(8,128)}, f32[520,128]{1,0:T(8,128)}, u32[]{:S(2)}, u32[]{:S(2)}) collective-permute-start(f32[520,128]{1,0:T(8,128)} %collective-permute-done.8.refs_1_), channel_id=1, source_target_pairs={{0,1},{1,2},{2,3},{3,4},{4,5},{5,6},{6,7},{7,8},{8,9},{9,10},{10,1... | collective-permute-start | bytes 798728 | tf_op jit(solution)/shard_map/ppermute | solution.py:44
  148.3 1.2 collective-permute-done.11.refs_1_
  149.6 1.9 %collective-permute-start.12 = (f32[520,128]{1,0:T(8,128)}, f32[520,128]{1,0:T(8,128)S(1)}, u32[]{:S(2)}, u32[]{:S(2)}) collective-permute-start(f32[520,128]{1,0:T(8,128)} %collective-permute-done.11.refs_1_), channel_id=1, source_target_pairs={{0,1},{1,2},{2,3},{3,4},{4,5},{5,6},{6,7},{7,8},{8,9},{9,10},{10,1... | collective-permute-start | bytes 798728 | tf_op jit(solution)/shard_map/ppermute | solution.py:44
  151.5 7.3 %collective-permute-done.14.refs_1_ = f32[520,128]{1,0:T(8,128)} collective-permute-done((f32[520,128]{1,0:T(8,128)}, f32[520,128]{1,0:T(8,128)}, u32[]{:S(2)}, u32[]{:S(2)}) %collective-permute-start.14) | collective-permute-done | bytes 266272 | tf_op jit(solution)/shard_map/ppermute | solution.py:44
  158.7 1.2 copy-done.3
  160.0 1.3 copy-done.10
  161.3 3.9 %galerkin.11.refs_2_ = f32[20,128,128]{2,1,0:T(8,128)S(1)} custom-call(s32[24,2]{1,0:T(8,128)S(1)} %fusion.3.slots, s32[1]{0:T(128)} %bitcast.7.first, bf16[24,128,256]{2,1,0:T(8,128)(2,1)S(1)} %get-tuple-element.47.high, bf16[24,128,256]{2,1,0:T(8,128)(2,1)S(1)} %get-tuple-element.48.low, bf16[16,256,128]{2,1,0:T(8,128)(2,1)S(1)} %copy-done.3, ...), custom_call_target="tpu_custom_call" | custom-call | flops 1 | bytes 1 | tf_op jit(solution)/shard_map/galerkin/pallas_call | solution.py:280
  165.2 3.7 %galerkin.12.refs_2_ = f32[20,128,128]{2,1,0:T(8,128)S(1)} custom-call(s32[24,2]{1,0:T(8,128)S(1)} %fusion.1.slots, s32[1]{0:T(128)} %bitcast.5.first, bf16[24,128,256]{2,1,0:T(8,128)(2,1)S(1)} %copy-done.6, bf16[24,128,256]{2,1,0:T(8,128)(2,1)S(1)} %copy-done.8, bf16[16,256,128]{2,1,0:T(8,128)(2,1)S(1)} %copy-done.12, ...), custom_call_target="tpu_custom_call" | custom-call | flops 1 | bytes 1 | tf_op jit(solution)/shard_map/galerkin/pallas_call | solution.py:280
  168.9 0.0 collective-permute-done.12.refs_1_
  168.9 2.9 %galerkin.13 = f32[20,128,128]{2,1,0:T(8,128)} custom-call(s32[24,2]{1,0:T(8,128)S(1)} %fusion.3.slots, s32[1]{0:T(128)} %bitcast.7.first, bf16[24,128,256]{2,1,0:T(8,128)(2,1)S(1)} %get-tuple-element.47.high, bf16[24,128,256]{2,1,0:T(8,128)(2,1)S(1)} %get-tuple-element.48.low, bf16[16,256,128]{2,1,0:T(8,128)(2,1)S(1)} %copy-done.4, ...), custom_call_target="tpu_custom_call" | custom-call | flops 1 | bytes 1 | tf_op jit(solution)/shard_map/galerkin/pallas_call | solution.py:280
  (37 shorter events, 0.1 us)
Async XLA Ops:
  3.6 26.1 %collective-permute-start.1 = (f32[2056,128]{1,0:T(8,128)}, f32[2056,128]{1,0:T(8,128)S(1)}, u32[]{:S(2)}, u32[]{:S(2)}) collective-permute-start(f32[2056,128]{1,0:T(8,128)} %get-tuple-element.39.refs_1_.refs_2_), channel_id=1, source_target_pairs={{1,0},{2,1},{3,2},{4,3},{5,4},{6,5},{7,6},{8,7},{9,8},{10,9},{11,1... | collective-permute-start | bytes 3158024 | tf_op jit(solution)/shard_map/ppermute | solution.py:44
  8.0 25.4 %collective-permute-start = (f32[2056,128]{1,0:T(8,128)}, f32[2056,128]{1,0:T(8,128)}, u32[]{:S(2)}, u32[]{:S(2)}) collective-permute-start(f32[2056,128]{1,0:T(8,128)} %get-tuple-element.39.refs_1_.refs_2_), channel_id=1, source_target_pairs={{0,1},{1,2},{2,3},{3,4},{4,5},{5,6},{6,7},{7,8},{8,9},{9,10},{10,1... | collective-permute-start | bytes 3158024 | tf_op jit(solution)/shard_map/ppermute | solution.py:44
  9.9 63.7 %collective-permute-start.7 = (f32[520,128]{1,0:T(8,128)}, f32[520,128]{1,0:T(8,128)}, u32[]{:S(2)}, u32[]{:S(2)}) collective-permute-start(f32[520,128]{1,0:T(8,128)} %get-tuple-element.64), channel_id=1, source_target_pairs={{0,320},{32,352},{64,384},{96,416},{128,448},{160,480},{192,0},{22... | collective-permute-start | bytes 798728 | tf_op jit(solution)/shard_map/ppermute | solution.py:38
  24.7 48.9 %collective-permute-start.3 = (f32[1032,128]{1,0:T(8,128)}, f32[1032,128]{1,0:T(8,128)}, u32[]{:S(2)}, u32[]{:S(2)}) collective-permute-start(f32[1032,128]{1,0:T(8,128)} %get-tuple-element.51), channel_id=1, source_target_pairs={{0,128},{32,160},{64,192},{96,224},{128,256},{160,288},{192,320},{... | collective-permute-start | bytes 1585160 | tf_op jit(solution)/shard_map/ppermute | solution.py:38
  29.7 19.7 %copy-start.14 = (f32[8,2]{1,0:T(8,128)}, f32[8,2]{1,0:T(8,128)S(1)}, u32[]{:S(2)}) copy-start(f32[8,2]{1,0:T(8,128)S(1)} %slice.18) | copy-start | bytes 196
  29.7 19.7 %copy-start = (f32[2056,128]{1,0:T(8,128)S(1)}, f32[2056,128]{1,0:T(8,128)}, u32[]{:S(2)}) copy-start(f32[2056,128]{1,0:T(8,128)} %get-tuple-element.39.refs_1_.refs_2_) | copy-start | bytes 3158020
  33.3 57.8 %collective-permute-start.10 = (f32[520,128]{1,0:T(8,128)}, f32[520,128]{1,0:T(8,128)}, u32[]{:S(2)}, u32[]{:S(2)}) collective-permute-start(f32[520,128]{1,0:T(8,128)} %get-tuple-element.70), channel_id=1, source_target_pairs={{0,320},{32,352},{64,384},{96,416},{128,448},{160,480},{192,0},{22... | collective-permute-start | bytes 798728 | tf_op jit(solution)/shard_map/ppermute | solution.py:38
  41.4 73.3 %collective-permute-start.6 = (f32[1032,128]{1,0:T(8,128)}, f32[1032,128]{1,0:T(8,128)}, u32[]{:S(2)}, u32[]{:S(2)}) collective-permute-start(f32[1032,128]{1,0:T(8,128)} %get-tuple-element.59), channel_id=1, source_target_pairs={{0,96},{32,128},{64,160},{96,192},{128,224},{160,256},{192,288},{2... | collective-permute-start | bytes 1585160 | tf_op jit(solution)/shard_map/ppermute | solution.py:38
  44.1 89.5 %collective-permute-start.5 = (f32[1032,128]{1,0:T(8,128)}, f32[1032,128]{1,0:T(8,128)}, u32[]{:S(2)}, u32[]{:S(2)}) collective-permute-start(f32[1032,128]{1,0:T(8,128)} %get-tuple-element.57), channel_id=1, source_target_pairs={{0,64},{32,96},{64,128},{96,160},{128,192},{160,224},{192,256},{22... | collective-permute-start | bytes 1585160 | tf_op jit(solution)/shard_map/ppermute | solution.py:38
  49.4 2.6 %copy-start.16 = (f32[8,2]{1,0:T(8,128)}, f32[8,2]{1,0:T(8,128)S(1)}, u32[]{:S(2)}) copy-start(f32[8,2]{1,0:T(8,128)S(1)} %slice.22) | copy-start | bytes 196
  49.5 2.6 %copy-start.13 = (f32[1032,128]{1,0:T(8,128)S(1)}, f32[1032,128]{1,0:T(8,128)}, u32[]{:S(2)}) copy-start(f32[1032,128]{1,0:T(8,128)} %get-tuple-element.44.refs_0_) | copy-start | bytes 1585156
  52.0 83.5 %copy-start.5 = (bf16[24,128,256]{2,1,0:T(8,128)(2,1)}, bf16[24,128,256]{2,1,0:T(8,128)(2,1)S(1)}, u32[]{:S(2)}) copy-start(bf16[24,128,256]{2,1,0:T(8,128)(2,1)S(1)} %get-tuple-element.40.high) | copy-start | bytes 4718596
  52.0 83.5 %copy-start.7 = (bf16[24,128,256]{2,1,0:T(8,128)(2,1)}, bf16[24,128,256]{2,1,0:T(8,128)(2,1)S(1)}, u32[]{:S(2)}) copy-start(bf16[24,128,256]{2,1,0:T(8,128)(2,1)S(1)} %get-tuple-element.41.low) | copy-start | bytes 4718596
  52.0 83.5 %copy-start.11 = (bf16[16,256,128]{2,1,0:T(8,128)(2,1)}, bf16[16,256,128]{2,1,0:T(8,128)(2,1)S(1)}, u32[]{:S(2)}) copy-start(bf16[16,256,128]{2,1,0:T(8,128)(2,1)S(1)} %get-tuple-element.42.turned) | copy-start | bytes 3145732
  73.6 50.6 %collective-permute-start.8 = (f32[520,128]{1,0:T(8,128)}, f32[520,128]{1,0:T(8,128)}, u32[]{:S(2)}, u32[]{:S(2)}) collective-permute-start(f32[520,128]{1,0:T(8,128)} %collective-permute-done.7), channel_id=1, source_target_pairs={{0,352},{32,384},{64,416},{96,448},{128,480},{160,0},{192,32},{224... | collective-permute-start | bytes 798728 | tf_op jit(solution)/shard_map/ppermute | solution.py:38
  84.9 18.6 %collective-permute-start.2 = (f32[2056,128]{1,0:T(8,128)}, f32[2056,128]{1,0:T(8,128)}, u32[]{:S(2)}, u32[]{:S(2)}) collective-permute-start(f32[2056,128]{1,0:T(8,128)} %collective-permute-done.refs_0_.refs_1_), channel_id=1, source_target_pairs={{0,1},{1,2},{2,3},{3,4},{4,5},{5,6},{6,7},{7,8},{8,9},{9,10},{10,1... | collective-permute-start | bytes 3158024 | tf_op jit(solution)/shard_map/ppermute | solution.py:44
  86.9 24.0 %copy-start.1 = (f32[2056,128]{1,0:T(8,128)S(1)}, f32[2056,128]{1,0:T(8,128)}, u32[]{:S(2)}) copy-start(f32[2056,128]{1,0:T(8,128)} %get-tuple-element.39.refs_1_.refs_2_) | copy-start | bytes 3158020
  90.6 24.1 %copy-start.15 = (f32[8,2]{1,0:T(8,128)S(1)}, f32[8,2]{1,0:T(8,128)}, u32[]{:S(2)}) copy-start(f32[8,2]{1,0:T(8,128)} %copy-done.14) | copy-start | bytes 196
  90.6 24.1 %copy-start.17 = (f32[8,2]{1,0:T(8,128)S(1)}, f32[8,2]{1,0:T(8,128)}, u32[]{:S(2)}) copy-start(f32[8,2]{1,0:T(8,128)} %copy-done.16) | copy-start | bytes 196
  91.2 51.8 %collective-permute-start.4 = (f32[1032,128]{1,0:T(8,128)}, f32[1032,128]{1,0:T(8,128)}, u32[]{:S(2)}, u32[]{:S(2)}) collective-permute-start(f32[1032,128]{1,0:T(8,128)} %get-tuple-element.55), channel_id=1, source_target_pairs={{0,32},{32,64},{64,96},{96,128},{128,160},{160,192},{192,224},{224... | collective-permute-start | bytes 1585160 | tf_op jit(solution)/shard_map/ppermute | solution.py:38
  103.5 46.0 %collective-permute-start.11 = (f32[520,128]{1,0:T(8,128)}, f32[520,128]{1,0:T(8,128)}, u32[]{:S(2)}, u32[]{:S(2)}) collective-permute-start(f32[520,128]{1,0:T(8,128)} %collective-permute-done.10), channel_id=1, source_target_pairs={{0,352},{32,384},{64,416},{96,448},{128,480},{160,0},{192,32},{224... | collective-permute-start | bytes 798728 | tf_op jit(solution)/shard_map/ppermute | solution.py:38
  113.7 1.0 copy-start.2
  119.4 39.3 %collective-permute-start.15 = (f32[16,128,128]{2,1,0:T(8,128)}, f32[16,128,128]{2,1,0:T(8,128)}, u32[]{:S(2)}, u32[]{:S(2)}) collective-permute-start(f32[16,128,128]{2,1,0:T(8,128)} %get-tuple-element.62), channel_id=1, source_target_pairs={{0,1},{1,2},{2,3},{3,4},{4,5},{5,6},{6,7},{7,8},{8,9},{9,10},{10,1... | collective-permute-start | bytes 3145736 | tf_op jit(solution)/shard_map/ppermute | solution.py:44
  133.6 25.1 %collective-permute-start.13 = (f32[1032,128]{1,0:T(8,128)}, f32[1032,128]{1,0:T(8,128)}, u32[]{:S(2)}, u32[]{:S(2)}) collective-permute-start(f32[1032,128]{1,0:T(8,128)} %collective-permute-done.5.refs_0_), channel_id=1, source_target_pairs={{0,1},{1,2},{2,3},{3,4},{4,5},{5,6},{6,7},{7,8},{8,9},{9,10},{10,1... | collective-permute-start | bytes 1585160 | tf_op jit(solution)/shard_map/ppermute | solution.py:44
  138.1 1.1 copy-start.9
  142.9 26.0 %collective-permute-start.9 = (f32[1032,128]{1,0:T(8,128)}, f32[1032,128]{1,0:T(8,128)}, u32[]{:S(2)}, u32[]{:S(2)}) collective-permute-start(f32[1032,128]{1,0:T(8,128)} %collective-permute-done.4.refs_0_), channel_id=1, source_target_pairs={{0,1},{1,2},{2,3},{3,4},{4,5},{5,6},{6,7},{7,8},{8,9},{9,10},{10,1... | collective-permute-start | bytes 1585160 | tf_op jit(solution)/shard_map/ppermute | solution.py:44
  145.0 13.7 %collective-permute-start.14 = (f32[520,128]{1,0:T(8,128)}, f32[520,128]{1,0:T(8,128)}, u32[]{:S(2)}, u32[]{:S(2)}) collective-permute-start(f32[520,128]{1,0:T(8,128)} %collective-permute-done.8.refs_1_), channel_id=1, source_target_pairs={{0,1},{1,2},{2,3},{3,4},{4,5},{5,6},{6,7},{7,8},{8,9},{9,10},{10,1... | collective-permute-start | bytes 798728 | tf_op jit(solution)/shard_map/ppermute | solution.py:44
  149.6 19.3 %collective-permute-start.12 = (f32[520,128]{1,0:T(8,128)}, f32[520,128]{1,0:T(8,128)S(1)}, u32[]{:S(2)}, u32[]{:S(2)}) collective-permute-start(f32[520,128]{1,0:T(8,128)} %collective-permute-done.11.refs_1_), channel_id=1, source_target_pairs={{0,1},{1,2},{2,3},{3,4},{4,5},{5,6},{6,7},{7,8},{8,9},{9,10},{10,1... | collective-permute-start | bytes 798728 | tf_op jit(solution)/shard_map/ppermute | solution.py:44
  158.7 1.2 copy-start.3
  160.0 1.3 copy-start.10
  161.3 3.9 %copy-start.6 = (bf16[24,128,256]{2,1,0:T(8,128)(2,1)S(1)}, bf16[24,128,256]{2,1,0:T(8,128)(2,1)}, u32[]{:S(2)}) copy-start(bf16[24,128,256]{2,1,0:T(8,128)(2,1)} %copy-done.5) | copy-start | bytes 4718596
  161.3 3.9 %copy-start.8 = (bf16[24,128,256]{2,1,0:T(8,128)(2,1)S(1)}, bf16[24,128,256]{2,1,0:T(8,128)(2,1)}, u32[]{:S(2)}) copy-start(bf16[24,128,256]{2,1,0:T(8,128)(2,1)} %copy-done.7) | copy-start | bytes 4718596
  161.3 3.9 %copy-start.12 = (bf16[16,256,128]{2,1,0:T(8,128)(2,1)S(1)}, bf16[16,256,128]{2,1,0:T(8,128)(2,1)}, u32[]{:S(2)}) copy-start(bf16[16,256,128]{2,1,0:T(8,128)(2,1)} %copy-done.11) | copy-start | bytes 3145732
  165.2 3.7 %copy-start.4 = (bf16[16,256,128]{2,1,0:T(8,128)(2,1)S(1)}, bf16[16,256,128]{2,1,0:T(8,128)(2,1)}, u32[]{:S(2)}) copy-start(bf16[16,256,128]{2,1,0:T(8,128)(2,1)} %copy-done.2) | copy-start | bytes 3145732

commit v9 on v6

--- a/solution.py
+++ b/solution.py
@@ -359,12 +359,10 @@
     f_far_a = beside(far_a, 1)
     f2 = beside(d2, 1)
     (own,) = add(mine, (0,), [d2, far_a], [own], 10**14)
-    mid = own
-    (own,) = add(theirs, (0,), [f2, f_far_a], [own], arrived=on)
+    f1 = beside(after(d1, own), 1)
     f_far_b = beside(after(far_b, own), 1)
-    f1 = beside(after(d1, mid), 1)
     (own,) = add(mine, (0,), [d1, far_b], [own], 10**14)
-    (own,) = add(theirs, (0,), [f1, f_far_b], [own])
+    (own,) = add(theirs, (0,), [f2, f_far_a, f1, f_far_b], [own], arrived=on)
     return own.reshape(coarse_rows, SLOTS, TILE, TILE)
 
 

time: 170 us -> 173 us (1.018); the launches traced: 167 us -> 172 us
  starting transfers between devices: 74.3 us -> 79.1 us
    ppermute x8, starting transfers between devices: 55.8 us -> 59.7 us  [hop(): lax.ppermute(value, axis, [(i, (i + steps) % count) for i in range(count)])]
    ppermute x8, waiting for transfers between devices: 36.2 us -> 39.8 us  [hop(): lax.ppermute(value, axis, [(i, (i + steps) % count) for i in range(count)])]
    ppermute x8, waiting for transfers between devices: 17.7 us -> 14.9 us  [beside(): return lax.ppermute(value, 'gy', route)]
    pallas_call x7 -> x6, Pallas kernels: 23.8 us -> 22.8 us  [galerkin(): pl.pallas_call(functools.partial(galerkin_kernel, rows, shapes, targets,...]
  transfers between devices with their start and end apart: 16 -> 16, of which waited for: 9 -> 8; matrix products, arithmetic and copies ran while one was open for 1% -> 1% of each run, Pallas kernels for 17% -> 15%
where the time goes in v9:
time: 173 us; the launch traced here: 172 us
  starting transfers between devices  79.1 us (46%)
  waiting for transfers between devices  54.8 us (32%)
  Pallas kernels  35.2 us (20%)
  local copies, waits for them, and re-layouts  2.64 us (2%)
    ppermute x8, starting transfers between devices, hop(): lax.ppermute(value, axis, [(i, (i + steps) % count) for i in range(count)])  59.7 us
    ppermute x8, waiting for transfers between devices, hop(): lax.ppermute(value, axis, [(i, (i + steps) % count) for i in range(count)])  39.8 us
    pallas_call x6, Pallas kernels, galerkin(): pl.pallas_call(functools.partial(galerkin_kernel, rows, shapes, targets,...  22.8 us
    ppermute x8, starting transfers between devices, beside(): return lax.ppermute(value, 'gy', route)  19.4 us
    ppermute x8, waiting for transfers between devices, beside(): return lax.ppermute(value, 'gy', route)  14.9 us
    pallas_call x2, Pallas kernels, buckets(): pl.pallas_call(functools.partial(bucket_kernel, rows, gx, rows * gy, layo...  7.17 us
    pallas_call x2, Pallas kernels, split(): pl.pallas_call(functools.partial(split_kernel, rows), out_shape=[wide, wi...  5.28 us
  transfers between devices with their start and end apart: 16, of which 8 were waited for; matrix products, arithmetic and copies ran while one was open for 1% of the time, Pallas kernels for 15%

profile of v9, /device:TPU:6, one launch (start us, length us, event | category | flops | bytes accessed | tf_op | source)
XLA Modules:
  0.0 172.2 jit_solution(3499285558465027198)
XLA Ops:
  0.0 3.4 %buckets.2 = (f32[2056,128]{1,0:T(8,128)}, f32[520,128]{1,0:T(8,128)}, f32[1032,128]{1,0:T(8,128)}) custom-call(s32[8]{0:T(128)} %new_row.3, s32[4,8]{1,0:T(4,128)} %bitcast.15, s32[2,8]{1,0:T(2,128)} %bitcast.17, s32[1]{0:T(128)} %bitcast.2.my_x, f32[8,512,128]{2,1,0:T(8,128)} %bitcast.11, f32[2048,128]{1,0:T(8,128)} %bitcast.13), custom_call_target="tpu_custom_call" | custom-call | tf_op jit(solution)/shard_map/buckets/pallas_call | solution.py:143
  3.4 4.5 %collective-permute-start.1 = (f32[2056,128]{1,0:T(8,128)}, f32[2056,128]{1,0:T(8,128)S(1)}, u32[]{:S(2)}, u32[]{:S(2)}) collective-permute-start(f32[2056,128]{1,0:T(8,128)} %get-tuple-element.39.refs_1_.refs_2_), channel_id=1, source_target_pairs={{1,0},{2,1},{3,2},{4,3},{5,4},{6,5},{7,6},{8,7},{9,8},{10,9},{11,1... | collective-permute-start | bytes 3158024 | tf_op jit(solution)/shard_map/ppermute | solution.py:44
  8.0 1.9 %collective-permute-start = (f32[2056,128]{1,0:T(8,128)}, f32[2056,128]{1,0:T(8,128)}, u32[]{:S(2)}, u32[]{:S(2)}) collective-permute-start(f32[2056,128]{1,0:T(8,128)} %get-tuple-element.39.refs_1_.refs_2_), channel_id=1, source_target_pairs={{0,1},{1,2},{2,3},{3,4},{4,5},{5,6},{6,7},{7,8},{8,9},{9,10},{10,1... | collective-permute-start | bytes 3158024 | tf_op jit(solution)/shard_map/ppermute | solution.py:44
  9.9 14.8 %collective-permute-start.7 = (f32[520,128]{1,0:T(8,128)}, f32[520,128]{1,0:T(8,128)}, u32[]{:S(2)}, u32[]{:S(2)}) collective-permute-start(f32[520,128]{1,0:T(8,128)} %get-tuple-element.62), channel_id=1, source_target_pairs={{0,320},{32,352},{64,384},{96,416},{128,448},{160,480},{192,0},{22... | collective-permute-start | bytes 798728 | tf_op jit(solution)/shard_map/ppermute | solution.py:38
  24.7 4.4 %collective-permute-start.5 = (f32[1032,128]{1,0:T(8,128)}, f32[1032,128]{1,0:T(8,128)}, u32[]{:S(2)}, u32[]{:S(2)}) collective-permute-start(f32[1032,128]{1,0:T(8,128)} %get-tuple-element.55), channel_id=1, source_target_pairs={{0,128},{32,160},{64,192},{96,224},{128,256},{160,288},{192,320},{... | collective-permute-start | bytes 1585160 | tf_op jit(solution)/shard_map/ppermute | solution.py:38
  29.2 0.7 slice.18
  29.8 0.0 collective-permute-done.1.refs_2_
  29.9 3.7 %buckets.3 = (f32[520,128]{1,0:T(8,128)}, f32[1032,128]{1,0:T(8,128)}, f32[1032,128]{1,0:T(8,128)}, f32[1032,128]{1,0:T(8,128)}, f32[1032,128]{1,0:T(8,128)}) custom-call(s32[8]{0:T(128)} %new_row.3, s32[4,8]{1,0:T(4,128)} %bitcast.16, s32[2,8]{1,0:T(2,128)} %bitcast.18, s32[1]{0:T(128)} %bitcast.2.my_x, f32[8,512,128]{2,1,0:T(8,128)} %bitcast.12, ...), custom_call_target="tpu_custom_call" | custom-call | tf_op jit(solution)/shard_map/buckets/pallas_call | solution.py:143
  33.6 0.0 collective-permute-done.refs_0_.refs_1_
  33.6 7.8 %collective-permute-start.12 = (f32[520,128]{1,0:T(8,128)}, f32[520,128]{1,0:T(8,128)}, u32[]{:S(2)}, u32[]{:S(2)}) collective-permute-start(f32[520,128]{1,0:T(8,128)} %get-tuple-element.70), channel_id=1, source_target_pairs={{0,320},{32,352},{64,384},{96,416},{128,448},{160,480},{192,0},{22... | collective-permute-start | bytes 798728 | tf_op jit(solution)/shard_map/ppermute | solution.py:38
  41.4 2.6 %collective-permute-start.4 = (f32[1032,128]{1,0:T(8,128)}, f32[1032,128]{1,0:T(8,128)}, u32[]{:S(2)}, u32[]{:S(2)}) collective-permute-start(f32[1032,128]{1,0:T(8,128)} %get-tuple-element.53), channel_id=1, source_target_pairs={{0,96},{32,128},{64,160},{96,192},{128,224},{160,256},{192,288},{2... | collective-permute-start | bytes 1585160 | tf_op jit(solution)/shard_map/ppermute | solution.py:38
  44.0 4.6 %collective-permute-start.3 = (f32[1032,128]{1,0:T(8,128)}, f32[1032,128]{1,0:T(8,128)}, u32[]{:S(2)}, u32[]{:S(2)}) collective-permute-start(f32[1032,128]{1,0:T(8,128)} %get-tuple-element.51), channel_id=1, source_target_pairs={{0,64},{32,96},{64,128},{96,160},{128,192},{160,224},{192,256},{22... | collective-permute-start | bytes 1585160 | tf_op jit(solution)/shard_map/ppermute | solution.py:38
  48.6 0.7 slice.22
  49.3 0.6 copy-done.4
  49.9 0.0 copy-done
  49.9 2.5 %split.2 = (bf16[24,128,256]{2,1,0:T(8,128)(2,1)S(1)}, bf16[24,128,256]{2,1,0:T(8,128)(2,1)S(1)}, bf16[16,256,128]{2,1,0:T(8,128)(2,1)S(1)}) custom-call(f32[2056,128]{1,0:T(8,128)} %collective-permute-done.refs_0_.refs_1_, f32[2056,128]{1,0:T(8,128)S(1)} %copy-done, f32[2056,128]{1,0:T(8,128)S(1)} %collective-permute-done.1.refs_2_), custom_call_target="tpu_custom_call" | custom-call | tf_op jit(solution)/shard_map/split/pallas_call | solution.py:190
  52.4 0.0 copy-done.1
  52.4 3.4 %galerkin.6 = (f32[20,128,128]{2,1,0:T(8,128)S(1)}, f32[16,128,128]{2,1,0:T(8,128)S(1)}) custom-call(s32[24,2]{1,0:T(8,128)S(1)} %fusion.1.slots, s32[1]{0:T(128)} %bitcast.5.first, bf16[24,128,256]{2,1,0:T(8,128)(2,1)S(1)} %get-tuple-element.40.high, bf16[24,128,256]{2,1,0:T(8,128)(2,1)S(1)} %get-tuple-element.41.low, ...), custom_call_target="tpu_custom_call" | custom-call | flops 100000000376832 | bytes 1 | tf_op jit(solution)/shard_map/galerkin/pallas_call | solution.py:280
  55.8 18.2 %collective-permute-done.7 = f32[520,128]{1,0:T(8,128)} collective-permute-done((f32[520,128]{1,0:T(8,128)}, f32[520,128]{1,0:T(8,128)}, u32[]{:S(2)}, u32[]{:S(2)}) %collective-permute-start.7) | collective-permute-done | bytes 266272 | tf_op jit(solution)/shard_map/ppermute | solution.py:38
  74.1 0.0 collective-permute-done.5.refs_0_
  74.1 11.1 %collective-permute-start.8 = (f32[520,128]{1,0:T(8,128)}, f32[520,128]{1,0:T(8,128)}, u32[]{:S(2)}, u32[]{:S(2)}) collective-permute-start(f32[520,128]{1,0:T(8,128)} %collective-permute-done.7), channel_id=1, source_target_pairs={{0,352},{32,384},{64,416},{96,448},{128,480},{160,0},{192,32},{224... | collective-permute-start | bytes 798728 | tf_op jit(solution)/shard_map/ppermute | solution.py:38
  85.2 1.9 %collective-permute-start.2 = (f32[2056,128]{1,0:T(8,128)}, f32[2056,128]{1,0:T(8,128)}, u32[]{:S(2)}, u32[]{:S(2)}) collective-permute-start(f32[2056,128]{1,0:T(8,128)} %collective-permute-done.refs_0_.refs_1_), channel_id=1, source_target_pairs={{0,1},{1,2},{2,3},{3,4},{4,5},{5,6},{6,7},{7,8},{8,9},{9,10},{10,1... | collective-permute-start | bytes 3158024 | tf_op jit(solution)/shard_map/ppermute | solution.py:44
  87.1 3.7 %galerkin.7 = (f32[20,128,128]{2,1,0:T(8,128)S(1)}, f32[16,128,128]{2,1,0:T(8,128)S(1)}) custom-call(s32[24,2]{1,0:T(8,128)S(1)} %fusion.1.slots, s32[1]{0:T(128)} %bitcast.5.first, bf16[24,128,256]{2,1,0:T(8,128)(2,1)S(1)} %get-tuple-element.40.high, bf16[24,128,256]{2,1,0:T(8,128)(2,1)S(1)} %get-tuple-element.41.low, ...), custom_call_target="tpu_custom_call" | custom-call | flops 100000000376832 | bytes 1 | tf_op jit(solution)/shard_map/galerkin/pallas_call | solution.py:280
  90.8 0.9 collective-permute-done.12
  91.7 5.7 %collective-permute-start.10 = (f32[1032,128]{1,0:T(8,128)}, f32[1032,128]{1,0:T(8,128)}, u32[]{:S(2)}, u32[]{:S(2)}) collective-permute-start(f32[1032,128]{1,0:T(8,128)} %get-tuple-element.66), channel_id=1, source_target_pairs={{0,32},{32,64},{64,96},{96,128},{128,160},{160,192},{192,224},{224... | collective-permute-start | bytes 1585160 | tf_op jit(solution)/shard_map/ppermute | solution.py:38
  97.4 6.3 %collective-permute-done.2.refs_0_ = f32[2056,128]{1,0:T(8,128)} collective-permute-done((f32[2056,128]{1,0:T(8,128)}, f32[2056,128]{1,0:T(8,128)}, u32[]{:S(2)}, u32[]{:S(2)}) %collective-permute-start.2) | collective-permute-done | bytes 1052704 | tf_op jit(solution)/shard_map/ppermute | solution.py:44
  103.7 8.7 %collective-permute-start.13 = (f32[520,128]{1,0:T(8,128)}, f32[520,128]{1,0:T(8,128)}, u32[]{:S(2)}, u32[]{:S(2)}) collective-permute-start(f32[520,128]{1,0:T(8,128)} %collective-permute-done.12), channel_id=1, source_target_pairs={{0,352},{32,384},{64,416},{96,448},{128,480},{160,0},{192,32},{224... | collective-permute-start | bytes 798728 | tf_op jit(solution)/shard_map/ppermute | solution.py:38
  112.4 0.7 slice.24
  113.1 2.8 %split.3 = (bf16[24,128,256]{2,1,0:T(8,128)(2,1)S(1)}, bf16[24,128,256]{2,1,0:T(8,128)(2,1)S(1)}, bf16[16,256,128]{2,1,0:T(8,128)(2,1)S(1)}) custom-call(f32[2056,128]{1,0:T(8,128)} %collective-permute-done.2.refs_0_, f32[2056,128]{1,0:T(8,128)} %collective-permute-done.refs_0_.refs_1_, f32[2056,128]{1,0:T(8,128)S(1)} %copy-done), custom_call_target="tpu_custom_call" | custom-call | tf_op jit(solution)/shard_map/split/pallas_call | solution.py:190
  115.9 0.0 collective-permute-done.4.refs_0_
  115.9 4.7 %galerkin.8 = (f32[20,128,128]{2,1,0:T(8,128)S(1)}, f32[16,128,128]{2,1,0:T(8,128)}) custom-call(s32[24,2]{1,0:T(8,128)S(1)} %fusion.1.slots, s32[1]{0:T(128)} %bitcast.5.first, bf16[24,128,256]{2,1,0:T(8,128)(2,1)S(1)} %get-tuple-element.40.high, bf16[24,128,256]{2,1,0:T(8,128)(2,1)S(1)} %get-tuple-element.41.low, ...), custom_call_target="tpu_custom_call" | custom-call | flops 100000000376832 | bytes 1 | tf_op jit(solution)/shard_map/galerkin/pallas_call | solution.py:280
  120.6 1.9 %collective-permute-start.15 = (f32[16,128,128]{2,1,0:T(8,128)}, f32[16,128,128]{2,1,0:T(8,128)}, u32[]{:S(2)}, u32[]{:S(2)}) collective-permute-start(f32[16,128,128]{2,1,0:T(8,128)} %get-tuple-element.60), channel_id=1, source_target_pairs={{0,1},{1,2},{2,3},{3,4},{4,5},{5,6},{6,7},{7,8},{8,9},{9,10},{10,1... | collective-permute-start | bytes 3145736 | tf_op jit(solution)/shard_map/ppermute | solution.py:44
  122.5 6.4 %collective-permute-done.8.refs_1_ = f32[520,128]{1,0:T(8,128)} collective-permute-done((f32[520,128]{1,0:T(8,128)}, f32[520,128]{1,0:T(8,128)}, u32[]{:S(2)}, u32[]{:S(2)}) %collective-permute-start.8) | collective-permute-done | bytes 266272 | tf_op jit(solution)/shard_map/ppermute | solution.py:38
  128.9 4.8 %collective-permute-done.3.refs_0_ = f32[1032,128]{1,0:T(8,128)} collective-permute-done((f32[1032,128]{1,0:T(8,128)}, f32[1032,128]{1,0:T(8,128)}, u32[]{:S(2)}, u32[]{:S(2)}) %collective-permute-start.3) | collective-permute-done | bytes 528416 | tf_op jit(solution)/shard_map/ppermute | solution.py:38
  133.6 1.9 %collective-permute-start.9 = (f32[520,128]{1,0:T(8,128)}, f32[520,128]{1,0:T(8,128)}, u32[]{:S(2)}, u32[]{:S(2)}) collective-permute-start(f32[520,128]{1,0:T(8,128)} %collective-permute-done.8.refs_1_), channel_id=1, source_target_pairs={{0,1},{1,2},{2,3},{3,4},{4,5},{5,6},{6,7},{7,8},{8,9},{9,10},{10,1... | collective-permute-start | bytes 798728 | tf_op jit(solution)/shard_map/ppermute | solution.py:44
  135.6 1.9 %collective-permute-start.6 = (f32[1032,128]{1,0:T(8,128)}, f32[1032,128]{1,0:T(8,128)}, u32[]{:S(2)}, u32[]{:S(2)}) collective-permute-start(f32[1032,128]{1,0:T(8,128)} %collective-permute-done.3.refs_0_), channel_id=1, source_target_pairs={{0,1},{1,2},{2,3},{3,4},{4,5},{5,6},{6,7},{7,8},{8,9},{9,10},{10,1... | collective-permute-start | bytes 1585160 | tf_op jit(solution)/shard_map/ppermute | solution.py:44
  137.5 3.0 %galerkin.9.refs_2_ = f32[20,128,128]{2,1,0:T(8,128)S(1)} custom-call(s32[24,2]{1,0:T(8,128)S(1)} %fusion.1.slots, s32[1]{0:T(128)} %bitcast.5.first, bf16[24,128,256]{2,1,0:T(8,128)(2,1)S(1)} %get-tuple-element.40.high, bf16[24,128,256]{2,1,0:T(8,128)(2,1)S(1)} %get-tuple-element.41.low, bf16[16,256,128]{2,1,0:T(8,128)(2,1)S(1)} %get-tuple-element.42.turned, ...), custom_call_target="tpu_custom_call" | custom-call | flops 100000000376832 | bytes 1 | tf_op jit(solution)/shard_map/galerkin/pallas_call | solution.py:280
  140.5 9.5 %collective-permute-done.13.refs_1_ = f32[520,128]{1,0:T(8,128)} collective-permute-done((f32[520,128]{1,0:T(8,128)}, f32[520,128]{1,0:T(8,128)}, u32[]{:S(2)}, u32[]{:S(2)}) %collective-permute-start.13) | collective-permute-done | bytes 266272 | tf_op jit(solution)/shard_map/ppermute | solution.py:38
  150.1 0.0 collective-permute-done.10.refs_0_
  150.1 2.1 %collective-permute-start.14 = (f32[520,128]{1,0:T(8,128)}, f32[520,128]{1,0:T(8,128)}, u32[]{:S(2)}, u32[]{:S(2)}) collective-permute-start(f32[520,128]{1,0:T(8,128)} %collective-permute-done.13.refs_1_), channel_id=1, source_target_pairs={{0,1},{1,2},{2,3},{3,4},{4,5},{5,6},{6,7},{7,8},{8,9},{9,10},{10,1... | collective-permute-start | bytes 798728 | tf_op jit(solution)/shard_map/ppermute | solution.py:44
  152.2 3.2 %collective-permute-start.11 = (f32[1032,128]{1,0:T(8,128)}, f32[1032,128]{1,0:T(8,128)}, u32[]{:S(2)}, u32[]{:S(2)}) collective-permute-start(f32[1032,128]{1,0:T(8,128)} %collective-permute-done.10.refs_0_), channel_id=1, source_target_pairs={{0,1},{1,2},{2,3},{3,4},{4,5},{5,6},{6,7},{7,8},{8,9},{9,10},{10,1... | collective-permute-start | bytes 1585160 | tf_op jit(solution)/shard_map/ppermute | solution.py:44
  155.4 1.9 %galerkin.10.refs_4_ = f32[20,128,128]{2,1,0:T(8,128)S(1)} custom-call(s32[24,2]{1,0:T(8,128)S(1)} %fusion.1.slots, s32[1]{0:T(128)} %bitcast.5.first, bf16[24,128,256]{2,1,0:T(8,128)(2,1)S(1)} %get-tuple-element.40.high, bf16[24,128,256]{2,1,0:T(8,128)(2,1)S(1)} %get-tuple-element.41.low, bf16[16,256,128]{2,1,0:T(8,128)(2,1)S(1)} %get-tuple-element.42.turned, ...), custom_call_target="tpu_custom_call" | custom-call | flops 100000000376832 | bytes 1 | tf_op jit(solution)/shard_map/galerkin/pallas_call | solution.py:280
  157.3 2.9 %collective-permute-done.14.refs_3_ = f32[520,128]{1,0:T(8,128)} collective-permute-done((f32[520,128]{1,0:T(8,128)}, f32[520,128]{1,0:T(8,128)}, u32[]{:S(2)}, u32[]{:S(2)}) %collective-permute-start.14) | collective-permute-done | bytes 266272 | tf_op jit(solution)/shard_map/ppermute | solution.py:44
  160.2 0.0 collective-permute-done.9.refs_1_
  160.2 5.7 %collective-permute-done.11.refs_2_ = f32[1032,128]{1,0:T(8,128)} collective-permute-done((f32[1032,128]{1,0:T(8,128)}, f32[1032,128]{1,0:T(8,128)}, u32[]{:S(2)}, u32[]{:S(2)}) %collective-permute-start.11) | collective-permute-done | bytes 528416 | tf_op jit(solution)/shard_map/ppermute | solution.py:44
  165.9 0.0 collective-permute-done.6.refs_0_
  165.9 0.0 collective-permute-done.15.refs_5_
  165.9 6.1 %galerkin.11 = f32[20,128,128]{2,1,0:T(8,128)} custom-call(s32[24,2]{1,0:T(8,128)S(1)} %fusion.3.slots, s32[1]{0:T(128)} %bitcast.7.first, bf16[24,128,256]{2,1,0:T(8,128)(2,1)S(1)} %get-tuple-element.47.high, bf16[24,128,256]{2,1,0:T(8,128)(2,1)S(1)} %get-tuple-element.48.low, bf16[16,256,128]{2,1,0:T(8,128)(2,1)S(1)} %get-tuple-element.49.turned, ...), custom_call_target="tpu_custom_call" | custom-call | flops 1 | bytes 1 | tf_op jit(solution)/shard_map/galerkin/pallas_call | solution.py:280
  (12 shorter events, 0.0 us)
Async XLA Ops:
  3.4 26.4 %collective-permute-start.1 = (f32[2056,128]{1,0:T(8,128)}, f32[2056,128]{1,0:T(8,128)S(1)}, u32[]{:S(2)}, u32[]{:S(2)}) collective-permute-start(f32[2056,128]{1,0:T(8,128)} %get-tuple-element.39.refs_1_.refs_2_), channel_id=1, source_target_pairs={{1,0},{2,1},{3,2},{4,3},{5,4},{6,5},{7,6},{8,7},{9,8},{10,9},{11,1... | collective-permute-start | bytes 3158024 | tf_op jit(solution)/shard_map/ppermute | solution.py:44
  8.0 25.6 %collective-permute-start = (f32[2056,128]{1,0:T(8,128)}, f32[2056,128]{1,0:T(8,128)}, u32[]{:S(2)}, u32[]{:S(2)}) collective-permute-start(f32[2056,128]{1,0:T(8,128)} %get-tuple-element.39.refs_1_.refs_2_), channel_id=1, source_target_pairs={{0,1},{1,2},{2,3},{3,4},{4,5},{5,6},{6,7},{7,8},{8,9},{9,10},{10,1... | collective-permute-start | bytes 3158024 | tf_op jit(solution)/shard_map/ppermute | solution.py:44
  9.9 64.2 %collective-permute-start.7 = (f32[520,128]{1,0:T(8,128)}, f32[520,128]{1,0:T(8,128)}, u32[]{:S(2)}, u32[]{:S(2)}) collective-permute-start(f32[520,128]{1,0:T(8,128)} %get-tuple-element.62), channel_id=1, source_target_pairs={{0,320},{32,352},{64,384},{96,416},{128,448},{160,480},{192,0},{22... | collective-permute-start | bytes 798728 | tf_op jit(solution)/shard_map/ppermute | solution.py:38
  24.7 49.3 %collective-permute-start.5 = (f32[1032,128]{1,0:T(8,128)}, f32[1032,128]{1,0:T(8,128)}, u32[]{:S(2)}, u32[]{:S(2)}) collective-permute-start(f32[1032,128]{1,0:T(8,128)} %get-tuple-element.55), channel_id=1, source_target_pairs={{0,128},{32,160},{64,192},{96,224},{128,256},{160,288},{192,320},{... | collective-permute-start | bytes 1585160 | tf_op jit(solution)/shard_map/ppermute | solution.py:38
  29.8 19.5 %copy-start.2 = (f32[8,2]{1,0:T(8,128)}, f32[8,2]{1,0:T(8,128)S(1)}, u32[]{:S(2)}) copy-start(f32[8,2]{1,0:T(8,128)S(1)} %slice.18) | copy-start | bytes 196
  29.9 20.0 %copy-start = (f32[2056,128]{1,0:T(8,128)S(1)}, f32[2056,128]{1,0:T(8,128)}, u32[]{:S(2)}) copy-start(f32[2056,128]{1,0:T(8,128)} %get-tuple-element.39.refs_1_.refs_2_) | copy-start | bytes 3158020
  33.6 58.1 %collective-permute-start.12 = (f32[520,128]{1,0:T(8,128)}, f32[520,128]{1,0:T(8,128)}, u32[]{:S(2)}, u32[]{:S(2)}) collective-permute-start(f32[520,128]{1,0:T(8,128)} %get-tuple-element.70), channel_id=1, source_target_pairs={{0,320},{32,352},{64,384},{96,416},{128,448},{160,480},{192,0},{22... | collective-permute-start | bytes 798728 | tf_op jit(solution)/shard_map/ppermute | solution.py:38
  41.4 74.5 %collective-permute-start.4 = (f32[1032,128]{1,0:T(8,128)}, f32[1032,128]{1,0:T(8,128)}, u32[]{:S(2)}, u32[]{:S(2)}) collective-permute-start(f32[1032,128]{1,0:T(8,128)} %get-tuple-element.53), channel_id=1, source_target_pairs={{0,96},{32,128},{64,160},{96,192},{128,224},{160,256},{192,288},{2... | collective-permute-start | bytes 1585160 | tf_op jit(solution)/shard_map/ppermute | solution.py:38
  44.0 89.6 %collective-permute-start.3 = (f32[1032,128]{1,0:T(8,128)}, f32[1032,128]{1,0:T(8,128)}, u32[]{:S(2)}, u32[]{:S(2)}) collective-permute-start(f32[1032,128]{1,0:T(8,128)} %get-tuple-element.51), channel_id=1, source_target_pairs={{0,64},{32,96},{64,128},{96,160},{128,192},{160,224},{192,256},{22... | collective-permute-start | bytes 1585160 | tf_op jit(solution)/shard_map/ppermute | solution.py:38
  49.3 0.6 copy-start.4
  49.9 2.5 %copy-start.1 = (f32[1032,128]{1,0:T(8,128)S(1)}, f32[1032,128]{1,0:T(8,128)}, u32[]{:S(2)}) copy-start(f32[1032,128]{1,0:T(8,128)} %get-tuple-element.44.refs_0_) | copy-start | bytes 1585156
  74.1 54.8 %collective-permute-start.8 = (f32[520,128]{1,0:T(8,128)}, f32[520,128]{1,0:T(8,128)}, u32[]{:S(2)}, u32[]{:S(2)}) collective-permute-start(f32[520,128]{1,0:T(8,128)} %collective-permute-done.7), channel_id=1, source_target_pairs={{0,352},{32,384},{64,416},{96,448},{128,480},{160,0},{192,32},{224... | collective-permute-start | bytes 798728 | tf_op jit(solution)/shard_map/ppermute | solution.py:38
  85.2 18.6 %collective-permute-start.2 = (f32[2056,128]{1,0:T(8,128)}, f32[2056,128]{1,0:T(8,128)}, u32[]{:S(2)}, u32[]{:S(2)}) collective-permute-start(f32[2056,128]{1,0:T(8,128)} %collective-permute-done.refs_0_.refs_1_), channel_id=1, source_target_pairs={{0,1},{1,2},{2,3},{3,4},{4,5},{5,6},{6,7},{7,8},{8,9},{9,10},{10,1... | collective-permute-start | bytes 3158024 | tf_op jit(solution)/shard_map/ppermute | solution.py:44
  90.8 25.1 %copy-start.3 = (f32[8,2]{1,0:T(8,128)S(1)}, f32[8,2]{1,0:T(8,128)}, u32[]{:S(2)}) copy-start(f32[8,2]{1,0:T(8,128)} %copy-done.2) | copy-start | bytes 196
  90.8 25.1 %copy-start.5 = (f32[8,2]{1,0:T(8,128)S(1)}, f32[8,2]{1,0:T(8,128)}, u32[]{:S(2)}) copy-start(f32[8,2]{1,0:T(8,128)} %copy-done.4) | copy-start | bytes 196
  91.7 58.4 %collective-permute-start.10 = (f32[1032,128]{1,0:T(8,128)}, f32[1032,128]{1,0:T(8,128)}, u32[]{:S(2)}, u32[]{:S(2)}) collective-permute-start(f32[1032,128]{1,0:T(8,128)} %get-tuple-element.66), channel_id=1, source_target_pairs={{0,32},{32,64},{64,96},{96,128},{128,160},{160,192},{192,224},{224... | collective-permute-start | bytes 1585160 | tf_op jit(solution)/shard_map/ppermute | solution.py:38
  103.7 46.3 %collective-permute-start.13 = (f32[520,128]{1,0:T(8,128)}, f32[520,128]{1,0:T(8,128)}, u32[]{:S(2)}, u32[]{:S(2)}) collective-permute-start(f32[520,128]{1,0:T(8,128)} %collective-permute-done.12), channel_id=1, source_target_pairs={{0,352},{32,384},{64,416},{96,448},{128,480},{160,0},{192,32},{224... | collective-permute-start | bytes 798728 | tf_op jit(solution)/shard_map/ppermute | solution.py:38
  120.6 45.3 %collective-permute-start.15 = (f32[16,128,128]{2,1,0:T(8,128)}, f32[16,128,128]{2,1,0:T(8,128)}, u32[]{:S(2)}, u32[]{:S(2)}) collective-permute-start(f32[16,128,128]{2,1,0:T(8,128)} %get-tuple-element.60), channel_id=1, source_target_pairs={{0,1},{1,2},{2,3},{3,4},{4,5},{5,6},{6,7},{7,8},{8,9},{9,10},{10,1... | collective-permute-start | bytes 3145736 | tf_op jit(solution)/shard_map/ppermute | solution.py:44
  133.6 26.6 %collective-permute-start.9 = (f32[520,128]{1,0:T(8,128)}, f32[520,128]{1,0:T(8,128)}, u32[]{:S(2)}, u32[]{:S(2)}) collective-permute-start(f32[520,128]{1,0:T(8,128)} %collective-permute-done.8.refs_1_), channel_id=1, source_target_pairs={{0,1},{1,2},{2,3},{3,4},{4,5},{5,6},{6,7},{7,8},{8,9},{9,10},{10,1... | collective-permute-start | bytes 798728 | tf_op jit(solution)/shard_map/ppermute | solution.py:44
  135.6 30.3 %collective-permute-start.6 = (f32[1032,128]{1,0:T(8,128)}, f32[1032,128]{1,0:T(8,128)}, u32[]{:S(2)}, u32[]{:S(2)}) collective-permute-start(f32[1032,128]{1,0:T(8,128)} %collective-permute-done.3.refs_0_), channel_id=1, source_target_pairs={{0,1},{1,2},{2,3},{3,4},{4,5},{5,6},{6,7},{7,8},{8,9},{9,10},{10,1... | collective-permute-start | bytes 1585160 | tf_op jit(solution)/shard_map/ppermute | solution.py:44
  150.1 10.2 %collective-permute-start.14 = (f32[520,128]{1,0:T(8,128)}, f32[520,128]{1,0:T(8,128)}, u32[]{:S(2)}, u32[]{:S(2)}) collective-permute-start(f32[520,128]{1,0:T(8,128)} %collective-permute-done.13.refs_1_), channel_id=1, source_target_pairs={{0,1},{1,2},{2,3},{3,4},{4,5},{5,6},{6,7},{7,8},{8,9},{9,10},{10,1... | collective-permute-start | bytes 798728 | tf_op jit(solution)/shard_map/ppermute | solution.py:44
  152.2 13.7 %collective-permute-start.11 = (f32[1032,128]{1,0:T(8,128)}, f32[1032,128]{1,0:T(8,128)}, u32[]{:S(2)}, u32[]{:S(2)}) collective-permute-start(f32[1032,128]{1,0:T(8,128)} %collective-permute-done.10.refs_0_), channel_id=1, source_target_pairs={{0,1},{1,2},{2,3},{3,4},{4,5},{5,6},{6,7},{7,8},{8,9},{9,10},{10,1... | collective-permute-start | bytes 1585160 | tf_op jit(solution)/shard_map/ppermute | solution.py:44

commit v10 on v7

--- a/solution.py
+++ b/solution.py
@@ -365,7 +365,7 @@
     (own,) = add(theirs, (0,), [after(f2, token), f_far_a], [own], arrived=on)
     f1 = beside(after(d1, mid), 1)
     f_far_b = beside(far_b, 1)
-    (own,) = add(mine, (0,), [d1, far_b], [own])
+    (own,) = add(mine, (0,), [d1, far_b], [own], 10**14)
     (own,) = add(theirs, (0,), [f1, f_far_b], [own])
     return own.reshape(coarse_rows, SLOTS, TILE, TILE)
 

time: 170 us -> 171 us (level)
  the two profiles are of different devices: /device:TPU:1 before, /device:TPU:6 now
where the time goes in v10:
time: 171 us; the launch traced here: 169 us
  starting transfers between devices  74 us (43%)
  waiting for transfers between devices  56.2 us (33%)
  Pallas kernels  36.1 us (21%)
  local copies, waits for them, and re-layouts  2.64 us (2%)
    ppermute x8, starting transfers between devices, hop(): lax.ppermute(value, axis, [(i, (i + steps) % count) for i in range(count)])  54.9 us
    ppermute x8, waiting for transfers between devices, hop(): lax.ppermute(value, axis, [(i, (i + steps) % count) for i in range(count)])  45.1 us
    pallas_call x7, Pallas kernels, galerkin(): pl.pallas_call(functools.partial(galerkin_kernel, rows, shapes, targets,...  23.8 us
    ppermute x8, starting transfers between devices, beside(): return lax.ppermute(value, 'gy', route)  19.1 us
    ppermute x8, waiting for transfers between devices, beside(): return lax.ppermute(value, 'gy', route)  11.1 us
    pallas_call x2, Pallas kernels, buckets(): pl.pallas_call(functools.partial(bucket_kernel, rows, gx, rows * gy, layo...  7.02 us
    pallas_call x2, Pallas kernels, split(): pl.pallas_call(functools.partial(split_kernel, rows), out_shape=[wide, wi...  5.28 us
  transfers between devices with their start and end apart: 16, of which 9 were waited for; matrix products, arithmetic and copies ran while one was open for 1% of the time, Pallas kernels for 17%

profile of v10, /device:TPU:6, one launch (start us, length us, event | category | flops | bytes accessed | tf_op | source)
XLA Modules:
  0.0 169.4 jit_solution(13021576199297483639)
XLA Ops:
  0.0 3.4 %buckets.2 = (f32[2056,128]{1,0:T(8,128)}, f32[520,128]{1,0:T(8,128)}, f32[1032,128]{1,0:T(8,128)}) custom-call(s32[8]{0:T(128)} %new_row.3, s32[4,8]{1,0:T(4,128)} %bitcast.17, s32[2,8]{1,0:T(2,128)} %bitcast.19, s32[1]{0:T(128)} %bitcast.2.my_x, f32[8,512,128]{2,1,0:T(8,128)} %bitcast.13, f32[2048,128]{1,0:T(8,128)} %bitcast.15), custom_call_target="tpu_custom_call" | custom-call | tf_op jit(solution)/shard_map/buckets/pallas_call | solution.py:143
  3.4 4.5 %collective-permute-start.1 = (f32[2056,128]{1,0:T(8,128)}, f32[2056,128]{1,0:T(8,128)S(1)}, u32[]{:S(2)}, u32[]{:S(2)}) collective-permute-start(f32[2056,128]{1,0:T(8,128)} %get-tuple-element.40.refs_1_.refs_2_), channel_id=1, source_target_pairs={{1,0},{2,1},{3,2},{4,3},{5,4},{6,5},{7,6},{8,7},{9,8},{10,9},{11,1... | collective-permute-start | bytes 3158024 | tf_op jit(solution)/shard_map/ppermute | solution.py:44
  7.9 1.9 %collective-permute-start = (f32[2056,128]{1,0:T(8,128)}, f32[2056,128]{1,0:T(8,128)}, u32[]{:S(2)}, u32[]{:S(2)}) collective-permute-start(f32[2056,128]{1,0:T(8,128)} %get-tuple-element.40.refs_1_.refs_2_), channel_id=1, source_target_pairs={{0,1},{1,2},{2,3},{3,4},{4,5},{5,6},{6,7},{7,8},{8,9},{9,10},{10,1... | collective-permute-start | bytes 3158024 | tf_op jit(solution)/shard_map/ppermute | solution.py:44
  9.8 14.8 %collective-permute-start.7 = (f32[520,128]{1,0:T(8,128)}, f32[520,128]{1,0:T(8,128)}, u32[]{:S(2)}, u32[]{:S(2)}) collective-permute-start(f32[520,128]{1,0:T(8,128)} %get-tuple-element.65), channel_id=1, source_target_pairs={{0,320},{32,352},{64,384},{96,416},{128,448},{160,480},{192,0},{22... | collective-permute-start | bytes 798728 | tf_op jit(solution)/shard_map/ppermute | solution.py:38
  24.7 4.4 %collective-permute-start.3 = (f32[1032,128]{1,0:T(8,128)}, f32[1032,128]{1,0:T(8,128)}, u32[]{:S(2)}, u32[]{:S(2)}) collective-permute-start(f32[1032,128]{1,0:T(8,128)} %get-tuple-element.52), channel_id=1, source_target_pairs={{0,128},{32,160},{64,192},{96,224},{128,256},{160,288},{192,320},{... | collective-permute-start | bytes 1585160 | tf_op jit(solution)/shard_map/ppermute | solution.py:38
  29.0 0.7 slice.21
  29.7 0.0 collective-permute-done.1.refs_2_
  29.7 3.6 %buckets.3 = (f32[520,128]{1,0:T(8,128)}, f32[1032,128]{1,0:T(8,128)}, f32[1032,128]{1,0:T(8,128)}, f32[1032,128]{1,0:T(8,128)}, f32[1032,128]{1,0:T(8,128)}) custom-call(s32[8]{0:T(128)} %new_row.3, s32[4,8]{1,0:T(4,128)} %bitcast.18, s32[2,8]{1,0:T(2,128)} %bitcast.20, s32[1]{0:T(128)} %bitcast.2.my_x, f32[8,512,128]{2,1,0:T(8,128)} %bitcast.14, ...), custom_call_target="tpu_custom_call" | custom-call | tf_op jit(solution)/shard_map/buckets/pallas_call | solution.py:143
  33.4 0.0 collective-permute-done.refs_0_.refs_1_
  33.4 7.9 %collective-permute-start.10 = (f32[520,128]{1,0:T(8,128)}, f32[520,128]{1,0:T(8,128)}, u32[]{:S(2)}, u32[]{:S(2)}) collective-permute-start(f32[520,128]{1,0:T(8,128)} %get-tuple-element.71), channel_id=1, source_target_pairs={{0,320},{32,352},{64,384},{96,416},{128,448},{160,480},{192,0},{22... | collective-permute-start | bytes 798728 | tf_op jit(solution)/shard_map/ppermute | solution.py:38
  41.3 2.7 %collective-permute-start.6 = (f32[1032,128]{1,0:T(8,128)}, f32[1032,128]{1,0:T(8,128)}, u32[]{:S(2)}, u32[]{:S(2)}) collective-permute-start(f32[1032,128]{1,0:T(8,128)} %get-tuple-element.60), channel_id=1, source_target_pairs={{0,96},{32,128},{64,160},{96,192},{128,224},{160,256},{192,288},{2... | collective-permute-start | bytes 1585160 | tf_op jit(solution)/shard_map/ppermute | solution.py:38
  44.0 4.5 %collective-permute-start.5 = (f32[1032,128]{1,0:T(8,128)}, f32[1032,128]{1,0:T(8,128)}, u32[]{:S(2)}, u32[]{:S(2)}) collective-permute-start(f32[1032,128]{1,0:T(8,128)} %get-tuple-element.58), channel_id=1, source_target_pairs={{0,64},{32,96},{64,128},{96,160},{128,192},{160,224},{192,256},{22... | collective-permute-start | bytes 1585160 | tf_op jit(solution)/shard_map/ppermute | solution.py:38
  48.5 0.7 slice.26
  49.2 0.6 copy-done.4
  49.8 2.5 %split.2 = (bf16[24,128,256]{2,1,0:T(8,128)(2,1)S(1)}, bf16[24,128,256]{2,1,0:T(8,128)(2,1)S(1)}, bf16[16,256,128]{2,1,0:T(8,128)(2,1)S(1)}) custom-call(f32[2056,128]{1,0:T(8,128)} %collective-permute-done.refs_0_.refs_1_, f32[2056,128]{1,0:T(8,128)S(1)} %copy-done, f32[2056,128]{1,0:T(8,128)S(1)} %collective-permute-done.1.refs_2_), custom_call_target="tpu_custom_call" | custom-call | tf_op jit(solution)/shard_map/split/pallas_call | solution.py:190
  52.4 3.3 %galerkin.7 = (f32[20,128,128]{2,1,0:T(8,128)S(1)}, f32[16,128,128]{2,1,0:T(8,128)S(1)}) custom-call(s32[24,2]{1,0:T(8,128)S(1)} %fusion.1.slots, s32[1]{0:T(128)} %bitcast.5.first, bf16[24,128,256]{2,1,0:T(8,128)(2,1)S(1)} %get-tuple-element.41.high, bf16[24,128,256]{2,1,0:T(8,128)(2,1)S(1)} %get-tuple-element.42.low, ...), custom_call_target="tpu_custom_call" | custom-call | flops 100000000376832 | bytes 1 | tf_op jit(solution)/shard_map/galerkin/pallas_call | solution.py:280
  55.7 17.8 %collective-permute-done.7 = f32[520,128]{1,0:T(8,128)} collective-permute-done((f32[520,128]{1,0:T(8,128)}, f32[520,128]{1,0:T(8,128)}, u32[]{:S(2)}, u32[]{:S(2)}) %collective-permute-start.7) | collective-permute-done | bytes 266272 | tf_op jit(solution)/shard_map/ppermute | solution.py:38
  73.5 0.0 collective-permute-done.3.refs_0_
  73.5 11.7 %collective-permute-start.8 = (f32[520,128]{1,0:T(8,128)}, f32[520,128]{1,0:T(8,128)}, u32[]{:S(2)}, u32[]{:S(2)}) collective-permute-start(f32[520,128]{1,0:T(8,128)} %collective-permute-done.7), channel_id=1, source_target_pairs={{0,352},{32,384},{64,416},{96,448},{128,480},{160,0},{192,32},{224... | collective-permute-start | bytes 798728 | tf_op jit(solution)/shard_map/ppermute | solution.py:38
  85.2 1.9 %collective-permute-start.2 = (f32[2056,128]{1,0:T(8,128)}, f32[2056,128]{1,0:T(8,128)}, u32[]{:S(2)}, u32[]{:S(2)}) collective-permute-start(f32[2056,128]{1,0:T(8,128)} %collective-permute-done.refs_0_.refs_1_), channel_id=1, source_target_pairs={{0,1},{1,2},{2,3},{3,4},{4,5},{5,6},{6,7},{7,8},{8,9},{9,10},{10,1... | collective-permute-start | bytes 3158024 | tf_op jit(solution)/shard_map/ppermute | solution.py:44
  87.1 3.7 %galerkin.8 = (f32[20,128,128]{2,1,0:T(8,128)S(1)}, f32[16,128,128]{2,1,0:T(8,128)S(1)}) custom-call(s32[24,2]{1,0:T(8,128)S(1)} %fusion.1.slots, s32[1]{0:T(128)} %bitcast.5.first, bf16[24,128,256]{2,1,0:T(8,128)(2,1)S(1)} %get-tuple-element.41.high, bf16[24,128,256]{2,1,0:T(8,128)(2,1)S(1)} %get-tuple-element.42.low, ...), custom_call_target="tpu_custom_call" | custom-call | flops 100000000376832 | bytes 1 | tf_op jit(solution)/shard_map/galerkin/pallas_call | solution.py:280
  90.8 0.9 collective-permute-done.10
  91.7 5.0 %collective-permute-start.4 = (f32[1032,128]{1,0:T(8,128)}, f32[1032,128]{1,0:T(8,128)}, u32[]{:S(2)}, u32[]{:S(2)}) collective-permute-start(f32[1032,128]{1,0:T(8,128)} %get-tuple-element.56), channel_id=1, source_target_pairs={{0,32},{32,64},{64,96},{96,128},{128,160},{160,192},{192,224},{224... | collective-permute-start | bytes 1585160 | tf_op jit(solution)/shard_map/ppermute | solution.py:38
  96.6 7.1 %collective-permute-done.2.refs_0_ = f32[2056,128]{1,0:T(8,128)} collective-permute-done((f32[2056,128]{1,0:T(8,128)}, f32[2056,128]{1,0:T(8,128)}, u32[]{:S(2)}, u32[]{:S(2)}) %collective-permute-start.2) | collective-permute-done | bytes 1052704 | tf_op jit(solution)/shard_map/ppermute | solution.py:44
  103.7 3.9 %collective-permute-start.11 = (f32[520,128]{1,0:T(8,128)}, f32[520,128]{1,0:T(8,128)}, u32[]{:S(2)}, u32[]{:S(2)}) collective-permute-start(f32[520,128]{1,0:T(8,128)} %collective-permute-done.10), channel_id=1, source_target_pairs={{0,352},{32,384},{64,416},{96,448},{128,480},{160,0},{192,32},{224... | collective-permute-start | bytes 798728 | tf_op jit(solution)/shard_map/ppermute | solution.py:38
  107.7 0.7 slice.28
  108.3 2.8 %split.3 = (bf16[24,128,256]{2,1,0:T(8,128)(2,1)S(1)}, bf16[24,128,256]{2,1,0:T(8,128)(2,1)S(1)}, bf16[16,256,128]{2,1,0:T(8,128)(2,1)S(1)}) custom-call(f32[2056,128]{1,0:T(8,128)} %collective-permute-done.2.refs_0_, f32[2056,128]{1,0:T(8,128)} %collective-permute-done.refs_0_.refs_1_, f32[2056,128]{1,0:T(8,128)S(1)} %copy-done), custom_call_target="tpu_custom_call" | custom-call | tf_op jit(solution)/shard_map/split/pallas_call | solution.py:190
  111.1 0.0 copy-done.3
  111.1 1.7 collective-permute-done.6.refs_0_
  112.8 2.8 %galerkin.9 = (f32[20,128,128]{2,1,0:T(8,128)S(1)}, f32[16,128,128]{2,1,0:T(8,128)}) custom-call(s32[24,2]{1,0:T(8,128)S(1)} %fusion.1.slots, s32[1]{0:T(128)} %bitcast.5.first, bf16[24,128,256]{2,1,0:T(8,128)(2,1)S(1)} %get-tuple-element.41.high, bf16[24,128,256]{2,1,0:T(8,128)(2,1)S(1)} %get-tuple-element.42.low, ...), custom_call_target="tpu_custom_call" | custom-call | flops 100000000376832 | bytes 1 | tf_op jit(solution)/shard_map/galerkin/pallas_call | solution.py:280
  115.6 1.9 %collective-permute-start.15 = (f32[16,128,128]{2,1,0:T(8,128)}, f32[16,128,128]{2,1,0:T(8,128)}, u32[]{:S(2)}, u32[]{:S(2)}) collective-permute-start(f32[16,128,128]{2,1,0:T(8,128)} %get-tuple-element.63), channel_id=1, source_target_pairs={{0,1},{1,2},{2,3},{3,4},{4,5},{5,6},{6,7},{7,8},{8,9},{9,10},{10,1... | collective-permute-start | bytes 3145736 | tf_op jit(solution)/shard_map/ppermute | solution.py:44
  117.5 9.5 %collective-permute-done.8.refs_1_ = f32[520,128]{1,0:T(8,128)} collective-permute-done((f32[520,128]{1,0:T(8,128)}, f32[520,128]{1,0:T(8,128)}, u32[]{:S(2)}, u32[]{:S(2)}) %collective-permute-start.8) | collective-permute-done | bytes 266272 | tf_op jit(solution)/shard_map/ppermute | solution.py:38
  127.0 6.9 %collective-permute-done.5.refs_0_ = f32[1032,128]{1,0:T(8,128)} collective-permute-done((f32[1032,128]{1,0:T(8,128)}, f32[1032,128]{1,0:T(8,128)}, u32[]{:S(2)}, u32[]{:S(2)}) %collective-permute-start.5) | collective-permute-done | bytes 528416 | tf_op jit(solution)/shard_map/ppermute | solution.py:38
  133.8 1.9 %collective-permute-start.14 = (f32[520,128]{1,0:T(8,128)}, f32[520,128]{1,0:T(8,128)}, u32[]{:S(2)}, u32[]{:S(2)}) collective-permute-start(f32[520,128]{1,0:T(8,128)} %collective-permute-done.8.refs_1_), channel_id=1, source_target_pairs={{0,1},{1,2},{2,3},{3,4},{4,5},{5,6},{6,7},{7,8},{8,9},{9,10},{10,1... | collective-permute-start | bytes 798728 | tf_op jit(solution)/shard_map/ppermute | solution.py:44
  135.8 1.9 %collective-permute-start.13 = (f32[1032,128]{1,0:T(8,128)}, f32[1032,128]{1,0:T(8,128)}, u32[]{:S(2)}, u32[]{:S(2)}) collective-permute-start(f32[1032,128]{1,0:T(8,128)} %collective-permute-done.5.refs_0_), channel_id=1, source_target_pairs={{0,1},{1,2},{2,3},{3,4},{4,5},{5,6},{6,7},{7,8},{8,9},{9,10},{10,1... | collective-permute-start | bytes 1585160 | tf_op jit(solution)/shard_map/ppermute | solution.py:44
  137.7 3.7 %galerkin.10.refs_2_ = f32[20,128,128]{2,1,0:T(8,128)S(1)} custom-call(s32[24,2]{1,0:T(8,128)S(1)} %fusion.1.slots, s32[1]{0:T(128)} %bitcast.5.first, bf16[24,128,256]{2,1,0:T(8,128)(2,1)S(1)} %get-tuple-element.41.high, bf16[24,128,256]{2,1,0:T(8,128)(2,1)S(1)} %get-tuple-element.42.low, bf16[16,256,128]{2,1,0:T(8,128)(2,1)S(1)} %get-tuple-element.43.turned, ...), custom_call_target="tpu_custom_call" | custom-call | flops 100000000376832 | bytes 1 | tf_op jit(solution)/shard_map/galerkin/pallas_call | solution.py:280
  141.4 1.6 collective-permute-done.4.refs_0_
  143.0 6.9 %collective-permute-done.11.refs_1_ = f32[520,128]{1,0:T(8,128)} collective-permute-done((f32[520,128]{1,0:T(8,128)}, f32[520,128]{1,0:T(8,128)}, u32[]{:S(2)}, u32[]{:S(2)}) %collective-permute-start.11) | collective-permute-done | bytes 266272 | tf_op jit(solution)/shard_map/ppermute | solution.py:38
  149.9 2.1 %collective-permute-start.12 = (f32[520,128]{1,0:T(8,128)}, f32[520,128]{1,0:T(8,128)}, u32[]{:S(2)}, u32[]{:S(2)}) collective-permute-start(f32[520,128]{1,0:T(8,128)} %collective-permute-done.11.refs_1_), channel_id=1, source_target_pairs={{0,1},{1,2},{2,3},{3,4},{4,5},{5,6},{6,7},{7,8},{8,9},{9,10},{10,1... | collective-permute-start | bytes 798728 | tf_op jit(solution)/shard_map/ppermute | solution.py:44
  152.0 2.9 %collective-permute-start.9 = (f32[1032,128]{1,0:T(8,128)}, f32[1032,128]{1,0:T(8,128)}, u32[]{:S(2)}, u32[]{:S(2)}) collective-permute-start(f32[1032,128]{1,0:T(8,128)} %collective-permute-done.4.refs_0_), channel_id=1, source_target_pairs={{0,1},{1,2},{2,3},{3,4},{4,5},{5,6},{6,7},{7,8},{8,9},{9,10},{10,1... | collective-permute-start | bytes 1585160 | tf_op jit(solution)/shard_map/ppermute | solution.py:44
  154.9 0.0 collective-permute-done.13.refs_0_
  154.9 0.0 collective-permute-done.14.refs_1_
  154.9 0.0 collective-permute-done.15.refs_3_
  154.9 4.2 %galerkin.11.refs_2_ = f32[20,128,128]{2,1,0:T(8,128)S(1)} custom-call(s32[24,2]{1,0:T(8,128)S(1)} %fusion.3.slots, s32[1]{0:T(128)} %bitcast.7.first, bf16[24,128,256]{2,1,0:T(8,128)(2,1)S(1)} %get-tuple-element.48.high, bf16[24,128,256]{2,1,0:T(8,128)(2,1)S(1)} %get-tuple-element.49.low, bf16[16,256,128]{2,1,0:T(8,128)(2,1)S(1)} %get-tuple-element.50.turned, ...), custom_call_target="tpu_custom_call" | custom-call | flops 1 | bytes 1 | tf_op jit(solution)/shard_map/galerkin/pallas_call | solution.py:280
  159.1 2.5 %galerkin.12.refs_2_ = f32[20,128,128]{2,1,0:T(8,128)S(1)} custom-call(s32[24,2]{1,0:T(8,128)S(1)} %fusion.1.slots, s32[1]{0:T(128)} %bitcast.5.first, bf16[24,128,256]{2,1,0:T(8,128)(2,1)S(1)} %get-tuple-element.41.high, bf16[24,128,256]{2,1,0:T(8,128)(2,1)S(1)} %get-tuple-element.42.low, bf16[16,256,128]{2,1,0:T(8,128)(2,1)S(1)} %get-tuple-element.43.turned, ...), custom_call_target="tpu_custom_call" | custom-call | flops 100000000376832 | bytes 1 | tf_op jit(solution)/shard_map/galerkin/pallas_call | solution.py:280
  161.7 0.0 collective-permute-done.12.refs_1_
  161.7 4.0 %collective-permute-done.9.refs_0_ = f32[1032,128]{1,0:T(8,128)} collective-permute-done((f32[1032,128]{1,0:T(8,128)}, f32[1032,128]{1,0:T(8,128)}, u32[]{:S(2)}, u32[]{:S(2)}) %collective-permute-start.9) | collective-permute-done | bytes 528416 | tf_op jit(solution)/shard_map/ppermute | solution.py:44
  165.7 3.6 %galerkin.13 = f32[20,128,128]{2,1,0:T(8,128)} custom-call(s32[24,2]{1,0:T(8,128)S(1)} %fusion.3.slots, s32[1]{0:T(128)} %bitcast.7.first, bf16[24,128,256]{2,1,0:T(8,128)(2,1)S(1)} %get-tuple-element.48.high, bf16[24,128,256]{2,1,0:T(8,128)(2,1)S(1)} %get-tuple-element.49.low, bf16[16,256,128]{2,1,0:T(8,128)(2,1)S(1)} %get-tuple-element.50.turned, ...), custom_call_target="tpu_custom_call" | custom-call | flops 1 | bytes 1 | tf_op jit(solution)/shard_map/galerkin/pallas_call | solution.py:280
  (13 shorter events, 0.0 us)
Async XLA Ops:
  3.4 26.3 %collective-permute-start.1 = (f32[2056,128]{1,0:T(8,128)}, f32[2056,128]{1,0:T(8,128)S(1)}, u32[]{:S(2)}, u32[]{:S(2)}) collective-permute-start(f32[2056,128]{1,0:T(8,128)} %get-tuple-element.40.refs_1_.refs_2_), channel_id=1, source_target_pairs={{1,0},{2,1},{3,2},{4,3},{5,4},{6,5},{7,6},{8,7},{9,8},{10,9},{11,1... | collective-permute-start | bytes 3158024 | tf_op jit(solution)/shard_map/ppermute | solution.py:44
  7.9 25.5 %collective-permute-start = (f32[2056,128]{1,0:T(8,128)}, f32[2056,128]{1,0:T(8,128)}, u32[]{:S(2)}, u32[]{:S(2)}) collective-permute-start(f32[2056,128]{1,0:T(8,128)} %get-tuple-element.40.refs_1_.refs_2_), channel_id=1, source_target_pairs={{0,1},{1,2},{2,3},{3,4},{4,5},{5,6},{6,7},{7,8},{8,9},{9,10},{10,1... | collective-permute-start | bytes 3158024 | tf_op jit(solution)/shard_map/ppermute | solution.py:44
  9.8 63.7 %collective-permute-start.7 = (f32[520,128]{1,0:T(8,128)}, f32[520,128]{1,0:T(8,128)}, u32[]{:S(2)}, u32[]{:S(2)}) collective-permute-start(f32[520,128]{1,0:T(8,128)} %get-tuple-element.65), channel_id=1, source_target_pairs={{0,320},{32,352},{64,384},{96,416},{128,448},{160,480},{192,0},{22... | collective-permute-start | bytes 798728 | tf_op jit(solution)/shard_map/ppermute | solution.py:38
  24.7 48.8 %collective-permute-start.3 = (f32[1032,128]{1,0:T(8,128)}, f32[1032,128]{1,0:T(8,128)}, u32[]{:S(2)}, u32[]{:S(2)}) collective-permute-start(f32[1032,128]{1,0:T(8,128)} %get-tuple-element.52), channel_id=1, source_target_pairs={{0,128},{32,160},{64,192},{96,224},{128,256},{160,288},{192,320},{... | collective-permute-start | bytes 1585160 | tf_op jit(solution)/shard_map/ppermute | solution.py:38
  29.7 19.5 %copy-start.2 = (f32[8,2]{1,0:T(8,128)}, f32[8,2]{1,0:T(8,128)S(1)}, u32[]{:S(2)}) copy-start(f32[8,2]{1,0:T(8,128)S(1)} %slice.21) | copy-start | bytes 196
  29.7 20.1 %copy-start = (f32[2056,128]{1,0:T(8,128)S(1)}, f32[2056,128]{1,0:T(8,128)}, u32[]{:S(2)}) copy-start(f32[2056,128]{1,0:T(8,128)} %get-tuple-element.40.refs_1_.refs_2_) | copy-start | bytes 3158020
  33.4 58.3 %collective-permute-start.10 = (f32[520,128]{1,0:T(8,128)}, f32[520,128]{1,0:T(8,128)}, u32[]{:S(2)}, u32[]{:S(2)}) collective-permute-start(f32[520,128]{1,0:T(8,128)} %get-tuple-element.71), channel_id=1, source_target_pairs={{0,320},{32,352},{64,384},{96,416},{128,448},{160,480},{192,0},{22... | collective-permute-start | bytes 798728 | tf_op jit(solution)/shard_map/ppermute | solution.py:38
  41.3 71.5 %collective-permute-start.6 = (f32[1032,128]{1,0:T(8,128)}, f32[1032,128]{1,0:T(8,128)}, u32[]{:S(2)}, u32[]{:S(2)}) collective-permute-start(f32[1032,128]{1,0:T(8,128)} %get-tuple-element.60), channel_id=1, source_target_pairs={{0,96},{32,128},{64,160},{96,192},{128,224},{160,256},{192,288},{2... | collective-permute-start | bytes 1585160 | tf_op jit(solution)/shard_map/ppermute | solution.py:38
  44.0 89.8 %collective-permute-start.5 = (f32[1032,128]{1,0:T(8,128)}, f32[1032,128]{1,0:T(8,128)}, u32[]{:S(2)}, u32[]{:S(2)}) collective-permute-start(f32[1032,128]{1,0:T(8,128)} %get-tuple-element.58), channel_id=1, source_target_pairs={{0,64},{32,96},{64,128},{96,160},{128,192},{160,224},{192,256},{22... | collective-permute-start | bytes 1585160 | tf_op jit(solution)/shard_map/ppermute | solution.py:38
  49.2 0.6 copy-start.4
  49.8 2.5 %copy-start.1 = (f32[1032,128]{1,0:T(8,128)S(1)}, f32[1032,128]{1,0:T(8,128)}, u32[]{:S(2)}) copy-start(f32[1032,128]{1,0:T(8,128)} %get-tuple-element.45.refs_0_) | copy-start | bytes 1585156
  73.5 53.5 %collective-permute-start.8 = (f32[520,128]{1,0:T(8,128)}, f32[520,128]{1,0:T(8,128)}, u32[]{:S(2)}, u32[]{:S(2)}) collective-permute-start(f32[520,128]{1,0:T(8,128)} %collective-permute-done.7), channel_id=1, source_target_pairs={{0,352},{32,384},{64,416},{96,448},{128,480},{160,0},{192,32},{224... | collective-permute-start | bytes 798728 | tf_op jit(solution)/shard_map/ppermute | solution.py:38
  85.2 18.6 %collective-permute-start.2 = (f32[2056,128]{1,0:T(8,128)}, f32[2056,128]{1,0:T(8,128)}, u32[]{:S(2)}, u32[]{:S(2)}) collective-permute-start(f32[2056,128]{1,0:T(8,128)} %collective-permute-done.refs_0_.refs_1_), channel_id=1, source_target_pairs={{0,1},{1,2},{2,3},{3,4},{4,5},{5,6},{6,7},{7,8},{8,9},{9,10},{10,1... | collective-permute-start | bytes 3158024 | tf_op jit(solution)/shard_map/ppermute | solution.py:44
  90.8 20.3 %copy-start.3 = (f32[8,2]{1,0:T(8,128)S(1)}, f32[8,2]{1,0:T(8,128)}, u32[]{:S(2)}) copy-start(f32[8,2]{1,0:T(8,128)} %copy-done.2) | copy-start | bytes 196
  90.8 20.3 %copy-start.5 = (f32[8,2]{1,0:T(8,128)S(1)}, f32[8,2]{1,0:T(8,128)}, u32[]{:S(2)}) copy-start(f32[8,2]{1,0:T(8,128)} %copy-done.4) | copy-start | bytes 196
  91.7 51.3 %collective-permute-start.4 = (f32[1032,128]{1,0:T(8,128)}, f32[1032,128]{1,0:T(8,128)}, u32[]{:S(2)}, u32[]{:S(2)}) collective-permute-start(f32[1032,128]{1,0:T(8,128)} %get-tuple-element.56), channel_id=1, source_target_pairs={{0,32},{32,64},{64,96},{96,128},{128,160},{160,192},{192,224},{224... | collective-permute-start | bytes 1585160 | tf_op jit(solution)/shard_map/ppermute | solution.py:38
  103.7 46.1 %collective-permute-start.11 = (f32[520,128]{1,0:T(8,128)}, f32[520,128]{1,0:T(8,128)}, u32[]{:S(2)}, u32[]{:S(2)}) collective-permute-start(f32[520,128]{1,0:T(8,128)} %collective-permute-done.10), channel_id=1, source_target_pairs={{0,352},{32,384},{64,416},{96,448},{128,480},{160,0},{192,32},{224... | collective-permute-start | bytes 798728 | tf_op jit(solution)/shard_map/ppermute | solution.py:38
  115.6 39.3 %collective-permute-start.15 = (f32[16,128,128]{2,1,0:T(8,128)}, f32[16,128,128]{2,1,0:T(8,128)}, u32[]{:S(2)}, u32[]{:S(2)}) collective-permute-start(f32[16,128,128]{2,1,0:T(8,128)} %get-tuple-element.63), channel_id=1, source_target_pairs={{0,1},{1,2},{2,3},{3,4},{4,5},{5,6},{6,7},{7,8},{8,9},{9,10},{10,1... | collective-permute-start | bytes 3145736 | tf_op jit(solution)/shard_map/ppermute | solution.py:44
  133.8 21.1 %collective-permute-start.14 = (f32[520,128]{1,0:T(8,128)}, f32[520,128]{1,0:T(8,128)}, u32[]{:S(2)}, u32[]{:S(2)}) collective-permute-start(f32[520,128]{1,0:T(8,128)} %collective-permute-done.8.refs_1_), channel_id=1, source_target_pairs={{0,1},{1,2},{2,3},{3,4},{4,5},{5,6},{6,7},{7,8},{8,9},{9,10},{10,1... | collective-permute-start | bytes 798728 | tf_op jit(solution)/shard_map/ppermute | solution.py:44
  135.8 19.1 %collective-permute-start.13 = (f32[1032,128]{1,0:T(8,128)}, f32[1032,128]{1,0:T(8,128)}, u32[]{:S(2)}, u32[]{:S(2)}) collective-permute-start(f32[1032,128]{1,0:T(8,128)} %collective-permute-done.5.refs_0_), channel_id=1, source_target_pairs={{0,1},{1,2},{2,3},{3,4},{4,5},{5,6},{6,7},{7,8},{8,9},{9,10},{10,1... | collective-permute-start | bytes 1585160 | tf_op jit(solution)/shard_map/ppermute | solution.py:44
  149.9 11.8 %collective-permute-start.12 = (f32[520,128]{1,0:T(8,128)}, f32[520,128]{1,0:T(8,128)}, u32[]{:S(2)}, u32[]{:S(2)}) collective-permute-start(f32[520,128]{1,0:T(8,128)} %collective-permute-done.11.refs_1_), channel_id=1, source_target_pairs={{0,1},{1,2},{2,3},{3,4},{4,5},{5,6},{6,7},{7,8},{8,9},{9,10},{10,1... | collective-permute-start | bytes 798728 | tf_op jit(solution)/shard_map/ppermute | solution.py:44
  152.0 13.7 %collective-permute-start.9 = (f32[1032,128]{1,0:T(8,128)}, f32[1032,128]{1,0:T(8,128)}, u32[]{:S(2)}, u32[]{:S(2)}) collective-permute-start(f32[1032,128]{1,0:T(8,128)} %collective-permute-done.4.refs_0_), channel_id=1, source_target_pairs={{0,1},{1,2},{2,3},{3,4},{4,5},{5,6},{6,7},{7,8},{8,9},{9,10},{10,1... | collective-permute-start | bytes 1585160 | tf_op jit(solution)/shard_map/ppermute | solution.py:44
